TPU v7x, 128 devices: a whole 4x4x4 slice. The times are simulated.
128 devices in a mesh: sec: 4 (over y_lo, core), brick: 32 (over z, y_hi, x).
Axes of the slice: x: 4, y: 4 (y_hi: 2, y_lo: 2; y = y_hi * 2 + y_lo), z: 4, core: 2. Of those that a mesh axis runs over, the one named last changes fastest.
Arguments:
- potentials: float32 [4, 1024, 32, 128], P('sec', 'brick'), may hold values from -0.3 to 1.2
- coefficient: float32 [4, 1024, 32, 128], P('sec', 'brick'), may hold values from 0.04 to 0.32
- recovery: float32 [1024, 32, 128], P('brick'), may hold values from 0 to 1
- excitable: int32 [1024, 32, 128], P('brick'), may hold values 0 or 1
- row_of: int32 [32], P('brick'), may hold values from 0 to 2
Outputs:
- updated: float32 [4, 1024, 32, 128], P('sec', 'brick')
Inputs may be any that keep to these rules, and one draw needn't show every extreme that they name: row_of[p] is the torso layer on which heart brick p lies.
All inputs are finite; a program needn't handle non-finite values. No bound on the sum of `excitable` on one device may be relied on, other than what follows from the above.
Results may differ from a plain program's by a relative error of at most 0.0003.
Values sent between devices are 32-bit elements; how exact they have to be, the bound alone decides.
No kernel may reach another device: no remote copies, remote signals or barrier semaphores. Data moves between devices by JAX's collectives and lax.ppermute only.
A program may use at most 64 MiB of HBM per device.

v0:
```python
import jax
import jax.numpy as jnp
from jax import lax
from jax.sharding import PartitionSpec as P

SUBSTEPS = 8
SWEEPS = 16
STEPS = 2


coupling_gain = 0.1
ionic_timestep = 0.05
ionic_gain = 8.0
recovery_rate = 0.1
recovery_decay = 0.5
spectrum_low = 0.04
spectrum_high = 12.32
rim_depth = 4
heart_row = 3


def extended_2(value, sides, width):
    for axis, dim in sides:
        devices, length = (lax.axis_size(axis), value.shape[dim])
        up = [(i, (i + 1) % devices) for i in range(devices - 1)]
        down = [(j, i) for i, j in up]
        last = lax.slice_in_dim(value, length - width, length, axis=dim)
        initial = lax.slice_in_dim(value, 0, width, axis=dim)
        before = lax.ppermute(last, axis, up)
        after = lax.ppermute(initial, axis, down)
        value = jnp.concatenate([before, value, after], axis=dim)
    return value


def with_halo(value, sides, width):
    edges = {}
    for axis, dim in sides:
        devices, length = (lax.axis_size(axis), value.shape[dim])
        up = [(i, (i + 1) % devices) for i in range(devices - 1)]
        last = lax.slice_in_dim(value, length - width, length, axis=dim)
        initial = lax.slice_in_dim(value, 0, width, axis=dim)
        edges[dim] = (
            lax.ppermute(last, axis, up),
            lax.ppermute(initial, axis, [(b, a) for a, b in up]),
        )
    done = []
    for _, dim in sides:
        low, high = edges[dim]
        around = [(width, width) if d in done else (0, 0) for d in range(value.ndim)]
        value = jnp.concatenate([jnp.pad(low, around), value, jnp.pad(high, around)], axis=dim)
        done.append(dim)
    return value


def broadcast(value, axis, root):
    return lax.dynamic_index_in_dim(lax.all_gather(value, axis), root, 0, keepdims=False)


def chebyshev_weights(count):
    center = 0.5 * (spectrum_high + spectrum_low)
    spread = 0.5 * (spectrum_high - spectrum_low)
    ratio = center / spread
    current = 1.0 / ratio
    keeps = []
    pushes = []
    for number in range(count):
        following = 1.0 / (2.0 * ratio - current)
        keeps.append(following * current)
        pushes.append(2.0 * following / spread)
        current = following
    return (center, keeps, pushes)


def ionic(voltage, recovery, threshold, active):
    for substep in range(SUBSTEPS):
        drive = ionic_gain * voltage * (voltage - threshold) * (1.0 - voltage) - recovery
        relax = recovery_rate * (voltage - recovery_decay * recovery)
        voltage = voltage + ionic_timestep * active * drive
        recovery = recovery + ionic_timestep * active * relax
    return (voltage, recovery)


def keep_state(voltage, recovery, threshold, active):
    return (voltage, recovery)


def voltage_laplace(voltage, is_first, is_last):
    extended = extended_2(voltage, (("brick", 0),), 1)
    lower = jnp.where(is_first, voltage[:1], extended[:1])
    upper = jnp.where(is_last, voltage[-1:], extended[-1:])
    forward = jnp.concatenate([voltage[1:], upper], axis=0)
    backward = jnp.concatenate([lower, voltage[:-1]], axis=0)
    sides = jnp.pad(voltage, ((0, 0), (1, 1), (1, 1)), mode="edge")
    total = forward + backward
    total = total + sides[:, 2:, 1:-1] + sides[:, :-2, 1:-1]
    total = total + sides[:, 1:-1, 2:] + sides[:, 1:-1, :-2]
    return total - 6.0 * voltage


def beside_all(extended):
    inner = jnp.pad(extended[1:-1, 1:-1], ((0, 0), (0, 0), (1, 1)))
    total = extended[2:, 1:-1] + extended[:-2, 1:-1]
    total = total + extended[1:-1, 2:] + extended[1:-1, :-2]
    total = total + inner[:, :, 2:] + inner[:, :, :-2]
    return total


def deep_group(state, first, count, absorb_wide, inside_wide, keeps, pushes):
    iterate, direction, residual = state
    size_x = iterate.shape[0]
    size_y = iterate.shape[1]
    wide_dir, wide_res = (
        extended_2(direction, (("sec", 1), ("brick", 0)), rim_depth),
        extended_2(residual, (("sec", 1), ("brick", 0)), rim_depth),
    )
    depth = rim_depth
    for offset in range(count):
        iterate = iterate + wide_dir[depth : depth + size_x, depth : depth + size_y]
        start = rim_depth - depth + 1
        span_x = size_x + 2 * depth - 2
        span_y = size_y + 2 * depth - 2
        absorb = absorb_wide[start : start + span_x, start : start + span_y]
        inside = inside_wide[start : start + span_x, start : start + span_y]
        inner = wide_dir[1:-1, 1:-1]
        wide_res = (wide_res[1:-1, 1:-1] - ((6.0 + absorb) * inner - beside_all(wide_dir))) * inside
        wide_dir = keeps[first + offset] * inner + pushes[first + offset] * wide_res
        depth = depth - 1
    direction = wide_dir[depth : depth + size_x, depth : depth + size_y]
    residual = wide_res[depth : depth + size_x, depth : depth + size_y]
    return (iterate, direction, residual)


def body(potentials, coefficient, recovery, excitable, row_of):
    field = potentials[0]
    local_coef = coefficient[0]
    sec_index = lax.axis_index("sec")
    brick_index = lax.axis_index("brick")
    is_para = sec_index == heart_row
    scale = jnp.where(is_para, 0.0, 1.0).astype(jnp.float32)
    is_first = brick_index == 0
    is_last = brick_index == lax.axis_size("brick") - 1
    owner_row = row_of[0]
    owner = sec_index == owner_row
    active = excitable.astype(jnp.float32)
    voltage = field
    potential = field * scale
    center, keep_list, push_list = chebyshev_weights(SWEEPS - 1)
    keeps = jnp.array(keep_list, dtype=jnp.float32)
    pushes = jnp.array(push_list, dtype=jnp.float32)
    absorb_wide, inside_wide = (
        extended_2(local_coef, (("sec", 1), ("brick", 0)), rim_depth),
        extended_2(jnp.zeros_like(local_coef) + scale, (("sec", 1), ("brick", 0)), rim_depth),
    )
    source = voltage_laplace(voltage, is_first, is_last)
    for coupling_step in range(STEPS):
        extended = with_halo(potential, (("sec", 1), ("brick", 0)), 1)
        neighbours = beside_all(extended)
        current = neighbours - 6.0 * potential
        to_elliptic = broadcast(source, "sec", heart_row)
        to_parabolic = broadcast(current, "sec", owner_row)
        voltage, recovery = lax.cond(
            is_para, ionic, keep_state, voltage, recovery, local_coef, active
        )
        fresh = voltage_laplace(voltage, is_first, is_last)
        voltage = voltage + coupling_gain * (fresh + to_parabolic)
        placed = jnp.where(owner, to_elliptic, 0.0)
        residual = (placed - ((6.0 + local_coef) * potential - neighbours)) * scale
        direction = residual / center
        state = (potential, direction, residual)
        updates = SWEEPS - 1
        groups = updates // rim_depth
        rest = updates % rim_depth

        def run_group(group_number, carried):
            return deep_group(
                carried,
                group_number * rim_depth,
                rim_depth,
                absorb_wide,
                inside_wide,
                keeps,
                pushes,
            )

        state = lax.fori_loop(0, groups, run_group, state)
        state = deep_group(state, groups * rim_depth, rest, absorb_wide, inside_wide, keeps, pushes)
        potential = state[0] + state[1]
        source = fresh
    return jnp.where(is_para, voltage, potential)[None]


def solution(mesh):
    in_specs = (
        P("sec", "brick", None, None),
        P("sec", "brick", None, None),
        P("brick", None, None),
        P("brick", None, None),
        P("brick"),
    )
    out_specs = P("sec", "brick", None, None)
    return jax.shard_map(body, mesh=mesh, in_specs=in_specs, out_specs=out_specs, check_vma=False)
```

profile of v0, /device:TPU:105, one launch (start us, length us, event | category | flops | bytes accessed | tf_op | source)
XLA Modules:
  0.0 497.8 jit_solution(18343053124632734887)
XLA Ops:
  10.5 6.7 %collective-permute-start.24 = (f32[1,32,128]{2,1,0:T(8,128)S(1)}, f32[1,32,128]{2,1,0:T(8,128)S(1)}, u32[]{:S(2)}, u32[]{:S(2)}) collective-permute-start(f32[1,32,128]{2,1,0:T(8,128)S(1)} %get-tuple-element.799), channel_id=1, source_target_pairs={{1,0},{2,1},{3,2},{4,3},{5,4},{6,5},{7,6},{8,7},{9,8},{10,9},{11,1... | collective-permute-start | bytes 49160 | tf_op jit(solution)/shard_map/ppermute | solution.py:30
  25.9 7.9 %collective-permute-start.16 = (f32[1,32,128]{2,1,0:T(8,128)S(1)}, f32[1,32,128]{2,1,0:T(8,128)S(1)}, u32[]{:S(2)}, u32[]{:S(2)}) collective-permute-start(f32[1,32,128]{2,1,0:T(8,128)S(1)} %get-tuple-element.782), channel_id=1, source_target_pairs={{1,0},{2,1},{3,2},{4,3},{5,4},{6,5},{7,6},{8,7},{9,8},{10,9},{11,1... | collective-permute-start | bytes 49160 | tf_op jit(solution)/shard_map/ppermute | solution.py:30
  44.8 7.9 %collective-permute-start.20 = (f32[1,32,128]{2,1,0:T(8,128)S(1)}, f32[1,32,128]{2,1,0:T(8,128)S(1)}, u32[]{:S(2)}, u32[]{:S(2)}) collective-permute-start(f32[1,32,128]{2,1,0:T(8,128)S(1)} %get-tuple-element.804), channel_id=1, source_target_pairs={{1,0},{2,1},{3,2},{4,3},{5,4},{6,5},{7,6},{8,7},{9,8},{10,9},{11,1... | collective-permute-start | bytes 49160 | tf_op jit(solution)/shard_map/ppermute | solution.py:44
  70.8 7.5 %collective-permute-start.29 = (f32[4,40,128]{2,1,0:T(8,128)S(1)}, f32[4,40,128]{2,1,0:T(8,128)S(1)}, u32[]{:S(2)}, u32[]{:S(2)}) collective-permute-start(f32[4,40,128]{2,1,0:T(8,128)S(1)} %get-tuple-element.763), channel_id=1, source_target_pairs={{1,0},{2,1},{3,2},{4,3},{5,4},{6,5},{7,6},{8,7},{9,8},{10,9},{11,1... | collective-permute-start | bytes 245768 | tf_op jit(solution)/shard_map/ppermute | solution.py:30
  81.3 6.7 %collective-permute-done.28 = f32[4,40,128]{2,1,0:T(8,128)S(1)} collective-permute-done((f32[4,40,128]{2,1,0:T(8,128)S(1)}, f32[4,40,128]{2,1,0:T(8,128)S(1)}, u32[]{:S(2)}, u32[]{:S(2)}) %collective-permute-start.28) | collective-permute-done | bytes 81952 | tf_op jit(solution)/shard_map/ppermute | solution.py:29
  92.3 134.1 %while.42 = (s32[]{:T(128)}, f32[32,32,128]{2,1,0:T(8,128)}, f32[32,32,128]{2,1,0:T(8,128)S(1)}, f32[32,32,128]{2,1,0:T(8,128)S(1)}, f32[40,40,128]{2,1,0:T(8,12...) while((s32[]{:T(128)}, f32[32,32,128]{2,1,0:T(8,128)}, ...), condition=%wide.region_5.6_spmd.clone.clone, body=%wide.region_4.5_spmd.sunk.clone.clone.sunk | while | flops 10433554 | bytes 45280088 | solution.py:185
  112.1 6.4 %collective-permute-start.6 = (f32[4,40,128]{2,1,0:T(8,128)S(1)}, f32[4,40,128]{2,1,0:T(8,128)S(1)}, u32[]{:S(2)}, u32[]{:S(2)}) collective-permute-start(f32[4,40,128]{2,1,0:T(8,128)S(1)} %get-tuple-element.964), channel_id=1, source_target_pairs={{1,0},{2,1},{3,2},{4,3},{5,4},{6,5},{7,6},{8,7},{9,8},{10,9},{11,1... | collective-permute-start | bytes 245768 | tf_op jit(solution)/shard_map/while/body/eval_jaxpr/ppermute | solution.py:30
  120.7 7.6 %collective-permute-done.7 = f32[4,40,128]{2,1,0:T(8,128)S(1)} collective-permute-done((f32[4,40,128]{2,1,0:T(8,128)S(1)}, f32[4,40,128]{2,1,0:T(8,128)S(1)}, u32[]{:S(2)}, u32[]{:S(2)}) %collective-permute-start.7) | collective-permute-done | bytes 81952 | tf_op jit(solution)/shard_map/while/body/eval_jaxpr/ppermute | solution.py:29
  156.6 6.4 %collective-permute-start.6 = (f32[4,40,128]{2,1,0:T(8,128)S(1)}, f32[4,40,128]{2,1,0:T(8,128)S(1)}, u32[]{:S(2)}, u32[]{:S(2)}) collective-permute-start(f32[4,40,128]{2,1,0:T(8,128)S(1)} %get-tuple-element.964), channel_id=1, source_target_pairs={{1,0},{2,1},{3,2},{4,3},{5,4},{6,5},{7,6},{8,7},{9,8},{10,9},{11,1... | collective-permute-start | bytes 245768 | tf_op jit(solution)/shard_map/while/body/eval_jaxpr/ppermute | solution.py:30
  165.2 7.6 %collective-permute-done.7 = f32[4,40,128]{2,1,0:T(8,128)S(1)} collective-permute-done((f32[4,40,128]{2,1,0:T(8,128)S(1)}, f32[4,40,128]{2,1,0:T(8,128)S(1)}, u32[]{:S(2)}, u32[]{:S(2)}) %collective-permute-start.7) | collective-permute-done | bytes 81952 | tf_op jit(solution)/shard_map/while/body/eval_jaxpr/ppermute | solution.py:29
  201.2 6.4 %collective-permute-start.6 = (f32[4,40,128]{2,1,0:T(8,128)S(1)}, f32[4,40,128]{2,1,0:T(8,128)S(1)}, u32[]{:S(2)}, u32[]{:S(2)}) collective-permute-start(f32[4,40,128]{2,1,0:T(8,128)S(1)} %get-tuple-element.964), channel_id=1, source_target_pairs={{1,0},{2,1},{3,2},{4,3},{5,4},{6,5},{7,6},{8,7},{9,8},{10,9},{11,1... | collective-permute-start | bytes 245768 | tf_op jit(solution)/shard_map/while/body/eval_jaxpr/ppermute | solution.py:30
  209.8 7.6 %collective-permute-done.7 = f32[4,40,128]{2,1,0:T(8,128)S(1)} collective-permute-done((f32[4,40,128]{2,1,0:T(8,128)S(1)}, f32[4,40,128]{2,1,0:T(8,128)S(1)}, u32[]{:S(2)}, u32[]{:S(2)}) %collective-permute-start.7) | collective-permute-done | bytes 81952 | tf_op jit(solution)/shard_map/while/body/eval_jaxpr/ppermute | solution.py:29
  252.8 7.9 %collective-permute-start.22 = (f32[1,32,128]{2,1,0:T(8,128)S(1)}, f32[1,32,128]{2,1,0:T(8,128)S(1)}, u32[]{:S(2)}, u32[]{:S(2)}) collective-permute-start(f32[1,32,128]{2,1,0:T(8,128)S(1)} %get-tuple-element.769), channel_id=1, source_target_pairs={{1,0},{2,1},{3,2},{4,3},{5,4},{6,5},{7,6},{8,7},{9,8},{10,9},{11,1... | collective-permute-start | bytes 49160 | tf_op jit(solution)/shard_map/ppermute | solution.py:30
  266.1 6.4 %collective-permute-start.41 = (f32[4,40,128]{2,1,0:T(8,128)S(1)}, f32[4,40,128]{2,1,0:T(8,128)S(1)}, u32[]{:S(2)}, u32[]{:S(2)}) collective-permute-start(f32[4,40,128]{2,1,0:T(8,128)S(1)} %get-tuple-element.757), channel_id=1, source_target_pairs={{1,0},{2,1},{3,2},{4,3},{5,4},{6,5},{7,6},{8,7},{9,8},{10,9},{11,1... | collective-permute-start | bytes 245768 | tf_op jit(solution)/shard_map/ppermute | solution.py:30
  274.7 7.6 %collective-permute-done.40 = f32[4,40,128]{2,1,0:T(8,128)S(1)} collective-permute-done((f32[4,40,128]{2,1,0:T(8,128)S(1)}, f32[4,40,128]{2,1,0:T(8,128)S(1)}, u32[]{:S(2)}, u32[]{:S(2)}) %collective-permute-start.40) | collective-permute-done | bytes 81952 | tf_op jit(solution)/shard_map/ppermute | solution.py:29
  295.4 7.9 %collective-permute-start.44 = (f32[1,32,128]{2,1,0:T(8,128)S(1)}, f32[1,32,128]{2,1,0:T(8,128)S(1)}, u32[]{:S(2)}, u32[]{:S(2)}) collective-permute-start(f32[1,32,128]{2,1,0:T(8,128)S(1)} %get-tuple-element.786), channel_id=1, source_target_pairs={{1,0},{2,1},{3,2},{4,3},{5,4},{6,5},{7,6},{8,7},{9,8},{10,9},{11,1... | collective-permute-start | bytes 49160 | tf_op jit(solution)/shard_map/ppermute | solution.py:44
  308.6 139.0 %while.43 = (s32[]{:T(128)}, f32[32,32,128]{2,1,0:T(8,128)}, f32[32,32,128]{2,1,0:T(8,128)S(1)}, f32[32,32,128]{2,1,0:T(8,128)S(1)}, f32[40,40,128]{2,1,0:T(8,12...) while((s32[]{:T(128)}, f32[32,32,128]{2,1,0:T(8,128)}, ...), condition=%wide.region_7.8_spmd.clone.clone, body=%wide.region_6.7_spmd.sunk.clone.clone.sunk | while | flops 10433554 | bytes 45280088 | solution.py:185
  321.1 8.4 %collective-permute-start.10 = (f32[4,40,128]{2,1,0:T(8,128)S(1)}, f32[4,40,128]{2,1,0:T(8,128)S(1)}, u32[]{:S(2)}, u32[]{:S(2)}) collective-permute-start(f32[4,40,128]{2,1,0:T(8,128)S(1)} %get-tuple-element.993), channel_id=1, source_target_pairs={{1,0},{2,1},{3,2},{4,3},{5,4},{6,5},{7,6},{8,7},{9,8},{10,9},{11,1... | collective-permute-start | bytes 245768 | tf_op jit(solution)/shard_map/while/body/eval_jaxpr/ppermute | solution.py:30
  331.5 7.9 %collective-permute-start.14 = (f32[4,40,128]{2,1,0:T(8,128)S(1)}, f32[4,40,128]{2,1,0:T(8,128)S(1)}, u32[]{:S(2)}, u32[]{:S(2)}) collective-permute-start(f32[4,40,128]{2,1,0:T(8,128)S(1)} %get-tuple-element.997), channel_id=1, source_target_pairs={{1,0},{2,1},{3,2},{4,3},{5,4},{6,5},{7,6},{8,7},{9,8},{10,9},{11,1... | collective-permute-start | bytes 245768 | tf_op jit(solution)/shard_map/while/body/eval_jaxpr/ppermute | solution.py:30
  341.5 7.6 %collective-permute-done.15 = f32[4,40,128]{2,1,0:T(8,128)S(1)} collective-permute-done((f32[4,40,128]{2,1,0:T(8,128)S(1)}, f32[4,40,128]{2,1,0:T(8,128)S(1)}, u32[]{:S(2)}, u32[]{:S(2)}) %collective-permute-start.15) | collective-permute-done | bytes 81952 | tf_op jit(solution)/shard_map/while/body/eval_jaxpr/ppermute | solution.py:29
  386.5 7.6 %collective-permute-done.15 = f32[4,40,128]{2,1,0:T(8,128)S(1)} collective-permute-done((f32[4,40,128]{2,1,0:T(8,128)S(1)}, f32[4,40,128]{2,1,0:T(8,128)S(1)}, u32[]{:S(2)}, u32[]{:S(2)}) %collective-permute-start.15) | collective-permute-done | bytes 81952 | tf_op jit(solution)/shard_map/while/body/eval_jaxpr/ppermute | solution.py:29
  422.4 6.4 %collective-permute-start.14 = (f32[4,40,128]{2,1,0:T(8,128)S(1)}, f32[4,40,128]{2,1,0:T(8,128)S(1)}, u32[]{:S(2)}, u32[]{:S(2)}) collective-permute-start(f32[4,40,128]{2,1,0:T(8,128)S(1)} %get-tuple-element.997), channel_id=1, source_target_pairs={{1,0},{2,1},{3,2},{4,3},{5,4},{6,5},{7,6},{8,7},{9,8},{10,9},{11,1... | collective-permute-start | bytes 245768 | tf_op jit(solution)/shard_map/while/body/eval_jaxpr/ppermute | solution.py:30
  431.0 7.6 %collective-permute-done.15 = f32[4,40,128]{2,1,0:T(8,128)S(1)} collective-permute-done((f32[4,40,128]{2,1,0:T(8,128)S(1)}, f32[4,40,128]{2,1,0:T(8,128)S(1)}, u32[]{:S(2)}, u32[]{:S(2)}) %collective-permute-start.15) | collective-permute-done | bytes 81952 | tf_op jit(solution)/shard_map/while/body/eval_jaxpr/ppermute | solution.py:29
  473.8 7.4 %collective-permute-done.52 = f32[4,40,128]{2,1,0:T(8,128)S(1)} collective-permute-done((f32[4,40,128]{2,1,0:T(8,128)S(1)}, f32[4,40,128]{2,1,0:T(8,128)S(1)}, u32[]{:S(2)}, u32[]{:S(2)}) %collective-permute-start.52) | collective-permute-done | bytes 81952 | tf_op jit(solution)/shard_map/ppermute | solution.py:29
  (393 shorter events, 328.4 us)
Async XLA Ops:
  6.5 82.5 %all-gather.11.cloned.1.call-start = ((), (), s32[]{:S(2)}) async-start(), calls=%async_computation.1 | async-start | bytes 2621440 | tf_op jit(solution)/shard_map/all_gather | solution.py:56
  7.4 27.8 %collective-permute-start.25 = (f32[1,32,128]{2,1,0:T(8,128)S(1)}, f32[1,32,128]{2,1,0:T(8,128)S(1)}, u32[]{:S(2)}, u32[]{:S(2)}) collective-permute-start(f32[1,32,128]{2,1,0:T(8,128)S(1)} %get-tuple-element.798), channel_id=1, source_target_pairs={{0,1},{1,2},{2,3},{3,4},{4,5},{5,6},{6,7},{7,8},{8,9},{9,10},{10,1... | collective-permute-start | bytes 49160 | tf_op jit(solution)/shard_map/ppermute | solution.py:29
  10.5 24.7 %collective-permute-start.24 = (f32[1,32,128]{2,1,0:T(8,128)S(1)}, f32[1,32,128]{2,1,0:T(8,128)S(1)}, u32[]{:S(2)}, u32[]{:S(2)}) collective-permute-start(f32[1,32,128]{2,1,0:T(8,128)S(1)} %get-tuple-element.799), channel_id=1, source_target_pairs={{1,0},{2,1},{3,2},{4,3},{5,4},{6,5},{7,6},{8,7},{9,8},{10,9},{11,1... | collective-permute-start | bytes 49160 | tf_op jit(solution)/shard_map/ppermute | solution.py:30
  38.4 196.6 %all-gather.9.cloned.1.call-start = ((), (), s32[]{:S(2)}) async-start(), calls=%async_computation | async-start | bytes 2621440 | tf_op jit(solution)/shard_map/all_gather | solution.py:56
  38.6 19.9 %collective-permute-start.18 = (f32[32,1,128]{2,1,0:T(1,128)S(1)}, f32[32,1,128]{2,1,0:T(1,128)S(1)}, u32[]{:S(2)}, u32[]{:S(2)}) collective-permute-start(f32[32,1,128]{2,1,0:T(1,128)S(1)} %get-tuple-element.807), channel_id=1, source_target_pairs={{0,32},{32,64},{64,96},{1,33},{33,65},{65,97},{2,34},{34,66},{66,9... | collective-permute-start | bytes 49160 | tf_op jit(solution)/shard_map/ppermute | solution.py:43
  39.9 19.9 %collective-permute-start.19 = (f32[32,1,128]{2,1,0:T(1,128)S(1)}, f32[32,1,128]{2,1,0:T(1,128)S(1)}, u32[]{:S(2)}, u32[]{:S(2)}) collective-permute-start(f32[32,1,128]{2,1,0:T(1,128)S(1)} %get-tuple-element.806), channel_id=1, source_target_pairs={{32,0},{64,32},{96,64},{33,1},{65,33},{97,65},{34,2},{66,34},{98,6... | collective-permute-start | bytes 49160 | tf_op jit(solution)/shard_map/ppermute | solution.py:44
  42.9 19.9 %collective-permute-start.21 = (f32[1,32,128]{2,1,0:T(8,128)S(1)}, f32[1,32,128]{2,1,0:T(8,128)S(1)}, u32[]{:S(2)}, u32[]{:S(2)}) collective-permute-start(f32[1,32,128]{2,1,0:T(8,128)S(1)} %get-tuple-element.805), channel_id=1, source_target_pairs={{0,1},{1,2},{2,3},{3,4},{4,5},{5,6},{6,7},{7,8},{8,9},{9,10},{10,1... | collective-permute-start | bytes 49160 | tf_op jit(solution)/shard_map/ppermute | solution.py:43
  44.8 19.3 %collective-permute-start.20 = (f32[1,32,128]{2,1,0:T(8,128)S(1)}, f32[1,32,128]{2,1,0:T(8,128)S(1)}, u32[]{:S(2)}, u32[]{:S(2)}) collective-permute-start(f32[1,32,128]{2,1,0:T(8,128)S(1)} %get-tuple-element.804), channel_id=1, source_target_pairs={{1,0},{2,1},{3,2},{4,3},{5,4},{6,5},{7,6},{8,7},{9,8},{10,9},{11,1... | collective-permute-start | bytes 49160 | tf_op jit(solution)/shard_map/ppermute | solution.py:44
  65.3 240.0 %all-gather.15.cloned.1.call-start = ((), (), s32[]{:S(2)}) async-start(), calls=%async_computation.3 | async-start | bytes 2621440 | tf_op jit(solution)/shard_map/all_gather | solution.py:56
  65.5 14.8 %collective-permute-start.33 = (f32[4,40,128]{2,1,0:T(8,128)S(1)}, f32[4,40,128]{2,1,0:T(8,128)S(1)}, u32[]{:S(2)}, u32[]{:S(2)}) collective-permute-start(f32[4,40,128]{2,1,0:T(8,128)S(1)} %get-tuple-element.761), channel_id=1, source_target_pairs={{1,0},{2,1},{3,2},{4,3},{5,4},{6,5},{7,6},{8,7},{9,8},{10,9},{11,1... | collective-permute-start | bytes 245768 | tf_op jit(solution)/shard_map/ppermute | solution.py:30
  151.3 13.7 %collective-permute-start.2 = (f32[4,40,128]{2,1,0:T(8,128)S(1)}, f32[4,40,128]{2,1,0:T(8,128)S(1)}, u32[]{:S(2)}, u32[]{:S(2)}) collective-permute-start(f32[4,40,128]{2,1,0:T(8,128)S(1)} %get-tuple-element.960), channel_id=1, source_target_pairs={{1,0},{2,1},{3,2},{4,3},{5,4},{6,5},{7,6},{8,7},{9,8},{10,9},{11,1... | collective-permute-start | bytes 245768 | tf_op jit(solution)/shard_map/while/body/eval_jaxpr/ppermute | solution.py:30
  195.8 13.7 %collective-permute-start.2 = (f32[4,40,128]{2,1,0:T(8,128)S(1)}, f32[4,40,128]{2,1,0:T(8,128)S(1)}, u32[]{:S(2)}, u32[]{:S(2)}) collective-permute-start(f32[4,40,128]{2,1,0:T(8,128)S(1)} %get-tuple-element.960), channel_id=1, source_target_pairs={{1,0},{2,1},{3,2},{4,3},{5,4},{6,5},{7,6},{8,7},{9,8},{10,9},{11,1... | collective-permute-start | bytes 245768 | tf_op jit(solution)/shard_map/while/body/eval_jaxpr/ppermute | solution.py:30
  227.1 25.7 %collective-permute-start.35 = (f32[32,4,128]{2,1,0:T(4,128)}, f32[32,4,128]{2,1,0:T(4,128)S(1)}, u32[]{:S(2)}, u32[]{:S(2)}) collective-permute-start(f32[32,4,128]{2,1,0:T(4,128)} %get-tuple-element.793), channel_id=1, source_target_pairs={{32,0},{64,32},{96,64},{33,1},{65,33},{97,65},{34,2},{66,34},{98,6... | collective-permute-start | bytes 196616 | tf_op jit(solution)/shard_map/ppermute | solution.py:30
  233.0 27.6 %collective-permute-start.34 = (f32[32,4,128]{2,1,0:T(4,128)}, f32[32,4,128]{2,1,0:T(4,128)S(1)}, u32[]{:S(2)}, u32[]{:S(2)}) collective-permute-start(f32[32,4,128]{2,1,0:T(4,128)} %get-tuple-element.792), channel_id=1, source_target_pairs={{0,32},{32,64},{64,96},{1,33},{33,65},{65,97},{2,34},{34,66},{66,9... | collective-permute-start | bytes 196616 | tf_op jit(solution)/shard_map/ppermute | solution.py:29
  239.6 246.7 %all-gather.13.cloned.1.call-start = ((), (), s32[]{:S(2)}) async-start(), calls=%async_computation.2 | async-start | bytes 2621440 | tf_op jit(solution)/shard_map/all_gather | solution.py:56
  248.3 14.4 %collective-permute-start.39 = (f32[32,4,128]{2,1,0:T(4,128)}, f32[32,4,128]{2,1,0:T(4,128)S(1)}, u32[]{:S(2)}, u32[]{:S(2)}) collective-permute-start(f32[32,4,128]{2,1,0:T(4,128)} %get-tuple-element.791), channel_id=1, source_target_pairs={{32,0},{64,32},{96,64},{33,1},{65,33},{97,65},{34,2},{66,34},{98,6... | collective-permute-start | bytes 196616 | tf_op jit(solution)/shard_map/ppermute | solution.py:30
  249.6 16.5 %collective-permute-start.38 = (f32[32,4,128]{2,1,0:T(4,128)S(1)}, f32[32,4,128]{2,1,0:T(4,128)S(1)}, u32[]{:S(2)}, u32[]{:S(2)}) collective-permute-start(f32[32,4,128]{2,1,0:T(4,128)S(1)} %copy-done.30), channel_id=1, source_target_pairs={{0,32},{32,64},{64,96},{1,33},{33,65},{65,97},{2,34},{34,66},{66,9... | collective-permute-start | bytes 196616 | tf_op jit(solution)/shard_map/ppermute | solution.py:29
  250.9 44.5 %collective-permute-start.23 = (f32[1,32,128]{2,1,0:T(8,128)S(1)}, f32[1,32,128]{2,1,0:T(8,128)S(1)}, u32[]{:S(2)}, u32[]{:S(2)}) collective-permute-start(f32[1,32,128]{2,1,0:T(8,128)S(1)} %get-tuple-element.768), channel_id=1, source_target_pairs={{0,1},{1,2},{2,3},{3,4},{4,5},{5,6},{6,7},{7,8},{8,9},{9,10},{10,1... | collective-permute-start | bytes 49160 | tf_op jit(solution)/shard_map/ppermute | solution.py:29
  252.8 50.5 %collective-permute-start.22 = (f32[1,32,128]{2,1,0:T(8,128)S(1)}, f32[1,32,128]{2,1,0:T(8,128)S(1)}, u32[]{:S(2)}, u32[]{:S(2)}) collective-permute-start(f32[1,32,128]{2,1,0:T(8,128)S(1)} %get-tuple-element.769), channel_id=1, source_target_pairs={{1,0},{2,1},{3,2},{4,3},{5,4},{6,5},{7,6},{8,7},{9,8},{10,9},{11,1... | collective-permute-start | bytes 49160 | tf_op jit(solution)/shard_map/ppermute | solution.py:30
  286.2 17.7 %collective-permute-start.42 = (f32[32,1,128]{2,1,0:T(1,128)S(1)}, f32[32,1,128]{2,1,0:T(1,128)S(1)}, u32[]{:S(2)}, u32[]{:S(2)}) collective-permute-start(f32[32,1,128]{2,1,0:T(1,128)S(1)} %get-tuple-element.789), channel_id=1, source_target_pairs={{0,32},{32,64},{64,96},{1,33},{33,65},{65,97},{2,34},{34,66},{66,9... | collective-permute-start | bytes 49160 | tf_op jit(solution)/shard_map/ppermute | solution.py:43
  287.5 16.4 %collective-permute-start.43 = (f32[32,1,128]{2,1,0:T(1,128)S(1)}, f32[32,1,128]{2,1,0:T(1,128)S(1)}, u32[]{:S(2)}, u32[]{:S(2)}) collective-permute-start(f32[32,1,128]{2,1,0:T(1,128)S(1)} %get-tuple-element.788), channel_id=1, source_target_pairs={{32,0},{64,32},{96,64},{33,1},{65,33},{97,65},{34,2},{66,34},{98,6... | collective-permute-start | bytes 49160 | tf_op jit(solution)/shard_map/ppermute | solution.py:44
  316.0 15.5 %collective-permute-start.12 = (f32[32,4,128]{2,1,0:T(4,128)}, f32[32,4,128]{2,1,0:T(4,128)S(1)}, u32[]{:S(2)}, u32[]{:S(2)}) collective-permute-start(f32[32,4,128]{2,1,0:T(4,128)} %get-tuple-element.995), channel_id=1, source_target_pairs={{32,0},{64,32},{96,64},{33,1},{65,33},{97,65},{34,2},{66,34},{98,6... | collective-permute-start | bytes 196616 | tf_op jit(solution)/shard_map/while/body/eval_jaxpr/ppermute | solution.py:30
  321.1 20.2 %collective-permute-start.10 = (f32[4,40,128]{2,1,0:T(8,128)S(1)}, f32[4,40,128]{2,1,0:T(8,128)S(1)}, u32[]{:S(2)}, u32[]{:S(2)}) collective-permute-start(f32[4,40,128]{2,1,0:T(8,128)S(1)} %get-tuple-element.993), channel_id=1, source_target_pairs={{1,0},{2,1},{3,2},{4,3},{5,4},{6,5},{7,6},{8,7},{9,8},{10,9},{11,1... | collective-permute-start | bytes 245768 | tf_op jit(solution)/shard_map/while/body/eval_jaxpr/ppermute | solution.py:30
  459.6 13.9 %collective-permute-start.49 = (f32[4,40,128]{2,1,0:T(8,128)S(1)}, f32[4,40,128]{2,1,0:T(8,128)S(1)}, u32[]{:S(2)}, u32[]{:S(2)}) collective-permute-start(f32[4,40,128]{2,1,0:T(8,128)S(1)} %get-tuple-element.753), channel_id=1, source_target_pairs={{1,0},{2,1},{3,2},{4,3},{5,4},{6,5},{7,6},{8,7},{9,8},{10,9},{11,1... | collective-permute-start | bytes 245768 | tf_op jit(solution)/shard_map/ppermute | solution.py:30
  (105 other events, 839.0 us)
Sparse Core Ops, SparseCore 0:
  38.5 31.6 all-gather.10
  71.9 31.9 all-gather.8
  239.7 29.5 all-gather.14
  305.4 38.0 all-gather.12
where the time goes:
time: 505 us; the launch traced here: 498 us
  starting transfers between devices  292 us (58%)
  other arithmetic  89.6 us (18%)
  waiting for transfers between devices  67.6 us (13%)
  local copies, waits for them, and re-layouts  32.7 us (6%)
  between operations  14.8 us (3%)
    ppermute x39, starting transfers between devices, extended_2(): after = lax.ppermute(initial, axis, down)  185 us
    ppermute x39, starting transfers between devices, extended_2(): before = lax.ppermute(last, axis, up)  75.5 us
    ppermute x39, waiting for transfers between devices, extended_2(): before = lax.ppermute(last, axis, up)  67.2 us
    add x28, other arithmetic, deep_group(): wide_dir = keeps[first + offset] * inner + pushes[first + offset] * wide_res  51.4 us
    ppermute x4, starting transfers between devices, with_halo(): lax.ppermute(initial, axis, [(b, a) for a, b in up])  24.7 us
  transfers between devices with their start and end apart: 90, of which 10 were waited for; matrix products, arithmetic and copies ran while one was open for 21% of the time, Pallas kernels for 0%

commit v1 on v0

v1 whole, which is shorter than its diff:
```python
import jax
import jax.numpy as jnp
from jax import lax
from jax.experimental import pallas as pl
from jax.experimental.pallas import tpu as pltpu
from jax.sharding import PartitionSpec as P

SUBSTEPS = 8
SWEEPS = 16

coupling_gain = 0.1
ionic_timestep = 0.05
ionic_gain = 8.0
recovery_rate = 0.1
recovery_decay = 0.5
spectrum_low = 0.04
spectrum_high = 12.32

SLAB = 8
ROWS = 96
HEART = 32
SLOTS = 40
OWN = 16
PAD = 8
AXES = ("sec", "brick")
V0_AT, V1_AT, D_AT, ROW_AT, MSG = 96, 128, 160, 256, 264
PHI_PAD = 112
V_PAD = 48


def chebyshev_weights(count):
    center = 0.5 * (spectrum_high + spectrum_low)
    spread = 0.5 * (spectrum_high - spectrum_low)
    ratio = center / spread
    current = 1.0 / ratio
    weights = [(0.0, 1.0 / center)]
    for number in range(count):
        following = 1.0 / (2.0 * ratio - current)
        weights.append((following * current, 2.0 * following / spread))
        current = following
    return weights


WEIGHTS = chebyshev_weights(SWEEPS - 1)


def ionic(voltage, recovery, threshold, active):
    for substep in range(SUBSTEPS):
        drive = ionic_gain * voltage * (voltage - threshold) * (1.0 - voltage) - recovery
        relax = recovery_rate * (voltage - recovery_decay * recovery)
        voltage = voltage + ionic_timestep * active * drive
        recovery = recovery + ionic_timestep * active * relax
    return voltage, recovery


def lanes(shape):
    return lax.broadcasted_iota(jnp.int32, shape, len(shape) - 1)


def side_sum_zero(value):
    lane = lanes(value.shape)
    before = jnp.where(lane == 0, 0.0, pltpu.roll(value, 1, 1))
    after = jnp.where(lane == 127, 0.0, pltpu.roll(value, 127, 1))
    return before + after


def side_sum_edge(value):
    lane = lanes(value.shape)
    before = jnp.where(lane == 0, value, pltpu.roll(value, 1, 1))
    after = jnp.where(lane == 127, value, pltpu.roll(value, 127, 1))
    return before + after


def heart_laplace(ref, x):
    here = ref[x, PAD : PAD + HEART]
    total = ref[x - 1, PAD : PAD + HEART] + ref[x + 1, PAD : PAD + HEART]
    total = total + ref[x, PAD - 1 : PAD - 1 + HEART] + ref[x, PAD + 1 : PAD + 1 + HEART]
    return total + side_sum_edge(here) - 6.0 * here


def put_heart(ref, x, value):
    ref[x, PAD : PAD + HEART] = value
    ref[x, PAD - 1 : PAD] = value[0:1]
    ref[x, PAD + HEART : PAD + HEART + 1] = value[HEART - 1 : HEART]


def torso_current(ref, x, row):
    at = PAD + HEART * row
    here = ref[x, at : at + HEART]
    total = ref[x - 1, at : at + HEART] + ref[x + 1, at : at + HEART]
    total = total + ref[x, at - 1 : at - 1 + HEART] + ref[x, at + 1 : at + 1 + HEART]
    return total + side_sum_zero(here) - 6.0 * here


def solve(scal, even, odd, absorb, source):
    low_end, high_end = scal[4], scal[5]
    for level, (keep, push) in enumerate(WEIGHTS, 1):
        src, dst = (even, odd) if level % 2 else (odd, even)
        shift = 6.0 - (1.0 + keep) / push

        def plane(x, carry, src=src, dst=dst, keep=keep, push=push, shift=shift, level=level):
            for start in range(0, ROWS, 48):
                at, to = PAD + start, PAD + start + 48
                here = src[x, at:to]
                total = src[x - 1, at:to] + src[x + 1, at:to]
                total = total + (src[x, at - 1 : to - 1] + src[x, at + 1 : to + 1])
                total = total + side_sum_zero(here)
                total = total + source[x, start : start + 48]
                total = total - (absorb[x, start : start + 48] + shift) * here
                if level == 1:
                    dst[x, at:to] = push * total
                else:
                    dst[x, at:to] = push * total - keep * dst[x, at:to]
            return carry

        lax.fori_loop(
            jnp.maximum(level, low_end), jnp.minimum(SLOTS - level, high_end), plane, 0
        )


def clear_edges(even, odd):
    zero = jnp.zeros((PAD, 128), jnp.float32)

    def edge(x, carry):
        for ref in (even, odd):
            ref[x, 0:PAD] = zero
            ref[x, PAD + ROWS : PHI_PAD] = zero
        return carry

    lax.fori_loop(0, SLOTS, edge, 0)
    none = jnp.zeros((PHI_PAD, 128), jnp.float32)
    odd[OWN - 1] = none
    odd[OWN + 2 * SLAB] = none


def slots():
    return ((0, OWN, 1), (1, OWN + 2 * SLAB - 1, -1), (2, OWN - 1, -1), (3, 0, 1), (4, OWN + 2 * SLAB, 1))


def gather_kernel(scal, pot, coef, rec, exc, got_1, got_2, got_3, msg, aux, deep):
    sec, chunk, flip = scal[0], scal[1], scal[2]
    strip = jnp.full((8, 128), scal[3].astype(jnp.float32))

    def plane(u, carry):
        x = jnp.where(flip == 1, SLAB - 1 - u, u)
        whole = SLAB * chunk + x
        for number, ref in enumerate((None, got_1, got_2, got_3)):
            at = pl.multiple_of((sec ^ number) * HEART, HEART)
            if number == 0:
                msg[u, pl.ds(at, HEART)] = pot[whole]
                deep[u, pl.ds(at, HEART)] = coef[whole]
            else:
                msg[u, pl.ds(at, HEART)] = ref[0, x]
                deep[u, pl.ds(at, HEART)] = ref[1, x]
        msg[u, D_AT : D_AT + ROWS] = deep[u, 0:ROWS]
        threshold = deep[u, ROWS : ROWS + HEART]
        active = exc[whole].astype(jnp.float32)
        voltage, recovery = ionic(msg[u, V0_AT : V0_AT + HEART], rec[whole], threshold, active)
        msg[u, V1_AT : V1_AT + HEART] = voltage
        msg[u, ROW_AT : ROW_AT + 8] = strip
        aux[0, u] = threshold
        aux[1, u] = recovery
        aux[2, u] = active
        return carry

    lax.fori_loop(0, SLAB, plane, 0)


def first_kernel(scal, own, on, near, far, on2, aux, msg, held, absorb, later, even, odd, source, volt, volt_1):
    refs = (own, on, near, far, on2)
    clear_edges(even, odd)
    for number, first, step in slots():
        ref = refs[number]

        def unpack(u, carry, ref=ref, first=first, step=step):
            x = first + step * u
            even[x, PAD : PAD + ROWS] = ref[u, 0:ROWS]
            absorb[x] = ref[u, D_AT : D_AT + ROWS]
            put_heart(volt, x, ref[u, V0_AT : V0_AT + HEART])
            put_heart(volt_1, x, ref[u, V1_AT : V1_AT + HEART])
            return carry

        lax.fori_loop(0, SLAB, unpack, 0)

    @pl.when(scal[4] == OWN)
    def _():
        for ref in (volt, volt_1):
            ref[OWN - 1] = ref[OWN]

    @pl.when(scal[5] == OWN + 2 * SLAB)
    def _():
        for ref in (volt, volt_1):
            ref[OWN + 2 * SLAB] = ref[OWN + 2 * SLAB - 1]

    row = scal[3].astype(jnp.float32)
    for low, high, mark in (
        (1, OWN, near[0, ROW_AT : ROW_AT + 1]),
        (OWN, OWN + 2 * SLAB, jnp.full((1, 128), row)),
        (OWN + 2 * SLAB, SLOTS - 1, on2[0, ROW_AT : ROW_AT + 1]),
    ):
        mark = jnp.broadcast_to(mark, (HEART, 128))

        def place(x, carry, mark=mark):
            for ref, out in ((volt, source), (volt_1, later)):
                gain = heart_laplace(ref, x)
                for layer in range(3):
                    out[x, layer * HEART : (layer + 1) * HEART] = jnp.where(
                        mark == layer, gain, 0.0
                    )
            return carry

        lax.fori_loop(low, high, place, 0)

    for layer in range(3):

        @pl.when(scal[3] == layer)
        def _():
            def heart(u, carry):
                x = OWN + u
                gain = heart_laplace(volt_1, x) + torso_current(even, x, layer)
                voltage = volt_1[x, PAD : PAD + HEART] + coupling_gain * gain
                voltage, _ = ionic(voltage, aux[1, u], aux[0, u], aux[2, u])
                held[u] = voltage
                return carry

            lax.fori_loop(0, SLAB, heart, 0)

    solve(scal, even, odd, absorb, source)
    for u in range(SLAB):
        msg[u] = even[OWN + u, PAD : PAD + ROWS]
    msg[SLAB, 0:HEART] = held[0]
    msg[SLAB, HEART : 2 * HEART] = held[SLAB - 1]
    msg[SLAB, 2 * HEART : ROWS] = jnp.zeros((HEART, 128), jnp.float32)


def second_kernel(scal, own, on, near, far, on2, held, absorb, source, out, even, odd, volt, joined):
    refs = (own, on, near, far, on2)
    clear_edges(even, odd)
    for number, first, step in slots():
        ref = refs[number]

        def unpack(u, carry, ref=ref, first=first, step=step):
            even[first + step * u, PAD : PAD + ROWS] = ref[u]
            return carry

        lax.fori_loop(0, SLAB, unpack, 0)

    def keep(u, carry):
        put_heart(volt, u + 1, held[u])
        return carry

    lax.fori_loop(0, SLAB, keep, 0)
    put_heart(volt, 0, near[SLAB, 0:HEART])
    put_heart(volt, SLAB + 1, on[SLAB, HEART : 2 * HEART])

    @pl.when(scal[4] == OWN)
    def _():
        volt[0] = volt[1]

    for layer in range(3):

        @pl.when(scal[3] == layer)
        def _():
            def heart(u, carry):
                gain = heart_laplace(volt, u + 1) + torso_current(even, OWN + u, layer)
                joined[u, ROWS : ROWS + HEART] = held[u] + coupling_gain * gain
                return carry

            lax.fori_loop(0, SLAB, heart, 0)

    solve(scal, even, odd, absorb, source)

    sec, flip = scal[0], scal[2]

    def plane(u, carry):
        joined[u, 0:ROWS] = even[OWN + u, PAD : PAD + ROWS]
        x = jnp.where(flip == 1, SLAB - 1 - u, u)
        for number in range(4):
            at = pl.multiple_of((sec ^ number) * HEART, HEART)
            out[number, x] = joined[u, pl.ds(at, HEART)]
        return carry

    lax.fori_loop(0, SLAB, plane, 0)


def spread_kernel(scal, own, got_1, got_2, got_3, out):
    for number, ref in enumerate((own, got_1, got_2, got_3)):
        at = scal[6 + number] * SLAB
        for u in range(SLAB):
            out[at + u] = ref[u]


def chain(sections, bricks):
    order = []
    for brick in range(bricks):
        forward = (brick + brick // 4) % 2 == 1
        for step in range(sections):
            sec = step if forward else sections - 1 - step
            order.append(sec * bricks + brick)
    return order


VMEM = pl.BlockSpec(memory_space=pltpu.VMEM)
SMEM = pl.BlockSpec(memory_space=pltpu.SMEM)


def call(kernel, args, outs, scratch, name, flops):
    arrays = [jax.ShapeDtypeStruct(shape, jnp.float32) for shape in outs]
    return pl.pallas_call(
        kernel,
        out_shape=arrays,
        in_specs=[SMEM] + [VMEM] * (len(args) - 1),
        out_specs=[VMEM] * len(outs),
        scratch_shapes=[pltpu.VMEM(shape, jnp.float32) for shape in scratch],
        cost_estimate=pl.CostEstimate(flops=flops, bytes_accessed=4000000, transcendentals=0),
        name=name,
    )(*args)


def body(potentials, coefficient, recovery, excitable, row_of):
    pot, coef = potentials[0], coefficient[0]
    sections, bricks = lax.axis_size("sec"), lax.axis_size("brick")
    order = chain(sections, bricks)
    count = len(order)
    last = count - 1
    partner = [(order[i], order[i ^ 1]) for i in range(count)]
    facing = []
    for i in range(1, last, 2):
        facing += [(order[i], order[i + 1]), (order[i + 1], order[i])]
    beyond = [(order[i], order[i + 2]) for i in range(0, count - 2, 2)]
    beyond += [(order[i], order[i - 2]) for i in range(3, count, 2)]

    def across(number):
        return [(sec, sec ^ number) for sec in range(sections)]

    sec = lax.axis_index("sec")
    brick = lax.axis_index("brick")
    forward = (brick + brick // 4) % 2 == 1

    def chunk_of(section):
        return jnp.where(forward, section, sections - 1 - section)

    chunk = chunk_of(sec)
    place = brick * sections + chunk
    no_facing = (place == 0) | (place == last)
    partner_end = (place == 1) | (place == last - 1)
    scal = jnp.stack(
        [
            sec,
            chunk,
            chunk % 2,
            row_of[0],
            jnp.where(no_facing, OWN, 0),
            jnp.where(partner_end, OWN + 2 * SLAB, SLOTS),
        ]
        + [chunk_of(sec ^ number) for number in range(4)]
    ).astype(jnp.int32)

    got = []
    for number in (1, 2, 3):
        start = SLAB * chunk_of(sec ^ number)
        piece = jnp.stack(
            [
                lax.dynamic_slice_in_dim(pot, start, SLAB, 0),
                lax.dynamic_slice_in_dim(coef, start, SLAB, 0),
            ]
        )
        got.append(lax.ppermute(piece, "sec", across(number)))

    msg, aux = call(
        gather_kernel,
        (scal, pot, coef, recovery, excitable, *got),
        [(SLAB, MSG, 128), (3, SLAB, HEART, 128)],
        [(SLAB, 128, 128)],
        "gather",
        4_000_000,
    )

    def halos(value):
        near = lax.ppermute(value, AXES, facing)
        far = lax.ppermute(value, AXES, beyond)
        on = lax.ppermute(value, AXES, partner)
        on2 = lax.ppermute(near, AXES, partner)
        return value, on, near, far, on2

    phi = (SLOTS, PHI_PAD, 128)
    wide = (SLOTS, ROWS, 128)
    volt = (SLOTS, V_PAD, 128)
    msg, held, absorb, later = call(
        first_kernel,
        (scal, *halos(msg), aux),
        [(SLAB + 1, ROWS, 128), (SLAB, HEART, 128), wide, wide],
        [phi, phi, wide, volt, volt],
        "first",
        80_000_000,
    )
    (out,) = call(
        second_kernel,
        (scal, *halos(msg), held, absorb, later),
        [(4, SLAB, HEART, 128)],
        [phi, phi, (SLAB + 2, V_PAD, 128), (SLAB, 128, 128)],
        "second",
        80_000_000,
    )
    back = [out[0]] + [lax.ppermute(out[number], "sec", across(number)) for number in (1, 2, 3)]
    (result,) = call(
        spread_kernel,
        (scal, *back),
        [(sections * SLAB, HEART, 128)],
        [],
        "spread",
        100_000,
    )
    return result[None]


def solution(mesh):
    in_specs = (
        P("sec", "brick", None, None),
        P("sec", "brick", None, None),
        P("brick", None, None),
        P("brick", None, None),
        P("brick"),
    )
    out_specs = P("sec", "brick", None, None)
    return jax.shard_map(body, mesh=mesh, in_specs=in_specs, out_specs=out_specs, check_vma=False)
```

time: 505 us -> 174 us (0.34); the launches traced: 498 us -> 172 us
  starting transfers between devices: 292 us -> 22.8 us
  Pallas kernels: 0 us -> 97.3 us
  other arithmetic: 89.6 us -> 0.06 us
  local copies, waits for them, and re-layouts: 32.7 us -> 7.87 us
  waiting for transfers between devices: 67.6 us -> 43.7 us
  between operations: 14.8 us -> 0.78 us
    ppermute x86 -> x14, starting transfers between devices: 291 us -> 22.8 us  [the longest x2 9.33 us: halos(): near = lax.ppermute(value, AXES, facing)]
    pallas_call x0 -> x4, Pallas kernels: none -> 97.3 us  [call(): pl.pallas_call(kernel, out_shape=arrays, in_specs=[SMEM] + [VMEM] * (len(...]
    add x36 -> x0, other arithmetic: 67.6 us -> none  [the longest x28 51.4 us: deep_group(): wide_dir = keeps[first + offset] * inner + pushes[first + offset] * wide_res]
    ppermute x86 -> x14, waiting for transfers between devices: 67.5 us -> 43.7 us  [the longest x2 22.5 us: halos(): near = lax.ppermute(value, AXES, facing)]
    slice x67 -> x0, local copies, waits for them, and re-layouts: 21.7 us -> none  [the longest x18 9.44 us: extended_2(): last = lax.slice_in_dim(value, length - width, length, axis=dim)]
    div x2 -> x0, other arithmetic: 6.44 us -> none  [body(): direction = residual / center]
  transfers between devices with their start and end apart: 90 -> 14, of which waited for: 10 -> 7; matrix products, arithmetic and copies ran while one was open for 21% -> 0% of each run, Pallas kernels for 0% -> 0%
where the time goes in v1:
time: 174 us; the launch traced here: 172 us
  Pallas kernels  97.3 us (56%)
  waiting for transfers between devices  43.7 us (25%)
  starting transfers between devices  22.8 us (13%)
  local copies, waits for them, and re-layouts  7.87 us (5%)
    pallas_call x4, Pallas kernels, call(): pl.pallas_call(kernel, out_shape=arrays, in_specs=[SMEM] + [VMEM] * (len(...  97.3 us
    ppermute x2, waiting for transfers between devices, halos(): near = lax.ppermute(value, AXES, facing)  22.5 us
    ppermute x3, waiting for transfers between devices, body(): got.append(lax.ppermute(piece, 'sec', across(number)))  9.84 us
    ppermute x2, starting transfers between devices, halos(): near = lax.ppermute(value, AXES, facing)  9.33 us
    ppermute x2, waiting for transfers between devices, halos(): far = lax.ppermute(value, AXES, beyond)  8.22 us
    ppermute x2, starting transfers between devices, halos(): on = lax.ppermute(value, AXES, partner)  4.9 us
    unnamed x28, local copies, waits for them, and re-layouts  4.23 us
    ppermute x2, starting transfers between devices, halos(): far = lax.ppermute(value, AXES, beyond)  3.84 us
  transfers between devices with their start and end apart: 14, of which 7 were waited for; matrix products, arithmetic and copies ran while one was open for 0% of the time, Pallas kernels for 0%

profile of v1, /device:TPU:105, one launch (start us, length us, event | category | flops | bytes accessed | tf_op | source)
XLA Modules:
  0.0 172.4 jit_solution(3595063540587268711)
XLA Ops:
  0.0 1.3 constant_dynamic-slice_fusion
  1.6 1.0 collective-permute-start
  2.6 1.3 collective-permute-start.2
  5.2 3.4 %collective-permute-done.1.got_2 = f32[2,8,32,128]{3,2,1,0:T(8,128)S(1)} collective-permute-done((f32[2,8,32,128]{3,2,1,0:T(8,128)S(1)}, f32[2,8,32,128]{3,2,1,0:T(8,128)S(1)}, u32[]{:S(2)}, u32[]{:S(2)}) %collective-permute-start.1) | collective-permute-done | bytes 262176 | tf_op jit(solution)/shard_map/ppermute | solution.py:368
  8.6 6.5 %collective-permute-done.2.got_3 = f32[2,8,32,128]{3,2,1,0:T(8,128)S(1)} collective-permute-done((f32[2,8,32,128]{3,2,1,0:T(8,128)S(1)}, f32[2,8,32,128]{3,2,1,0:T(8,128)S(1)}, u32[]{:S(2)}, u32[]{:S(2)}) %collective-permute-start.2) | collective-permute-done | bytes 262176 | tf_op jit(solution)/shard_map/ppermute | solution.py:368
  15.7 3.5 %gather.1 = (f32[8,264,128]{2,1,0:T(8,128)}, f32[3,8,32,128]{3,2,1,0:T(8,128)}) custom-call(s32[10]{0:T(128)} %stack.51.scal, f32[32,32,128]{2,1,0:T(8,128)} %bitcast.19, f32[32,32,128]{2,1,0:T(8,128)} %bitcast.20, f32[32,32,128]{2,1,0:T(8,128)} %rec.1, s32[32,32,128]{2,1,0:T(8,128)} %exc.1, f32[2,8,32,128]{3,2,1,0:T(8,128)} %copy-done.9, ...), custom_call_target="tpu_custom_call" | custom-call | flops 4000000 | bytes 4000000 | tf_op jit(solution)/shard_map/gather/pallas_call | solution.py:309
  19.2 4.7 %collective-permute-start.4 = (f32[8,264,128]{2,1,0:T(8,128)}, f32[8,264,128]{2,1,0:T(8,128)S(1)}, u32[]{:S(2)}, u32[]{:S(2)}) collective-permute-start(f32[8,264,128]{2,1,0:T(8,128)} %get-tuple-element.11.own), channel_id=1, source_target_pairs={{64,32},{32,64},{0,1},{1,0},{33,65},{65,33},{97,98},{98,97},{66,34... | collective-permute-start | bytes 3244040 | tf_op jit(solution)/shard_map/ppermute | solution.py:380
  23.9 1.9 %collective-permute-start.5 = (f32[8,264,128]{2,1,0:T(8,128)}, f32[8,264,128]{2,1,0:T(8,128)S(1)}, u32[]{:S(2)}, u32[]{:S(2)}) collective-permute-start(f32[8,264,128]{2,1,0:T(8,128)} %get-tuple-element.11.own), channel_id=1, source_target_pairs={{96,32},{32,1},{1,65},{65,98},{98,34},{34,3},{3,67},{67,4},{4,68},... | collective-permute-start | bytes 3244040 | tf_op jit(solution)/shard_map/ppermute | solution.py:381
  25.8 2.4 %collective-permute-start.3 = (f32[8,264,128]{2,1,0:T(8,128)}, f32[8,264,128]{2,1,0:T(8,128)S(1)}, u32[]{:S(2)}, u32[]{:S(2)}) collective-permute-start(f32[8,264,128]{2,1,0:T(8,128)} %get-tuple-element.11.own), channel_id=1, source_target_pairs={{96,64},{64,96},{32,0},{0,32},{1,33},{33,1},{65,97},{97,65},{98,66... | collective-permute-start | bytes 3244040 | tf_op jit(solution)/shard_map/ppermute | solution.py:382
  28.2 18.1 %collective-permute-done.4.near = f32[8,264,128]{2,1,0:T(8,128)S(1)} collective-permute-done((f32[8,264,128]{2,1,0:T(8,128)}, f32[8,264,128]{2,1,0:T(8,128)S(1)}, u32[]{:S(2)}, u32[]{:S(2)}) %collective-permute-start.4) | collective-permute-done | bytes 1081376 | tf_op jit(solution)/shard_map/ppermute | solution.py:380
  46.3 4.1 %collective-permute-done.5.far = f32[8,264,128]{2,1,0:T(8,128)S(1)} collective-permute-done((f32[8,264,128]{2,1,0:T(8,128)}, f32[8,264,128]{2,1,0:T(8,128)S(1)}, u32[]{:S(2)}, u32[]{:S(2)}) %collective-permute-start.5) | collective-permute-done | bytes 1081376 | tf_op jit(solution)/shard_map/ppermute | solution.py:381
  50.5 1.1 copy-done.3
  52.2 48.5 %first.1 = (f32[9,96,128]{2,1,0:T(8,128)}, f32[8,32,128]{2,1,0:T(8,128)}, f32[40,96,128]{2,1,0:T(8,128)}, f32[40,96,128]{2,1,0:T(8,128)}) custom-call(s32[10]{0:T(128)} %stack.51.scal, f32[8,264,128]{2,1,0:T(8,128)} %get-tuple-element.11.own, f32[8,264,128]{2,1,0:T(8,128)} %copy-done.2, f32[8,264,128]{2,1,0:T(8,128)} %copy-done, f32[8,264,128]{2,1,0:T(8,128)} %copy-done.1, ...), custom_call_target="tpu_custom_call" | custom-call | flops 80000000 | bytes 4000000 | tf_op jit(solution)/shard_map/first/pallas_call | solution.py:309
  100.7 4.7 %collective-permute-start.8 = (f32[9,96,128]{2,1,0:T(8,128)}, f32[9,96,128]{2,1,0:T(8,128)S(1)}, u32[]{:S(2)}, u32[]{:S(2)}) collective-permute-start(f32[9,96,128]{2,1,0:T(8,128)} %get-tuple-element.13.own), channel_id=1, source_target_pairs={{64,32},{32,64},{0,1},{1,0},{33,65},{65,33},{97,98},{98,97},{66,34... | collective-permute-start | bytes 1327112 | tf_op jit(solution)/shard_map/ppermute | solution.py:380
  105.4 1.9 %collective-permute-start.9 = (f32[9,96,128]{2,1,0:T(8,128)}, f32[9,96,128]{2,1,0:T(8,128)S(1)}, u32[]{:S(2)}, u32[]{:S(2)}) collective-permute-start(f32[9,96,128]{2,1,0:T(8,128)} %get-tuple-element.13.own), channel_id=1, source_target_pairs={{96,32},{32,1},{1,65},{65,98},{98,34},{34,3},{3,67},{67,4},{4,68},... | collective-permute-start | bytes 1327112 | tf_op jit(solution)/shard_map/ppermute | solution.py:381
  107.3 2.4 %collective-permute-start.7 = (f32[9,96,128]{2,1,0:T(8,128)}, f32[9,96,128]{2,1,0:T(8,128)S(1)}, u32[]{:S(2)}, u32[]{:S(2)}) collective-permute-start(f32[9,96,128]{2,1,0:T(8,128)} %get-tuple-element.13.own), channel_id=1, source_target_pairs={{96,64},{64,96},{32,0},{0,32},{1,33},{33,1},{65,97},{97,65},{98,66... | collective-permute-start | bytes 1327112 | tf_op jit(solution)/shard_map/ppermute | solution.py:382
  109.8 4.4 %collective-permute-done.8.near = f32[9,96,128]{2,1,0:T(8,128)S(1)} collective-permute-done((f32[9,96,128]{2,1,0:T(8,128)}, f32[9,96,128]{2,1,0:T(8,128)S(1)}, u32[]{:S(2)}, u32[]{:S(2)}) %collective-permute-start.8) | collective-permute-done | bytes 442400 | tf_op jit(solution)/shard_map/ppermute | solution.py:380
  114.2 4.1 %collective-permute-done.9.far = f32[9,96,128]{2,1,0:T(8,128)S(1)} collective-permute-done((f32[9,96,128]{2,1,0:T(8,128)}, f32[9,96,128]{2,1,0:T(8,128)S(1)}, u32[]{:S(2)}, u32[]{:S(2)}) %collective-permute-start.9) | collective-permute-done | bytes 442400 | tf_op jit(solution)/shard_map/ppermute | solution.py:381
  118.3 0.7 copy-done.5
  119.3 43.4 %second.1 = f32[4,8,32,128]{3,2,1,0:T(8,128)} custom-call(s32[10]{0:T(128)} %stack.51.scal, f32[9,96,128]{2,1,0:T(8,128)} %get-tuple-element.13.own, f32[9,96,128]{2,1,0:T(8,128)} %copy-done.6, f32[9,96,128]{2,1,0:T(8,128)} %copy-done.4, f32[9,96,128]{2,1,0:T(8,128)} %copy-done.5, f32[9,96,128]{2,1,0:T(8,128)} %copy-done.7, ...), custom_call_target="tpu_custom_call" | custom-call | flops 80000000 | bytes 4000000 | tf_op jit(solution)/shard_map/second/pallas_call | solution.py:309
  162.7 1.8 %slice_bitcast_fusion = (f32[8,32,128]{2,1,0:T(8,128)S(1)}, f32[8,32,128]{2,1,0:T(8,128)S(1)}, f32[8,32,128]{2,1,0:T(8,128)S(1)}, f32[8,32,128]{2,1,0:T(8,128)}) fusion(f32[4,8,32,128]{3,2,1,0:T(8,128)} %second.1), kind=kLoop, calls=%fused_computation.3 | loop fusion | bytes 1048576 | tf_op jit(solution)/shard_map/squeeze | solution.py:405
  164.5 2.1 %collective-permute-start.11 = (f32[8,32,128]{2,1,0:T(8,128)S(1)}, f32[8,32,128]{2,1,0:T(8,128)S(1)}, u32[]{:S(2)}, u32[]{:S(2)}) collective-permute-start(f32[8,32,128]{2,1,0:T(8,128)S(1)} %get-tuple-element.19), channel_id=1, source_target_pairs={{0,32},{32,0},{64,96},{96,64},{1,33},{33,1},{65,97},{97,65},{2,34}... | collective-permute-start | bytes 393224 | tf_op jit(solution)/shard_map/ppermute | solution.py:405
  166.7 3.1 %collective-permute-done.13.got_3 = f32[8,32,128]{2,1,0:T(8,128)S(1)} collective-permute-done((f32[8,32,128]{2,1,0:T(8,128)S(1)}, f32[8,32,128]{2,1,0:T(8,128)S(1)}, u32[]{:S(2)}, u32[]{:S(2)}) %collective-permute-start.13) | collective-permute-done | bytes 131104 | tf_op jit(solution)/shard_map/ppermute | solution.py:405
  170.5 1.9 %spread.1 = f32[32,32,128]{2,1,0:T(8,128)} custom-call(s32[10]{0:T(128)} %stack.51.scal, f32[8,32,128]{2,1,0:T(8,128)} %get-tuple-element.20.own, f32[8,32,128]{2,1,0:T(8,128)} %copy-done.13, f32[8,32,128]{2,1,0:T(8,128)} %copy-done.12, f32[8,32,128]{2,1,0:T(8,128)} %copy-done.11), custom_call_target="tpu_custom_call" | custom-call | flops 100000 | bytes 4000000 | tf_op jit(solution)/shard_map/spread/pallas_call | solution.py:309
  (42 shorter events, 3.3 us)
Async XLA Ops:
  1.3 7.3 %collective-permute-start.1 = (f32[2,8,32,128]{3,2,1,0:T(8,128)S(1)}, f32[2,8,32,128]{3,2,1,0:T(8,128)S(1)}, u32[]{:S(2)}, u32[]{:S(2)}) collective-permute-start(f32[2,8,32,128]{3,2,1,0:T(8,128)S(1)} %pad_maximum_fusion.1), channel_id=1, source_target_pairs={{0,64},{32,96},{64,0},{96,32},{1,65},{33,97},{65,1},{97,33},{2,66}... | collective-permute-start | bytes 786440 | tf_op jit(solution)/shard_map/ppermute | solution.py:368
  1.6 7.0 %collective-permute-start = (f32[2,8,32,128]{3,2,1,0:T(8,128)S(1)}, f32[2,8,32,128]{3,2,1,0:T(8,128)S(1)}, u32[]{:S(2)}, u32[]{:S(2)}) collective-permute-start(f32[2,8,32,128]{3,2,1,0:T(8,128)S(1)} %pad_maximum_fusion), channel_id=1, source_target_pairs={{0,32},{32,0},{64,96},{96,64},{1,33},{33,1},{65,97},{97,65},{2,34}... | collective-permute-start | bytes 786440 | tf_op jit(solution)/shard_map/ppermute | solution.py:368
  2.6 12.4 %collective-permute-start.2 = (f32[2,8,32,128]{3,2,1,0:T(8,128)S(1)}, f32[2,8,32,128]{3,2,1,0:T(8,128)S(1)}, u32[]{:S(2)}, u32[]{:S(2)}) collective-permute-start(f32[2,8,32,128]{3,2,1,0:T(8,128)S(1)} %pad_maximum_fusion.2), channel_id=1, source_target_pairs={{0,96},{32,64},{64,32},{96,0},{1,97},{33,65},{65,33},{97,1},{2,98}... | collective-permute-start | bytes 786440 | tf_op jit(solution)/shard_map/ppermute | solution.py:368
  8.6 6.5 %copy-start.8 = (f32[2,8,32,128]{3,2,1,0:T(8,128)}, f32[2,8,32,128]{3,2,1,0:T(8,128)S(1)}, u32[]{:S(2)}) copy-start(f32[2,8,32,128]{3,2,1,0:T(8,128)S(1)} %collective-permute-done.1.got_2) | copy-start | bytes 786436
  8.6 6.5 %copy-start.9 = (f32[2,8,32,128]{3,2,1,0:T(8,128)}, f32[2,8,32,128]{3,2,1,0:T(8,128)S(1)}, u32[]{:S(2)}) copy-start(f32[2,8,32,128]{3,2,1,0:T(8,128)S(1)} %collective-permute-done.got_1) | copy-start | bytes 786436
  19.2 27.1 %collective-permute-start.4 = (f32[8,264,128]{2,1,0:T(8,128)}, f32[8,264,128]{2,1,0:T(8,128)S(1)}, u32[]{:S(2)}, u32[]{:S(2)}) collective-permute-start(f32[8,264,128]{2,1,0:T(8,128)} %get-tuple-element.11.own), channel_id=1, source_target_pairs={{64,32},{32,64},{0,1},{1,0},{33,65},{65,33},{97,98},{98,97},{66,34... | collective-permute-start | bytes 3244040 | tf_op jit(solution)/shard_map/ppermute | solution.py:380
  23.9 26.6 %collective-permute-start.5 = (f32[8,264,128]{2,1,0:T(8,128)}, f32[8,264,128]{2,1,0:T(8,128)S(1)}, u32[]{:S(2)}, u32[]{:S(2)}) collective-permute-start(f32[8,264,128]{2,1,0:T(8,128)} %get-tuple-element.11.own), channel_id=1, source_target_pairs={{96,32},{32,1},{1,65},{65,98},{98,34},{34,3},{3,67},{67,4},{4,68},... | collective-permute-start | bytes 3244040 | tf_op jit(solution)/shard_map/ppermute | solution.py:381
  25.8 24.7 %collective-permute-start.3 = (f32[8,264,128]{2,1,0:T(8,128)}, f32[8,264,128]{2,1,0:T(8,128)S(1)}, u32[]{:S(2)}, u32[]{:S(2)}) collective-permute-start(f32[8,264,128]{2,1,0:T(8,128)} %get-tuple-element.11.own), channel_id=1, source_target_pairs={{96,64},{64,96},{32,0},{0,32},{1,33},{33,1},{65,97},{97,65},{98,66... | collective-permute-start | bytes 3244040 | tf_op jit(solution)/shard_map/ppermute | solution.py:382
  46.3 5.2 %copy-start = (f32[8,264,128]{2,1,0:T(8,128)}, f32[8,264,128]{2,1,0:T(8,128)S(1)}, u32[]{:S(2)}) copy-start(f32[8,264,128]{2,1,0:T(8,128)S(1)} %collective-permute-done.4.near) | copy-start | bytes 3244036
  46.3 4.1 %collective-permute-start.6 = (f32[8,264,128]{2,1,0:T(8,128)S(1)}, f32[8,264,128]{2,1,0:T(8,128)S(1)}, u32[]{:S(2)}, u32[]{:S(2)}) collective-permute-start(f32[8,264,128]{2,1,0:T(8,128)S(1)} %collective-permute-done.4.near), channel_id=1, source_target_pairs={{96,64},{64,96},{32,0},{0,32},{1,33},{33,1},{65,97},{97,65},{98,66... | collective-permute-start | bytes 3244040 | tf_op jit(solution)/shard_map/ppermute | solution.py:383
  50.5 1.4 copy-start.1
  50.5 1.8 %copy-start.2 = (f32[8,264,128]{2,1,0:T(8,128)}, f32[8,264,128]{2,1,0:T(8,128)S(1)}, u32[]{:S(2)}) copy-start(f32[8,264,128]{2,1,0:T(8,128)S(1)} %collective-permute-done.3.on) | copy-start | bytes 3244036
  50.5 1.1 copy-start.3
  100.7 13.5 %collective-permute-start.8 = (f32[9,96,128]{2,1,0:T(8,128)}, f32[9,96,128]{2,1,0:T(8,128)S(1)}, u32[]{:S(2)}, u32[]{:S(2)}) collective-permute-start(f32[9,96,128]{2,1,0:T(8,128)} %get-tuple-element.13.own), channel_id=1, source_target_pairs={{64,32},{32,64},{0,1},{1,0},{33,65},{65,33},{97,98},{98,97},{66,34... | collective-permute-start | bytes 1327112 | tf_op jit(solution)/shard_map/ppermute | solution.py:380
  105.4 12.9 %collective-permute-start.9 = (f32[9,96,128]{2,1,0:T(8,128)}, f32[9,96,128]{2,1,0:T(8,128)S(1)}, u32[]{:S(2)}, u32[]{:S(2)}) collective-permute-start(f32[9,96,128]{2,1,0:T(8,128)} %get-tuple-element.13.own), channel_id=1, source_target_pairs={{96,32},{32,1},{1,65},{65,98},{98,34},{34,3},{3,67},{67,4},{4,68},... | collective-permute-start | bytes 1327112 | tf_op jit(solution)/shard_map/ppermute | solution.py:381
  107.3 11.0 %collective-permute-start.7 = (f32[9,96,128]{2,1,0:T(8,128)}, f32[9,96,128]{2,1,0:T(8,128)S(1)}, u32[]{:S(2)}, u32[]{:S(2)}) collective-permute-start(f32[9,96,128]{2,1,0:T(8,128)} %get-tuple-element.13.own), channel_id=1, source_target_pairs={{96,64},{64,96},{32,0},{0,32},{1,33},{33,1},{65,97},{97,65},{98,66... | collective-permute-start | bytes 1327112 | tf_op jit(solution)/shard_map/ppermute | solution.py:382
  114.2 4.1 %copy-start.4 = (f32[9,96,128]{2,1,0:T(8,128)}, f32[9,96,128]{2,1,0:T(8,128)S(1)}, u32[]{:S(2)}) copy-start(f32[9,96,128]{2,1,0:T(8,128)S(1)} %collective-permute-done.8.near) | copy-start | bytes 1327108
  114.2 4.1 %collective-permute-start.10 = (f32[9,96,128]{2,1,0:T(8,128)S(1)}, f32[9,96,128]{2,1,0:T(8,128)S(1)}, u32[]{:S(2)}, u32[]{:S(2)}) collective-permute-start(f32[9,96,128]{2,1,0:T(8,128)S(1)} %collective-permute-done.8.near), channel_id=1, source_target_pairs={{96,64},{64,96},{32,0},{0,32},{1,33},{33,1},{65,97},{97,65},{98,66... | collective-permute-start | bytes 1327112 | tf_op jit(solution)/shard_map/ppermute | solution.py:383
  118.3 0.8 copy-start.5
  118.3 0.9 copy-start.6
  118.3 1.0 copy-start.7
  164.5 5.2 %collective-permute-start.13 = (f32[8,32,128]{2,1,0:T(8,128)S(1)}, f32[8,32,128]{2,1,0:T(8,128)S(1)}, u32[]{:S(2)}, u32[]{:S(2)}) collective-permute-start(f32[8,32,128]{2,1,0:T(8,128)S(1)} %get-tuple-element.17), channel_id=1, source_target_pairs={{0,96},{32,64},{64,32},{96,0},{1,97},{33,65},{65,33},{97,1},{2,98}... | collective-permute-start | bytes 393224 | tf_op jit(solution)/shard_map/ppermute | solution.py:405
  164.5 5.2 %collective-permute-start.12 = (f32[8,32,128]{2,1,0:T(8,128)S(1)}, f32[8,32,128]{2,1,0:T(8,128)S(1)}, u32[]{:S(2)}, u32[]{:S(2)}) collective-permute-start(f32[8,32,128]{2,1,0:T(8,128)S(1)} %get-tuple-element.18), channel_id=1, source_target_pairs={{0,64},{32,96},{64,0},{96,32},{1,65},{33,97},{65,1},{97,33},{2,66}... | collective-permute-start | bytes 393224 | tf_op jit(solution)/shard_map/ppermute | solution.py:405
  164.5 5.2 %collective-permute-start.11 = (f32[8,32,128]{2,1,0:T(8,128)S(1)}, f32[8,32,128]{2,1,0:T(8,128)S(1)}, u32[]{:S(2)}, u32[]{:S(2)}) collective-permute-start(f32[8,32,128]{2,1,0:T(8,128)S(1)} %get-tuple-element.19), channel_id=1, source_target_pairs={{0,32},{32,0},{64,96},{96,64},{1,33},{33,1},{65,97},{97,65},{2,34}... | collective-permute-start | bytes 393224 | tf_op jit(solution)/shard_map/ppermute | solution.py:405
  (4 other events, 2.8 us)

commit v2 on v1

--- a/solution.py
+++ b/solution.py
@@ -21,7 +21,10 @@
 HEART = 32
 SLOTS = 40
 OWN = 16
+OFF = 1
 PAD = 8
+PART = 16
+PARTS = ROWS // PART
 AXES = ("sec", "brick")
 V0_AT, V1_AT, D_AT, ROW_AT, MSG = 96, 128, 160, 256, 264
 PHI_PAD = 112
@@ -42,6 +45,7 @@
 
 
 WEIGHTS = chebyshev_weights(SWEEPS - 1)
+SHIFT = 6.0 - 0.5 * (spectrum_high + spectrum_low)
 
 
 def ionic(voltage, recovery, threshold, active):
@@ -92,30 +96,85 @@
     return total + side_sum_zero(here) - 6.0 * here
 
 
+def halves(value):
+    high = value.astype(jnp.bfloat16)
+    return high, (value - high.astype(jnp.float32)).astype(jnp.bfloat16)
+
+
 def solve(scal, even, odd, absorb, source):
-    low_end, high_end = scal[4], scal[5]
+    accs = [pltpu.ACC(part % 2)((PART, 256), jnp.float32) for part in range(2 * PARTS)]
+    pl.run_scoped(lambda *refs: sweeps(scal, even, odd, absorb, source, refs), *accs)
+
+
+def sweeps(scal, even, odd, absorb, source, accs):
+    accs = (accs[:PARTS], accs[PARTS:])
+    row = lax.broadcasted_iota(jnp.int32, (256, 256), 0)
+    column = lax.broadcasted_iota(jnp.int32, (256, 256), 1)
+    same = (row >= 128) == (column >= 128)
+    apart = jnp.abs(row - column)
+    beside = ((same & (apart == 1)) | (apart == 128)).astype(jnp.bfloat16)
+    none = jnp.zeros((PART, 256), jnp.bfloat16)
+    for unit in range(2):
+        pltpu.matmul_push_rhs(beside, 0, unit)
+    for number, acc in enumerate(accs[0] + accs[1]):
+        pltpu.matmul_acc_lhs(acc, none, load_staged_rhs=0 if number < 2 else None)
+    for acc in accs[0] + accs[1]:
+        pltpu.matmul_pop(acc)
+
     for level, (keep, push) in enumerate(WEIGHTS, 1):
         src, dst = (even, odd) if level % 2 else (odd, even)
-        shift = 6.0 - (1.0 + keep) / push
-
-        def plane(x, carry, src=src, dst=dst, keep=keep, push=push, shift=shift, level=level):
-            for start in range(0, ROWS, 48):
-                at, to = PAD + start, PAD + start + 48
-                here = src[x, at:to]
-                total = src[x - 1, at:to] + src[x + 1, at:to]
-                total = total + (src[x, at - 1 : to - 1] + src[x, at + 1 : to + 1])
-                total = total + side_sum_zero(here)
-                total = total + source[x, start : start + 48]
-                total = total - (absorb[x, start : start + 48] + shift) * here
-                if level == 1:
-                    dst[x, at:to] = push * total
-                else:
-                    dst[x, at:to] = push * total - keep * dst[x, at:to]
+        low = jnp.maximum(level, scal[4])
+        high = jnp.minimum(SLOTS - level, scal[5])
+        low = jnp.where(scal[5] < SLOTS, low - low % 2, low)
+        pairs = (high - low + 1) // 2
+        last = low + 2 * (pairs - 1)
+
+        def begin(x, acc, src=src):
+            for part in range(PARTS):
+                at, to = PAD + PART * part, PAD + PART * (part + 1)
+                high_0, low_0 = halves(src[x + OFF, at:to])
+                high_1, low_1 = halves(src[x + OFF + 1, at:to])
+                pltpu.matmul_acc_lhs(acc[part], jnp.concatenate([high_0, high_1], 1))
+                pltpu.matmul_acc_lhs(acc[part], jnp.concatenate([low_0, low_1], 1))
+
+        def finish(x, acc, src=src, dst=dst, level=level, keep=keep, push=push):
+            for part in range(PARTS):
+                start, stop = PART * part, PART * (part + 1)
+                at, to = PAD + start, PAD + stop
+                sums = pltpu.matmul_pop(acc[part])
+                for plane in range(2):
+                    here = x + plane
+                    total = src[here + OFF - 1 + 2 * plane, at:to]
+                    total = total + (src[here + OFF, at - 1 : to - 1] + src[here + OFF, at + 1 : to + 1])
+                    total = total + source[here, start:stop]
+                    total = total - absorb[here, start:stop] * src[here + OFF, at:to]
+                    total = total + sums[:, 128 * plane : 128 * (plane + 1)]
+                    if level == 1:
+                        dst[here + OFF, at:to] = push * total
+                    else:
+                        dst[here + OFF, at:to] = push * total - keep * dst[here + OFF, at:to]
+
+        begin(low, accs[0])
+
+        def two_pairs(step, carry, low=low, last=last, begin=begin, finish=finish):
+            x = low + 4 * step
+            after = jnp.minimum(x + 2, last)
+            begin(after, accs[1])
+            finish(x, accs[0])
+            begin(jnp.minimum(x + 4, last), accs[0])
+            finish(after, accs[1])
             return carry
 
-        lax.fori_loop(
-            jnp.maximum(level, low_end), jnp.minimum(SLOTS - level, high_end), plane, 0
-        )
+        lax.fori_loop(0, pairs // 2, two_pairs, 0)
+
+        @pl.when(pairs % 2 == 1)
+        def _(last=last, finish=finish):
+            finish(last, accs[0])
+
+        @pl.when(pairs % 2 == 0)
+        def _():
+            for acc in accs[0]:
+                pltpu.matmul_pop(acc)
 
 
 def clear_edges(even, odd):
@@ -127,10 +186,10 @@
             ref[x, PAD + ROWS : PHI_PAD] = zero
         return carry
 
-    lax.fori_loop(0, SLOTS, edge, 0)
+    lax.fori_loop(0, SLOTS + 2, edge, 0)
     none = jnp.zeros((PHI_PAD, 128), jnp.float32)
-    odd[OWN - 1] = none
-    odd[OWN + 2 * SLAB] = none
+    odd[OFF + OWN - 1] = none
+    odd[OFF + OWN + 2 * SLAB] = none
 
 
 def slots():
@@ -174,8 +233,8 @@
 
         def unpack(u, carry, ref=ref, first=first, step=step):
             x = first + step * u
-            even[x, PAD : PAD + ROWS] = ref[u, 0:ROWS]
-            absorb[x] = ref[u, D_AT : D_AT + ROWS]
+            even[x + OFF, PAD : PAD + ROWS] = ref[u, 0:ROWS]
+            absorb[x] = ref[u, D_AT : D_AT + ROWS] + SHIFT
             put_heart(volt, x, ref[u, V0_AT : V0_AT + HEART])
             put_heart(volt_1, x, ref[u, V1_AT : V1_AT + HEART])
             return carry
@@ -217,7 +276,7 @@
         def _():
             def heart(u, carry):
                 x = OWN + u
-                gain = heart_laplace(volt_1, x) + torso_current(even, x, layer)
+                gain = heart_laplace(volt_1, x) + torso_current(even, x + OFF, layer)
                 voltage = volt_1[x, PAD : PAD + HEART] + coupling_gain * gain
                 voltage, _ = ionic(voltage, aux[1, u], aux[0, u], aux[2, u])
                 held[u] = voltage
@@ -227,20 +286,21 @@
 
     solve(scal, even, odd, absorb, source)
     for u in range(SLAB):
-        msg[u] = even[OWN + u, PAD : PAD + ROWS]
+        msg[u] = even[OFF + OWN + u, PAD : PAD + ROWS]
     msg[SLAB, 0:HEART] = held[0]
     msg[SLAB, HEART : 2 * HEART] = held[SLAB - 1]
     msg[SLAB, 2 * HEART : ROWS] = jnp.zeros((HEART, 128), jnp.float32)
 
 
-def second_kernel(scal, own, on, near, far, on2, held, absorb, source, out, even, odd, volt, joined):
+def second_kernel(scal, own, on, near, far, on2, held, absorb, source, *rest):
+    outs, (even, odd, volt, joined) = rest[:4], rest[4:]
     refs = (own, on, near, far, on2)
     clear_edges(even, odd)
     for number, first, step in slots():
         ref = refs[number]
 
         def unpack(u, carry, ref=ref, first=first, step=step):
-            even[first + step * u, PAD : PAD + ROWS] = ref[u]
+            even[OFF + first + step * u, PAD : PAD + ROWS] = ref[u]
             return carry
 
         lax.fori_loop(0, SLAB, unpack, 0)
@@ -262,7 +322,7 @@
         @pl.when(scal[3] == layer)
         def _():
             def heart(u, carry):
-                gain = heart_laplace(volt, u + 1) + torso_current(even, OWN + u, layer)
+                gain = heart_laplace(volt, u + 1) + torso_current(even, OWN + OFF + u, layer)
                 joined[u, ROWS : ROWS + HEART] = held[u] + coupling_gain * gain
                 return carry
 
@@ -273,11 +333,11 @@
     sec, flip = scal[0], scal[2]
 
     def plane(u, carry):
-        joined[u, 0:ROWS] = even[OWN + u, PAD : PAD + ROWS]
+        joined[u, 0:ROWS] = even[OFF + OWN + u, PAD : PAD + ROWS]
         x = jnp.where(flip == 1, SLAB - 1 - u, u)
         for number in range(4):
             at = pl.multiple_of((sec ^ number) * HEART, HEART)
-            out[number, x] = joined[u, pl.ds(at, HEART)]
+            outs[number][x] = joined[u, pl.ds(at, HEART)]
         return carry
 
     lax.fori_loop(0, SLAB, plane, 0)
@@ -383,7 +443,7 @@
         on2 = lax.ppermute(near, AXES, partner)
         return value, on, near, far, on2
 
-    phi = (SLOTS, PHI_PAD, 128)
+    phi = (SLOTS + 2, PHI_PAD, 128)
     wide = (SLOTS, ROWS, 128)
     volt = (SLOTS, V_PAD, 128)
     msg, held, absorb, later = call(
@@ -394,15 +454,15 @@
         "first",
         80_000_000,
     )
-    (out,) = call(
+    outs = call(
         second_kernel,
         (scal, *halos(msg), held, absorb, later),
-        [(4, SLAB, HEART, 128)],
+        [(SLAB, HEART, 128)] * 4,
         [phi, phi, (SLAB + 2, V_PAD, 128), (SLAB, 128, 128)],
         "second",
         80_000_000,
     )
-    back = [out[0]] + [lax.ppermute(out[number], "sec", across(number)) for number in (1, 2, 3)]
+    back = [outs[0]] + [lax.ppermute(outs[number], "sec", across(number)) for number in (1, 2, 3)]
     (result,) = call(
         spread_kernel,
         (scal, *back),

time: 174 us -> 129 us (0.74)
  Pallas kernels: 97.3 us -> 52.1 us
  waiting for transfers between devices: 43.7 us -> 46.7 us
  local copies, waits for them, and re-layouts: 7.87 us -> 6.02 us
    pallas_call x4, Pallas kernels: 97.3 us -> 52.1 us  [call(): pl.pallas_call(kernel, out_shape=arrays, in_specs=[SMEM] + [VMEM] * (len(...]
    ppermute x3, waiting for transfers between devices: 3.09 us -> 6.15 us  [body(): lax.ppermute(outs[number], 'sec', across(number))]
    squeeze x1 -> x0, local copies, waits for them, and re-layouts: 1.78 us -> none  [body(): out[number]]
  transfers between devices with their start and end apart: 14 -> 14, of which waited for: 7 -> 8; matrix products, arithmetic and copies ran while one was open for 0% -> 1% of each run, Pallas kernels for 0% -> 0%
where the time goes in v2:
time: 129 us; the launch traced here: 128 us
  Pallas kernels  52.1 us (40%)
  waiting for transfers between devices  46.7 us (36%)
  starting transfers between devices  22.8 us (18%)
  local copies, waits for them, and re-layouts  6.02 us (5%)
    pallas_call x4, Pallas kernels, call(): pl.pallas_call(kernel, out_shape=arrays, in_specs=[SMEM] + [VMEM] * (len(...  52.1 us
    ppermute x2, waiting for transfers between devices, halos(): near = lax.ppermute(value, AXES, facing)  22.5 us
    ppermute x3, waiting for transfers between devices, body(): got.append(lax.ppermute(piece, 'sec', across(number)))  9.82 us
    ppermute x2, starting transfers between devices, halos(): near = lax.ppermute(value, AXES, facing)  9.34 us
    ppermute x2, waiting for transfers between devices, halos(): far = lax.ppermute(value, AXES, beyond)  8.22 us
    ppermute x3, waiting for transfers between devices, body(): lax.ppermute(outs[number], 'sec', across(number))  6.15 us
    ppermute x2, starting transfers between devices, halos(): on = lax.ppermute(value, AXES, partner)  4.89 us
    unnamed x28, local copies, waits for them, and re-layouts  4.14 us
  transfers between devices with their start and end apart: 14, of which 8 were waited for; matrix products, arithmetic and copies ran while one was open for 1% of the time, Pallas kernels for 0%

profile of v2, /device:TPU:105, one launch (start us, length us, event | category | flops | bytes accessed | tf_op | source)
XLA Modules:
  0.0 128.4 jit_solution(14556264750627225091)
XLA Ops:
  0.0 1.3 constant_dynamic-slice_fusion
  1.6 1.0 collective-permute-start
  2.6 1.3 collective-permute-start.2
  5.2 3.4 %collective-permute-done.1.got_2 = f32[2,8,32,128]{3,2,1,0:T(8,128)S(1)} collective-permute-done((f32[2,8,32,128]{3,2,1,0:T(8,128)S(1)}, f32[2,8,32,128]{3,2,1,0:T(8,128)S(1)}, u32[]{:S(2)}, u32[]{:S(2)}) %collective-permute-start.1) | collective-permute-done | bytes 262176 | tf_op jit(solution)/shard_map/ppermute | solution.py:428
  8.6 6.5 %collective-permute-done.2.got_3 = f32[2,8,32,128]{3,2,1,0:T(8,128)S(1)} collective-permute-done((f32[2,8,32,128]{3,2,1,0:T(8,128)S(1)}, f32[2,8,32,128]{3,2,1,0:T(8,128)S(1)}, u32[]{:S(2)}, u32[]{:S(2)}) %collective-permute-start.2) | collective-permute-done | bytes 262176 | tf_op jit(solution)/shard_map/ppermute | solution.py:428
  15.7 3.5 %gather.1 = (f32[8,264,128]{2,1,0:T(8,128)}, f32[3,8,32,128]{3,2,1,0:T(8,128)}) custom-call(s32[10]{0:T(128)} %stack.51.scal, f32[32,32,128]{2,1,0:T(8,128)} %bitcast.11, f32[32,32,128]{2,1,0:T(8,128)} %bitcast.12, f32[32,32,128]{2,1,0:T(8,128)} %rec.1, s32[32,32,128]{2,1,0:T(8,128)} %exc.1, f32[2,8,32,128]{3,2,1,0:T(8,128)} %copy-done.9, ...), custom_call_target="tpu_custom_call" | custom-call | flops 4000000 | bytes 4000000 | tf_op jit(solution)/shard_map/gather/pallas_call | solution.py:369
  19.2 4.7 %collective-permute-start.4 = (f32[8,264,128]{2,1,0:T(8,128)}, f32[8,264,128]{2,1,0:T(8,128)S(1)}, u32[]{:S(2)}, u32[]{:S(2)}) collective-permute-start(f32[8,264,128]{2,1,0:T(8,128)} %get-tuple-element.15.own), channel_id=1, source_target_pairs={{64,32},{32,64},{0,1},{1,0},{33,65},{65,33},{97,98},{98,97},{66,34... | collective-permute-start | bytes 3244040 | tf_op jit(solution)/shard_map/ppermute | solution.py:440
  23.9 1.9 %collective-permute-start.5 = (f32[8,264,128]{2,1,0:T(8,128)}, f32[8,264,128]{2,1,0:T(8,128)S(1)}, u32[]{:S(2)}, u32[]{:S(2)}) collective-permute-start(f32[8,264,128]{2,1,0:T(8,128)} %get-tuple-element.15.own), channel_id=1, source_target_pairs={{96,32},{32,1},{1,65},{65,98},{98,34},{34,3},{3,67},{67,4},{4,68},... | collective-permute-start | bytes 3244040 | tf_op jit(solution)/shard_map/ppermute | solution.py:441
  25.8 2.4 %collective-permute-start.3 = (f32[8,264,128]{2,1,0:T(8,128)}, f32[8,264,128]{2,1,0:T(8,128)S(1)}, u32[]{:S(2)}, u32[]{:S(2)}) collective-permute-start(f32[8,264,128]{2,1,0:T(8,128)} %get-tuple-element.15.own), channel_id=1, source_target_pairs={{96,64},{64,96},{32,0},{0,32},{1,33},{33,1},{65,97},{97,65},{98,66... | collective-permute-start | bytes 3244040 | tf_op jit(solution)/shard_map/ppermute | solution.py:442
  28.3 18.1 %collective-permute-done.4.near = f32[8,264,128]{2,1,0:T(8,128)S(1)} collective-permute-done((f32[8,264,128]{2,1,0:T(8,128)}, f32[8,264,128]{2,1,0:T(8,128)S(1)}, u32[]{:S(2)}, u32[]{:S(2)}) %collective-permute-start.4) | collective-permute-done | bytes 1081376 | tf_op jit(solution)/shard_map/ppermute | solution.py:440
  46.4 4.1 %collective-permute-done.5.far = f32[8,264,128]{2,1,0:T(8,128)S(1)} collective-permute-done((f32[8,264,128]{2,1,0:T(8,128)}, f32[8,264,128]{2,1,0:T(8,128)S(1)}, u32[]{:S(2)}, u32[]{:S(2)}) %collective-permute-start.5) | collective-permute-done | bytes 1081376 | tf_op jit(solution)/shard_map/ppermute | solution.py:441
  50.5 1.1 copy-done.3
  52.3 25.9 %first.1 = (f32[9,96,128]{2,1,0:T(8,128)}, f32[8,32,128]{2,1,0:T(8,128)}, f32[40,96,128]{2,1,0:T(8,128)}, f32[40,96,128]{2,1,0:T(8,128)}) custom-call(s32[10]{0:T(128)} %stack.51.scal, f32[8,264,128]{2,1,0:T(8,128)} %get-tuple-element.15.own, f32[8,264,128]{2,1,0:T(8,128)} %copy-done.2, f32[8,264,128]{2,1,0:T(8,128)} %copy-done, f32[8,264,128]{2,1,0:T(8,128)} %copy-done.1, ...), custom_call_target="tpu_custom_call" | custom-call | flops 80000000 | bytes 4000000 | tf_op jit(solution)/shard_map/first/pallas_call | solution.py:369
  78.1 4.7 %collective-permute-start.8 = (f32[9,96,128]{2,1,0:T(8,128)}, f32[9,96,128]{2,1,0:T(8,128)S(1)}, u32[]{:S(2)}, u32[]{:S(2)}) collective-permute-start(f32[9,96,128]{2,1,0:T(8,128)} %get-tuple-element.17.own), channel_id=1, source_target_pairs={{64,32},{32,64},{0,1},{1,0},{33,65},{65,33},{97,98},{98,97},{66,34... | collective-permute-start | bytes 1327112 | tf_op jit(solution)/shard_map/ppermute | solution.py:440
  82.8 1.9 %collective-permute-start.9 = (f32[9,96,128]{2,1,0:T(8,128)}, f32[9,96,128]{2,1,0:T(8,128)S(1)}, u32[]{:S(2)}, u32[]{:S(2)}) collective-permute-start(f32[9,96,128]{2,1,0:T(8,128)} %get-tuple-element.17.own), channel_id=1, source_target_pairs={{96,32},{32,1},{1,65},{65,98},{98,34},{34,3},{3,67},{67,4},{4,68},... | collective-permute-start | bytes 1327112 | tf_op jit(solution)/shard_map/ppermute | solution.py:441
  84.8 2.4 %collective-permute-start.7 = (f32[9,96,128]{2,1,0:T(8,128)}, f32[9,96,128]{2,1,0:T(8,128)S(1)}, u32[]{:S(2)}, u32[]{:S(2)}) collective-permute-start(f32[9,96,128]{2,1,0:T(8,128)} %get-tuple-element.17.own), channel_id=1, source_target_pairs={{96,64},{64,96},{32,0},{0,32},{1,33},{33,1},{65,97},{97,65},{98,66... | collective-permute-start | bytes 1327112 | tf_op jit(solution)/shard_map/ppermute | solution.py:442
  87.2 4.4 %collective-permute-done.8.near = f32[9,96,128]{2,1,0:T(8,128)S(1)} collective-permute-done((f32[9,96,128]{2,1,0:T(8,128)}, f32[9,96,128]{2,1,0:T(8,128)S(1)}, u32[]{:S(2)}, u32[]{:S(2)}) %collective-permute-start.8) | collective-permute-done | bytes 442400 | tf_op jit(solution)/shard_map/ppermute | solution.py:440
  91.6 4.1 %collective-permute-done.9.far = f32[9,96,128]{2,1,0:T(8,128)S(1)} collective-permute-done((f32[9,96,128]{2,1,0:T(8,128)}, f32[9,96,128]{2,1,0:T(8,128)S(1)}, u32[]{:S(2)}, u32[]{:S(2)}) %collective-permute-start.9) | collective-permute-done | bytes 442400 | tf_op jit(solution)/shard_map/ppermute | solution.py:441
  95.7 0.7 copy-done.5
  96.8 20.8 %second.1 = (f32[8,32,128]{2,1,0:T(8,128)}, f32[8,32,128]{2,1,0:T(8,128)}, f32[8,32,128]{2,1,0:T(8,128)}, f32[8,32,128]{2,1,0:T(8,128)}) custom-call(s32[10]{0:T(128)} %stack.51.scal, f32[9,96,128]{2,1,0:T(8,128)} %get-tuple-element.17.own, f32[9,96,128]{2,1,0:T(8,128)} %copy-done.6, f32[9,96,128]{2,1,0:T(8,128)} %copy-done.4, f32[9,96,128]{2,1,0:T(8,128)} %copy-done.5, ...), custom_call_target="tpu_custom_call" | custom-call | flops 80000000 | bytes 4000000 | tf_op jit(solution)/shard_map/second/pallas_call | solution.py:369
  117.6 2.1 %collective-permute-start.13 = (f32[8,32,128]{2,1,0:T(8,128)}, f32[8,32,128]{2,1,0:T(8,128)S(1)}, u32[]{:S(2)}, u32[]{:S(2)}) collective-permute-start(f32[8,32,128]{2,1,0:T(8,128)} %get-tuple-element.24), channel_id=1, source_target_pairs={{0,96},{32,64},{64,32},{96,0},{1,97},{33,65},{65,33},{97,1},{2,98}... | collective-permute-start | bytes 393224 | tf_op jit(solution)/shard_map/ppermute | solution.py:465
  119.7 2.7 %collective-permute-done.12.got_2 = f32[8,32,128]{2,1,0:T(8,128)S(1)} collective-permute-done((f32[8,32,128]{2,1,0:T(8,128)}, f32[8,32,128]{2,1,0:T(8,128)S(1)}, u32[]{:S(2)}, u32[]{:S(2)}) %collective-permute-start.12) | collective-permute-done | bytes 131104 | tf_op jit(solution)/shard_map/ppermute | solution.py:465
  122.4 3.4 %collective-permute-done.13.got_3 = f32[8,32,128]{2,1,0:T(8,128)S(1)} collective-permute-done((f32[8,32,128]{2,1,0:T(8,128)}, f32[8,32,128]{2,1,0:T(8,128)S(1)}, u32[]{:S(2)}, u32[]{:S(2)}) %collective-permute-start.13) | collective-permute-done | bytes 131104 | tf_op jit(solution)/shard_map/ppermute | solution.py:465
  126.5 1.9 %spread.1 = f32[32,32,128]{2,1,0:T(8,128)} custom-call(s32[10]{0:T(128)} %stack.51.scal, f32[8,32,128]{2,1,0:T(8,128)} %get-tuple-element.21.own, f32[8,32,128]{2,1,0:T(8,128)} %copy-done.11, f32[8,32,128]{2,1,0:T(8,128)} %copy-done.12, f32[8,32,128]{2,1,0:T(8,128)} %copy-done.13), custom_call_target="tpu_custom_call" | custom-call | flops 100000 | bytes 4000000 | tf_op jit(solution)/shard_map/spread/pallas_call | solution.py:369
  (41 shorter events, 3.3 us)
Async XLA Ops:
  1.3 7.3 %collective-permute-start.1 = (f32[2,8,32,128]{3,2,1,0:T(8,128)S(1)}, f32[2,8,32,128]{3,2,1,0:T(8,128)S(1)}, u32[]{:S(2)}, u32[]{:S(2)}) collective-permute-start(f32[2,8,32,128]{3,2,1,0:T(8,128)S(1)} %pad_maximum_fusion.1), channel_id=1, source_target_pairs={{0,64},{32,96},{64,0},{96,32},{1,65},{33,97},{65,1},{97,33},{2,66}... | collective-permute-start | bytes 786440 | tf_op jit(solution)/shard_map/ppermute | solution.py:428
  1.6 7.0 %collective-permute-start = (f32[2,8,32,128]{3,2,1,0:T(8,128)S(1)}, f32[2,8,32,128]{3,2,1,0:T(8,128)S(1)}, u32[]{:S(2)}, u32[]{:S(2)}) collective-permute-start(f32[2,8,32,128]{3,2,1,0:T(8,128)S(1)} %pad_maximum_fusion), channel_id=1, source_target_pairs={{0,32},{32,0},{64,96},{96,64},{1,33},{33,1},{65,97},{97,65},{2,34}... | collective-permute-start | bytes 786440 | tf_op jit(solution)/shard_map/ppermute | solution.py:428
  2.6 12.4 %collective-permute-start.2 = (f32[2,8,32,128]{3,2,1,0:T(8,128)S(1)}, f32[2,8,32,128]{3,2,1,0:T(8,128)S(1)}, u32[]{:S(2)}, u32[]{:S(2)}) collective-permute-start(f32[2,8,32,128]{3,2,1,0:T(8,128)S(1)} %pad_maximum_fusion.2), channel_id=1, source_target_pairs={{0,96},{32,64},{64,32},{96,0},{1,97},{33,65},{65,33},{97,1},{2,98}... | collective-permute-start | bytes 786440 | tf_op jit(solution)/shard_map/ppermute | solution.py:428
  8.6 6.5 %copy-start.8 = (f32[2,8,32,128]{3,2,1,0:T(8,128)}, f32[2,8,32,128]{3,2,1,0:T(8,128)S(1)}, u32[]{:S(2)}) copy-start(f32[2,8,32,128]{3,2,1,0:T(8,128)S(1)} %collective-permute-done.1.got_2) | copy-start | bytes 786436
  8.6 6.5 %copy-start.9 = (f32[2,8,32,128]{3,2,1,0:T(8,128)}, f32[2,8,32,128]{3,2,1,0:T(8,128)S(1)}, u32[]{:S(2)}) copy-start(f32[2,8,32,128]{3,2,1,0:T(8,128)S(1)} %collective-permute-done.got_1) | copy-start | bytes 786436
  19.2 27.1 %collective-permute-start.4 = (f32[8,264,128]{2,1,0:T(8,128)}, f32[8,264,128]{2,1,0:T(8,128)S(1)}, u32[]{:S(2)}, u32[]{:S(2)}) collective-permute-start(f32[8,264,128]{2,1,0:T(8,128)} %get-tuple-element.15.own), channel_id=1, source_target_pairs={{64,32},{32,64},{0,1},{1,0},{33,65},{65,33},{97,98},{98,97},{66,34... | collective-permute-start | bytes 3244040 | tf_op jit(solution)/shard_map/ppermute | solution.py:440
  23.9 26.6 %collective-permute-start.5 = (f32[8,264,128]{2,1,0:T(8,128)}, f32[8,264,128]{2,1,0:T(8,128)S(1)}, u32[]{:S(2)}, u32[]{:S(2)}) collective-permute-start(f32[8,264,128]{2,1,0:T(8,128)} %get-tuple-element.15.own), channel_id=1, source_target_pairs={{96,32},{32,1},{1,65},{65,98},{98,34},{34,3},{3,67},{67,4},{4,68},... | collective-permute-start | bytes 3244040 | tf_op jit(solution)/shard_map/ppermute | solution.py:441
  25.8 24.7 %collective-permute-start.3 = (f32[8,264,128]{2,1,0:T(8,128)}, f32[8,264,128]{2,1,0:T(8,128)S(1)}, u32[]{:S(2)}, u32[]{:S(2)}) collective-permute-start(f32[8,264,128]{2,1,0:T(8,128)} %get-tuple-element.15.own), channel_id=1, source_target_pairs={{96,64},{64,96},{32,0},{0,32},{1,33},{33,1},{65,97},{97,65},{98,66... | collective-permute-start | bytes 3244040 | tf_op jit(solution)/shard_map/ppermute | solution.py:442
  46.4 5.2 %copy-start = (f32[8,264,128]{2,1,0:T(8,128)}, f32[8,264,128]{2,1,0:T(8,128)S(1)}, u32[]{:S(2)}) copy-start(f32[8,264,128]{2,1,0:T(8,128)S(1)} %collective-permute-done.4.near) | copy-start | bytes 3244036
  46.4 4.1 %collective-permute-start.6 = (f32[8,264,128]{2,1,0:T(8,128)S(1)}, f32[8,264,128]{2,1,0:T(8,128)S(1)}, u32[]{:S(2)}, u32[]{:S(2)}) collective-permute-start(f32[8,264,128]{2,1,0:T(8,128)S(1)} %collective-permute-done.4.near), channel_id=1, source_target_pairs={{96,64},{64,96},{32,0},{0,32},{1,33},{33,1},{65,97},{97,65},{98,66... | collective-permute-start | bytes 3244040 | tf_op jit(solution)/shard_map/ppermute | solution.py:443
  50.5 1.4 %copy-start.1 = (f32[8,264,128]{2,1,0:T(8,128)}, f32[8,264,128]{2,1,0:T(8,128)S(1)}, u32[]{:S(2)}) copy-start(f32[8,264,128]{2,1,0:T(8,128)S(1)} %collective-permute-done.5.far) | copy-start | bytes 3244036
  50.5 1.8 %copy-start.2 = (f32[8,264,128]{2,1,0:T(8,128)}, f32[8,264,128]{2,1,0:T(8,128)S(1)}, u32[]{:S(2)}) copy-start(f32[8,264,128]{2,1,0:T(8,128)S(1)} %collective-permute-done.3.on) | copy-start | bytes 3244036
  50.5 1.1 copy-start.3
  78.1 13.4 %collective-permute-start.8 = (f32[9,96,128]{2,1,0:T(8,128)}, f32[9,96,128]{2,1,0:T(8,128)S(1)}, u32[]{:S(2)}, u32[]{:S(2)}) collective-permute-start(f32[9,96,128]{2,1,0:T(8,128)} %get-tuple-element.17.own), channel_id=1, source_target_pairs={{64,32},{32,64},{0,1},{1,0},{33,65},{65,33},{97,98},{98,97},{66,34... | collective-permute-start | bytes 1327112 | tf_op jit(solution)/shard_map/ppermute | solution.py:440
  82.8 12.9 %collective-permute-start.9 = (f32[9,96,128]{2,1,0:T(8,128)}, f32[9,96,128]{2,1,0:T(8,128)S(1)}, u32[]{:S(2)}, u32[]{:S(2)}) collective-permute-start(f32[9,96,128]{2,1,0:T(8,128)} %get-tuple-element.17.own), channel_id=1, source_target_pairs={{96,32},{32,1},{1,65},{65,98},{98,34},{34,3},{3,67},{67,4},{4,68},... | collective-permute-start | bytes 1327112 | tf_op jit(solution)/shard_map/ppermute | solution.py:441
  84.8 11.0 %collective-permute-start.7 = (f32[9,96,128]{2,1,0:T(8,128)}, f32[9,96,128]{2,1,0:T(8,128)S(1)}, u32[]{:S(2)}, u32[]{:S(2)}) collective-permute-start(f32[9,96,128]{2,1,0:T(8,128)} %get-tuple-element.17.own), channel_id=1, source_target_pairs={{96,64},{64,96},{32,0},{0,32},{1,33},{33,1},{65,97},{97,65},{98,66... | collective-permute-start | bytes 1327112 | tf_op jit(solution)/shard_map/ppermute | solution.py:442
  91.6 4.1 %copy-start.4 = (f32[9,96,128]{2,1,0:T(8,128)}, f32[9,96,128]{2,1,0:T(8,128)S(1)}, u32[]{:S(2)}) copy-start(f32[9,96,128]{2,1,0:T(8,128)S(1)} %collective-permute-done.8.near) | copy-start | bytes 1327108
  91.6 4.1 %collective-permute-start.10 = (f32[9,96,128]{2,1,0:T(8,128)S(1)}, f32[9,96,128]{2,1,0:T(8,128)S(1)}, u32[]{:S(2)}, u32[]{:S(2)}) collective-permute-start(f32[9,96,128]{2,1,0:T(8,128)S(1)} %collective-permute-done.8.near), channel_id=1, source_target_pairs={{96,64},{64,96},{32,0},{0,32},{1,33},{33,1},{65,97},{97,65},{98,66... | collective-permute-start | bytes 1327112 | tf_op jit(solution)/shard_map/ppermute | solution.py:443
  95.7 1.0 copy-start.7
  117.5 2.1 %collective-permute-start.11 = (f32[8,32,128]{2,1,0:T(8,128)}, f32[8,32,128]{2,1,0:T(8,128)S(1)}, u32[]{:S(2)}, u32[]{:S(2)}) collective-permute-start(f32[8,32,128]{2,1,0:T(8,128)} %get-tuple-element.22), channel_id=1, source_target_pairs={{0,32},{32,0},{64,96},{96,64},{1,33},{33,1},{65,97},{97,65},{2,34}... | collective-permute-start | bytes 393224 | tf_op jit(solution)/shard_map/ppermute | solution.py:465
  117.5 4.9 %collective-permute-start.12 = (f32[8,32,128]{2,1,0:T(8,128)}, f32[8,32,128]{2,1,0:T(8,128)S(1)}, u32[]{:S(2)}, u32[]{:S(2)}) collective-permute-start(f32[8,32,128]{2,1,0:T(8,128)} %get-tuple-element.23), channel_id=1, source_target_pairs={{0,64},{32,96},{64,0},{96,32},{1,65},{33,97},{65,1},{97,33},{2,66}... | collective-permute-start | bytes 393224 | tf_op jit(solution)/shard_map/ppermute | solution.py:465
  117.6 8.2 %collective-permute-start.13 = (f32[8,32,128]{2,1,0:T(8,128)}, f32[8,32,128]{2,1,0:T(8,128)S(1)}, u32[]{:S(2)}, u32[]{:S(2)}) collective-permute-start(f32[8,32,128]{2,1,0:T(8,128)} %get-tuple-element.24), channel_id=1, source_target_pairs={{0,96},{32,64},{64,32},{96,0},{1,97},{33,65},{65,33},{97,1},{2,98}... | collective-permute-start | bytes 393224 | tf_op jit(solution)/shard_map/ppermute | solution.py:465
  119.7 6.2 %copy-start.11 = (f32[8,32,128]{2,1,0:T(8,128)}, f32[8,32,128]{2,1,0:T(8,128)S(1)}, u32[]{:S(2)}) copy-start(f32[8,32,128]{2,1,0:T(8,128)S(1)} %collective-permute-done.11.got_1) | copy-start | bytes 393220
  122.4 3.4 %copy-start.12 = (f32[8,32,128]{2,1,0:T(8,128)}, f32[8,32,128]{2,1,0:T(8,128)S(1)}, u32[]{:S(2)}) copy-start(f32[8,32,128]{2,1,0:T(8,128)S(1)} %collective-permute-done.12.got_2) | copy-start | bytes 393220
  (4 other events, 3.1 us)

commit v3 on v2

--- a/solution.py
+++ b/solution.py
@@ -364,7 +364,7 @@
 SMEM = pl.BlockSpec(memory_space=pltpu.SMEM)
 
 
-def call(kernel, args, outs, scratch, name, flops):
+def call(kernel, args, outs, scratch, name, flops, limit=28):
     arrays = [jax.ShapeDtypeStruct(shape, jnp.float32) for shape in outs]
     return pl.pallas_call(
         kernel,
@@ -373,6 +373,7 @@
         out_specs=[VMEM] * len(outs),
         scratch_shapes=[pltpu.VMEM(shape, jnp.float32) for shape in scratch],
         cost_estimate=pl.CostEstimate(flops=flops, bytes_accessed=4000000, transcendentals=0),
+        compiler_params=pltpu.CompilerParams(vmem_limit_bytes=limit << 20),
         name=name,
     )(*args)
 

time: 129 us -> 115 us (0.89)
  Pallas kernels: 52.1 us -> 42.7 us
  local copies, waits for them, and re-layouts: 6.02 us -> 1.42 us
    pallas_call x4, Pallas kernels: 52.1 us -> 42.7 us  [call(): pl.pallas_call(kernel, out_shape=arrays, in_specs=[SMEM] + [VMEM] * (len(...]
    unnamed x28 -> x8, local copies, waits for them, and re-layouts: 4.14 us -> 0.02 us
where the time goes in v3:
time: 115 us; the launch traced here: 114 us
  waiting for transfers between devices  46.1 us (40%)
  Pallas kernels  42.7 us (37%)
  starting transfers between devices  22.8 us (20%)
  local copies, waits for them, and re-layouts  1.42 us (1%)
    pallas_call x4, Pallas kernels, call(): pl.pallas_call(kernel, out_shape=arrays, in_specs=[SMEM] + [VMEM] * (len(...  42.7 us
    ppermute x2, waiting for transfers between devices, halos(): near = lax.ppermute(value, AXES, facing)  22 us
    ppermute x3, waiting for transfers between devices, body(): got.append(lax.ppermute(piece, 'sec', across(number)))  9.76 us
    ppermute x2, starting transfers between devices, halos(): near = lax.ppermute(value, AXES, facing)  9.42 us
    ppermute x2, waiting for transfers between devices, halos(): far = lax.ppermute(value, AXES, beyond)  8.28 us
    ppermute x3, waiting for transfers between devices, body(): lax.ppermute(outs[number], 'sec', across(number))  5.98 us
    ppermute x2, starting transfers between devices, halos(): on = lax.ppermute(value, AXES, partner)  4.83 us
    ppermute x2, starting transfers between devices, halos(): far = lax.ppermute(value, AXES, beyond)  3.84 us
  transfers between devices with their start and end apart: 14, of which 8 were waited for; matrix products, arithmetic and copies ran while one was open for 1% of the time, Pallas kernels for 0%

profile of v3, /device:TPU:105, one launch (start us, length us, event | category | flops | bytes accessed | tf_op | source)
XLA Modules:
  0.0 114.5 jit_solution(11550682093932141512)
XLA Ops:
  0.0 1.3 %constant_dynamic-slice_fusion = (f32[1,8,32,128]{3,2,1,0:T(8,128)S(1)}, f32[1,8,32,128]{3,2,1,0:T(8,128)S(1)}, f32[1,8,32,128]{3,2,1,0:T(8,128)S(1)}, f32[1,8,3...) fusion(f32[1,32,32,128]{3,2,1,0:T(8,128)} %param.6, s32[]{:T(128)S(6)} %select_n.61, ...), kind=kLoop, calls=%fused_computation.3 | loop fusion | bytes 1572876 | tf_op jit(solution)/shard_map/dynamic_slice | solution.py:426
  1.4 0.2 collective-permute-start.1
  1.6 1.0 collective-permute-start
  2.7 0.7 pad_maximum_fusion.2
  3.4 1.2 %collective-permute-start.2 = (f32[2,8,32,128]{3,2,1,0:T(8,128)}, f32[2,8,32,128]{3,2,1,0:T(8,128)S(1)}, u32[]{:S(2)}, u32[]{:S(2)}) collective-permute-start(f32[2,8,32,128]{3,2,1,0:T(8,128)} %pad_maximum_fusion.2), channel_id=1, source_target_pairs={{0,96},{32,64},{64,32},{96,0},{1,97},{33,65},{65,33},{97,1},{2,98}... | collective-permute-start | bytes 786440 | tf_op jit(solution)/shard_map/ppermute | solution.py:429
  5.3 3.3 %collective-permute-done.1.got_2 = f32[2,8,32,128]{3,2,1,0:T(8,128)S(1)} collective-permute-done((f32[2,8,32,128]{3,2,1,0:T(8,128)S(1)}, f32[2,8,32,128]{3,2,1,0:T(8,128)S(1)}, u32[]{:S(2)}, u32[]{:S(2)}) %collective-permute-start.1) | collective-permute-done | bytes 262176 | tf_op jit(solution)/shard_map/ppermute | solution.py:429
  8.6 6.5 %collective-permute-done.2.got_3 = f32[2,8,32,128]{3,2,1,0:T(8,128)S(1)} collective-permute-done((f32[2,8,32,128]{3,2,1,0:T(8,128)}, f32[2,8,32,128]{3,2,1,0:T(8,128)S(1)}, u32[]{:S(2)}, u32[]{:S(2)}) %collective-permute-start.2) | collective-permute-done | bytes 262176 | tf_op jit(solution)/shard_map/ppermute | solution.py:429
  15.1 1.2 %gather.1 = (f32[8,264,128]{2,1,0:T(8,128)S(1)}, f32[3,8,32,128]{3,2,1,0:T(8,128)S(1)}) custom-call(s32[10]{0:T(128)S(1)} %stack.51.scal, f32[32,32,128]{2,1,0:T(8,128)S(1)} %bitcast.11, f32[32,32,128]{2,1,0:T(8,128)S(1)} %bitcast.12, f32[32,32,128]{2,1,0:T(8,128)S(1)} %copy-done.2, s32[32,32,128]{2,1,0:T(8,128)S(1)} %copy-done.3, ...), custom_call_target="tpu_custom_call" | custom-call | flops 4000000 | bytes 4000000 | tf_op jit(solution)/shard_map/gather/pallas_call | solution.py:369
  16.3 4.7 %collective-permute-start.4 = (f32[8,264,128]{2,1,0:T(8,128)S(1)}, f32[8,264,128]{2,1,0:T(8,128)S(1)}, u32[]{:S(2)}, u32[]{:S(2)}) collective-permute-start(f32[8,264,128]{2,1,0:T(8,128)S(1)} %get-tuple-element.15.own), channel_id=1, source_target_pairs={{64,32},{32,64},{0,1},{1,0},{33,65},{65,33},{97,98},{98,97},{66,34... | collective-permute-start | bytes 3244040 | tf_op jit(solution)/shard_map/ppermute | solution.py:441
  21.0 1.9 %collective-permute-start.5 = (f32[8,264,128]{2,1,0:T(8,128)S(1)}, f32[8,264,128]{2,1,0:T(8,128)S(1)}, u32[]{:S(2)}, u32[]{:S(2)}) collective-permute-start(f32[8,264,128]{2,1,0:T(8,128)S(1)} %get-tuple-element.15.own), channel_id=1, source_target_pairs={{96,32},{32,1},{1,65},{65,98},{98,34},{34,3},{3,67},{67,4},{4,68},... | collective-permute-start | bytes 3244040 | tf_op jit(solution)/shard_map/ppermute | solution.py:442
  22.9 2.4 %collective-permute-start.3 = (f32[8,264,128]{2,1,0:T(8,128)S(1)}, f32[8,264,128]{2,1,0:T(8,128)S(1)}, u32[]{:S(2)}, u32[]{:S(2)}) collective-permute-start(f32[8,264,128]{2,1,0:T(8,128)S(1)} %get-tuple-element.15.own), channel_id=1, source_target_pairs={{96,64},{64,96},{32,0},{0,32},{1,33},{33,1},{65,97},{97,65},{98,66... | collective-permute-start | bytes 3244040 | tf_op jit(solution)/shard_map/ppermute | solution.py:443
  25.4 17.9 %collective-permute-done.4.near = f32[8,264,128]{2,1,0:T(8,128)S(1)} collective-permute-done((f32[8,264,128]{2,1,0:T(8,128)S(1)}, f32[8,264,128]{2,1,0:T(8,128)S(1)}, u32[]{:S(2)}, u32[]{:S(2)}) %collective-permute-start.4) | collective-permute-done | bytes 1081376 | tf_op jit(solution)/shard_map/ppermute | solution.py:441
  43.2 4.1 %collective-permute-done.5.far = f32[8,264,128]{2,1,0:T(8,128)S(1)} collective-permute-done((f32[8,264,128]{2,1,0:T(8,128)S(1)}, f32[8,264,128]{2,1,0:T(8,128)S(1)}, u32[]{:S(2)}, u32[]{:S(2)}) %collective-permute-start.5) | collective-permute-done | bytes 1081376 | tf_op jit(solution)/shard_map/ppermute | solution.py:442
  47.4 22.1 %first.1 = (f32[9,96,128]{2,1,0:T(8,128)S(1)}, f32[8,32,128]{2,1,0:T(8,128)S(1)}, f32[40,96,128]{2,1,0:T(8,128)S(1)}, f32[40,96,128]{2,1,0:T(8,128)S(1)}) custom-call(s32[10]{0:T(128)S(1)} %stack.51.scal, f32[8,264,128]{2,1,0:T(8,128)S(1)} %get-tuple-element.15.own, f32[8,264,128]{2,1,0:T(8,128)S(1)} %collective-permute-done.3.on, ...), custom_call_target="tpu_custom_call" | custom-call | flops 80000000 | bytes 4000000 | tf_op jit(solution)/shard_map/first/pallas_call | solution.py:369
  69.4 4.7 %collective-permute-start.8 = (f32[9,96,128]{2,1,0:T(8,128)S(1)}, f32[9,96,128]{2,1,0:T(8,128)S(1)}, u32[]{:S(2)}, u32[]{:S(2)}) collective-permute-start(f32[9,96,128]{2,1,0:T(8,128)S(1)} %get-tuple-element.17.own), channel_id=1, source_target_pairs={{64,32},{32,64},{0,1},{1,0},{33,65},{65,33},{97,98},{98,97},{66,34... | collective-permute-start | bytes 1327112 | tf_op jit(solution)/shard_map/ppermute | solution.py:441
  74.2 1.9 %collective-permute-start.9 = (f32[9,96,128]{2,1,0:T(8,128)S(1)}, f32[9,96,128]{2,1,0:T(8,128)S(1)}, u32[]{:S(2)}, u32[]{:S(2)}) collective-permute-start(f32[9,96,128]{2,1,0:T(8,128)S(1)} %get-tuple-element.17.own), channel_id=1, source_target_pairs={{96,32},{32,1},{1,65},{65,98},{98,34},{34,3},{3,67},{67,4},{4,68},... | collective-permute-start | bytes 1327112 | tf_op jit(solution)/shard_map/ppermute | solution.py:442
  76.1 2.4 %collective-permute-start.7 = (f32[9,96,128]{2,1,0:T(8,128)S(1)}, f32[9,96,128]{2,1,0:T(8,128)S(1)}, u32[]{:S(2)}, u32[]{:S(2)}) collective-permute-start(f32[9,96,128]{2,1,0:T(8,128)S(1)} %get-tuple-element.17.own), channel_id=1, source_target_pairs={{96,64},{64,96},{32,0},{0,32},{1,33},{33,1},{65,97},{97,65},{98,66... | collective-permute-start | bytes 1327112 | tf_op jit(solution)/shard_map/ppermute | solution.py:443
  78.5 4.2 %collective-permute-done.8.near = f32[9,96,128]{2,1,0:T(8,128)S(1)} collective-permute-done((f32[9,96,128]{2,1,0:T(8,128)S(1)}, f32[9,96,128]{2,1,0:T(8,128)S(1)}, u32[]{:S(2)}, u32[]{:S(2)}) %collective-permute-start.8) | collective-permute-done | bytes 442400 | tf_op jit(solution)/shard_map/ppermute | solution.py:441
  82.7 4.1 %collective-permute-done.9.far = f32[9,96,128]{2,1,0:T(8,128)S(1)} collective-permute-done((f32[9,96,128]{2,1,0:T(8,128)S(1)}, f32[9,96,128]{2,1,0:T(8,128)S(1)}, u32[]{:S(2)}, u32[]{:S(2)}) %collective-permute-start.9) | collective-permute-done | bytes 442400 | tf_op jit(solution)/shard_map/ppermute | solution.py:442
  86.8 18.1 %second.1 = (f32[8,32,128]{2,1,0:T(8,128)S(1)}, f32[8,32,128]{2,1,0:T(8,128)S(1)}, f32[8,32,128]{2,1,0:T(8,128)S(1)}, f32[8,32,128]{2,1,0:T(8,128)S(1)}) custom-call(s32[10]{0:T(128)S(1)} %stack.51.scal, f32[9,96,128]{2,1,0:T(8,128)S(1)} %get-tuple-element.17.own, f32[9,96,128]{2,1,0:T(8,128)S(1)} %collective-permute-done.7.on, ...), custom_call_target="tpu_custom_call" | custom-call | flops 80000000 | bytes 4000000 | tf_op jit(solution)/shard_map/second/pallas_call | solution.py:369
  105.1 2.0 %collective-permute-start.13 = (f32[8,32,128]{2,1,0:T(8,128)S(1)}, f32[8,32,128]{2,1,0:T(8,128)S(1)}, u32[]{:S(2)}, u32[]{:S(2)}) collective-permute-start(f32[8,32,128]{2,1,0:T(8,128)S(1)} %get-tuple-element.24), channel_id=1, source_target_pairs={{0,96},{32,64},{64,32},{96,0},{1,97},{33,65},{65,33},{97,1},{2,98}... | collective-permute-start | bytes 393224 | tf_op jit(solution)/shard_map/ppermute | solution.py:466
  107.1 2.6 %collective-permute-done.12.got_2 = f32[8,32,128]{2,1,0:T(8,128)S(1)} collective-permute-done((f32[8,32,128]{2,1,0:T(8,128)S(1)}, f32[8,32,128]{2,1,0:T(8,128)S(1)}, u32[]{:S(2)}, u32[]{:S(2)}) %collective-permute-start.12) | collective-permute-done | bytes 131104 | tf_op jit(solution)/shard_map/ppermute | solution.py:466
  109.7 3.4 %collective-permute-done.13.got_3 = f32[8,32,128]{2,1,0:T(8,128)S(1)} collective-permute-done((f32[8,32,128]{2,1,0:T(8,128)S(1)}, f32[8,32,128]{2,1,0:T(8,128)S(1)}, u32[]{:S(2)}, u32[]{:S(2)}) %collective-permute-start.13) | collective-permute-done | bytes 131104 | tf_op jit(solution)/shard_map/ppermute | solution.py:466
  113.1 1.4 %spread.1 = f32[32,32,128]{2,1,0:T(8,128)} custom-call(s32[10]{0:T(128)S(1)} %stack.51.scal, f32[8,32,128]{2,1,0:T(8,128)S(1)} %get-tuple-element.21.own, f32[8,32,128]{2,1,0:T(8,128)S(1)} %collective-permute-done.11.got_1, f32[8,32,128]{2,1,0:T(8,128)S(1)} %collective-permute-done.12.got_2, f32[8,32,128]{2,1,0:T(8,128)S(1)} %collective-permute-done.13.got_3), custom_call_target="tpu_custom_call" | custom-call | flops 100000 | bytes 4000000 | tf_op jit(solution)/shard_map/spread/pallas_call | solution.py:369
  (21 shorter events, 0.3 us)
Async XLA Ops:
  0.0 15.1 %copy-start.3 = (s32[32,32,128]{2,1,0:T(8,128)S(1)}, s32[32,32,128]{2,1,0:T(8,128)}, u32[]{:S(2)}) copy-start(s32[32,32,128]{2,1,0:T(8,128)} %exc.1) | copy-start | bytes 1572868
  1.3 13.8 %copy-start = (f32[1,32,32,128]{3,2,1,0:T(8,128)S(1)}, f32[1,32,32,128]{3,2,1,0:T(8,128)}, u32[]{:S(2)}) copy-start(f32[1,32,32,128]{3,2,1,0:T(8,128)} %param.5) | copy-start | bytes 1572868
  1.3 13.8 %copy-start.1 = (f32[1,32,32,128]{3,2,1,0:T(8,128)S(1)}, f32[1,32,32,128]{3,2,1,0:T(8,128)}, u32[]{:S(2)}) copy-start(f32[1,32,32,128]{3,2,1,0:T(8,128)} %param.6) | copy-start | bytes 1572868
  1.3 13.8 %copy-start.2 = (f32[32,32,128]{2,1,0:T(8,128)S(1)}, f32[32,32,128]{2,1,0:T(8,128)}, u32[]{:S(2)}) copy-start(f32[32,32,128]{2,1,0:T(8,128)} %rec.1) | copy-start | bytes 1572868
  1.4 7.3 %collective-permute-start.1 = (f32[2,8,32,128]{3,2,1,0:T(8,128)S(1)}, f32[2,8,32,128]{3,2,1,0:T(8,128)S(1)}, u32[]{:S(2)}, u32[]{:S(2)}) collective-permute-start(f32[2,8,32,128]{3,2,1,0:T(8,128)S(1)} %pad_maximum_fusion.1), channel_id=1, source_target_pairs={{0,64},{32,96},{64,0},{96,32},{1,65},{33,97},{65,1},{97,33},{2,66}... | collective-permute-start | bytes 786440 | tf_op jit(solution)/shard_map/ppermute | solution.py:429
  1.6 7.0 %collective-permute-start = (f32[2,8,32,128]{3,2,1,0:T(8,128)S(1)}, f32[2,8,32,128]{3,2,1,0:T(8,128)S(1)}, u32[]{:S(2)}, u32[]{:S(2)}) collective-permute-start(f32[2,8,32,128]{3,2,1,0:T(8,128)S(1)} %pad_maximum_fusion), channel_id=1, source_target_pairs={{0,32},{32,0},{64,96},{96,64},{1,33},{33,1},{65,97},{97,65},{2,34}... | collective-permute-start | bytes 786440 | tf_op jit(solution)/shard_map/ppermute | solution.py:429
  3.4 11.7 %collective-permute-start.2 = (f32[2,8,32,128]{3,2,1,0:T(8,128)}, f32[2,8,32,128]{3,2,1,0:T(8,128)S(1)}, u32[]{:S(2)}, u32[]{:S(2)}) collective-permute-start(f32[2,8,32,128]{3,2,1,0:T(8,128)} %pad_maximum_fusion.2), channel_id=1, source_target_pairs={{0,96},{32,64},{64,32},{96,0},{1,97},{33,65},{65,33},{97,1},{2,98}... | collective-permute-start | bytes 786440 | tf_op jit(solution)/shard_map/ppermute | solution.py:429
  16.3 26.9 %collective-permute-start.4 = (f32[8,264,128]{2,1,0:T(8,128)S(1)}, f32[8,264,128]{2,1,0:T(8,128)S(1)}, u32[]{:S(2)}, u32[]{:S(2)}) collective-permute-start(f32[8,264,128]{2,1,0:T(8,128)S(1)} %get-tuple-element.15.own), channel_id=1, source_target_pairs={{64,32},{32,64},{0,1},{1,0},{33,65},{65,33},{97,98},{98,97},{66,34... | collective-permute-start | bytes 3244040 | tf_op jit(solution)/shard_map/ppermute | solution.py:441
  21.0 26.3 %collective-permute-start.5 = (f32[8,264,128]{2,1,0:T(8,128)S(1)}, f32[8,264,128]{2,1,0:T(8,128)S(1)}, u32[]{:S(2)}, u32[]{:S(2)}) collective-permute-start(f32[8,264,128]{2,1,0:T(8,128)S(1)} %get-tuple-element.15.own), channel_id=1, source_target_pairs={{96,32},{32,1},{1,65},{65,98},{98,34},{34,3},{3,67},{67,4},{4,68},... | collective-permute-start | bytes 3244040 | tf_op jit(solution)/shard_map/ppermute | solution.py:442
  22.9 24.4 %collective-permute-start.3 = (f32[8,264,128]{2,1,0:T(8,128)S(1)}, f32[8,264,128]{2,1,0:T(8,128)S(1)}, u32[]{:S(2)}, u32[]{:S(2)}) collective-permute-start(f32[8,264,128]{2,1,0:T(8,128)S(1)} %get-tuple-element.15.own), channel_id=1, source_target_pairs={{96,64},{64,96},{32,0},{0,32},{1,33},{33,1},{65,97},{97,65},{98,66... | collective-permute-start | bytes 3244040 | tf_op jit(solution)/shard_map/ppermute | solution.py:443
  43.2 4.2 %collective-permute-start.6 = (f32[8,264,128]{2,1,0:T(8,128)S(1)}, f32[8,264,128]{2,1,0:T(8,128)S(1)}, u32[]{:S(2)}, u32[]{:S(2)}) collective-permute-start(f32[8,264,128]{2,1,0:T(8,128)S(1)} %collective-permute-done.4.near), channel_id=1, source_target_pairs={{96,64},{64,96},{32,0},{0,32},{1,33},{33,1},{65,97},{97,65},{98,66... | collective-permute-start | bytes 3244040 | tf_op jit(solution)/shard_map/ppermute | solution.py:444
  69.4 13.2 %collective-permute-start.8 = (f32[9,96,128]{2,1,0:T(8,128)S(1)}, f32[9,96,128]{2,1,0:T(8,128)S(1)}, u32[]{:S(2)}, u32[]{:S(2)}) collective-permute-start(f32[9,96,128]{2,1,0:T(8,128)S(1)} %get-tuple-element.17.own), channel_id=1, source_target_pairs={{64,32},{32,64},{0,1},{1,0},{33,65},{65,33},{97,98},{98,97},{66,34... | collective-permute-start | bytes 1327112 | tf_op jit(solution)/shard_map/ppermute | solution.py:441
  74.2 12.7 %collective-permute-start.9 = (f32[9,96,128]{2,1,0:T(8,128)S(1)}, f32[9,96,128]{2,1,0:T(8,128)S(1)}, u32[]{:S(2)}, u32[]{:S(2)}) collective-permute-start(f32[9,96,128]{2,1,0:T(8,128)S(1)} %get-tuple-element.17.own), channel_id=1, source_target_pairs={{96,32},{32,1},{1,65},{65,98},{98,34},{34,3},{3,67},{67,4},{4,68},... | collective-permute-start | bytes 1327112 | tf_op jit(solution)/shard_map/ppermute | solution.py:442
  76.1 10.7 %collective-permute-start.7 = (f32[9,96,128]{2,1,0:T(8,128)S(1)}, f32[9,96,128]{2,1,0:T(8,128)S(1)}, u32[]{:S(2)}, u32[]{:S(2)}) collective-permute-start(f32[9,96,128]{2,1,0:T(8,128)S(1)} %get-tuple-element.17.own), channel_id=1, source_target_pairs={{96,64},{64,96},{32,0},{0,32},{1,33},{33,1},{65,97},{97,65},{98,66... | collective-permute-start | bytes 1327112 | tf_op jit(solution)/shard_map/ppermute | solution.py:443
  82.7 4.1 %collective-permute-start.10 = (f32[9,96,128]{2,1,0:T(8,128)S(1)}, f32[9,96,128]{2,1,0:T(8,128)S(1)}, u32[]{:S(2)}, u32[]{:S(2)}) collective-permute-start(f32[9,96,128]{2,1,0:T(8,128)S(1)} %collective-permute-done.8.near), channel_id=1, source_target_pairs={{96,64},{64,96},{32,0},{0,32},{1,33},{33,1},{65,97},{97,65},{98,66... | collective-permute-start | bytes 1327112 | tf_op jit(solution)/shard_map/ppermute | solution.py:444
  104.9 2.2 %collective-permute-start.11 = (f32[8,32,128]{2,1,0:T(8,128)S(1)}, f32[8,32,128]{2,1,0:T(8,128)S(1)}, u32[]{:S(2)}, u32[]{:S(2)}) collective-permute-start(f32[8,32,128]{2,1,0:T(8,128)S(1)} %get-tuple-element.22), channel_id=1, source_target_pairs={{0,32},{32,0},{64,96},{96,64},{1,33},{33,1},{65,97},{97,65},{2,34}... | collective-permute-start | bytes 393224 | tf_op jit(solution)/shard_map/ppermute | solution.py:466
  105.0 4.7 %collective-permute-start.12 = (f32[8,32,128]{2,1,0:T(8,128)S(1)}, f32[8,32,128]{2,1,0:T(8,128)S(1)}, u32[]{:S(2)}, u32[]{:S(2)}) collective-permute-start(f32[8,32,128]{2,1,0:T(8,128)S(1)} %get-tuple-element.23), channel_id=1, source_target_pairs={{0,64},{32,96},{64,0},{96,32},{1,65},{33,97},{65,1},{97,33},{2,66}... | collective-permute-start | bytes 393224 | tf_op jit(solution)/shard_map/ppermute | solution.py:466
  105.1 8.0 %collective-permute-start.13 = (f32[8,32,128]{2,1,0:T(8,128)S(1)}, f32[8,32,128]{2,1,0:T(8,128)S(1)}, u32[]{:S(2)}, u32[]{:S(2)}) collective-permute-start(f32[8,32,128]{2,1,0:T(8,128)S(1)} %get-tuple-element.24), channel_id=1, source_target_pairs={{0,96},{32,64},{64,32},{96,0},{1,97},{33,65},{65,33},{97,1},{2,98}... | collective-permute-start | bytes 393224 | tf_op jit(solution)/shard_map/ppermute | solution.py:466

commit v4 on v3

v4 whole, which is shorter than its diff:
```python
import jax
import jax.numpy as jnp
from jax import lax
from jax.experimental import pallas as pl
from jax.experimental.pallas import tpu as pltpu
from jax.sharding import PartitionSpec as P

SUBSTEPS = 8
SWEEPS = 16

coupling_gain = 0.1
ionic_timestep = 0.05
ionic_gain = 8.0
recovery_rate = 0.1
recovery_decay = 0.5
spectrum_low = 0.04
spectrum_high = 12.32

SLAB = 8
ROWS = 96
HEART = 32
SLOTS = 40
OWN = 16
OFF = 1
PAD = 8
PART = 16
PARTS = ROWS // PART
AXES = ("sec", "brick")
V0_AT, V1_AT, D_AT, ROW_AT, MSG = 96, 128, 160, 256, 264
PHI_PAD = 112
V_PAD = 48


def chebyshev_weights(count):
    center = 0.5 * (spectrum_high + spectrum_low)
    spread = 0.5 * (spectrum_high - spectrum_low)
    ratio = center / spread
    current = 1.0 / ratio
    weights = [(0.0, 1.0 / center)]
    for _ in range(count):
        following = 1.0 / (2.0 * ratio - current)
        weights.append((following * current, 2.0 * following / spread))
        current = following
    return weights


WEIGHTS = chebyshev_weights(SWEEPS - 1)
SHIFT = 6.0 - 0.5 * (spectrum_high + spectrum_low)


def ionic(voltage, recovery, threshold, active):
    for _ in range(SUBSTEPS):
        drive = ionic_gain * voltage * (voltage - threshold) * (1.0 - voltage) - recovery
        relax = recovery_rate * (voltage - recovery_decay * recovery)
        voltage = voltage + ionic_timestep * active * drive
        recovery = recovery + ionic_timestep * active * relax
    return voltage, recovery


def lanes(shape):
    return lax.broadcasted_iota(jnp.int32, shape, len(shape) - 1)


def side_sum_zero(value):
    lane = lanes(value.shape)
    before = jnp.where(lane == 0, 0.0, pltpu.roll(value, 1, 1))
    after = jnp.where(lane == 127, 0.0, pltpu.roll(value, 127, 1))
    return before + after


def side_sum_edge(value):
    lane = lanes(value.shape)
    before = jnp.where(lane == 0, value, pltpu.roll(value, 1, 1))
    after = jnp.where(lane == 127, value, pltpu.roll(value, 127, 1))
    return before + after


def heart_laplace(ref, x):
    here = ref[x, PAD : PAD + HEART]
    total = ref[x - 1, PAD : PAD + HEART] + ref[x + 1, PAD : PAD + HEART]
    total = total + ref[x, PAD - 1 : PAD - 1 + HEART] + ref[x, PAD + 1 : PAD + 1 + HEART]
    return total + side_sum_edge(here) - 6.0 * here


def put_heart(ref, x, value):
    ref[x, PAD : PAD + HEART] = value
    ref[x, PAD - 1 : PAD] = value[0:1]
    ref[x, PAD + HEART : PAD + HEART + 1] = value[HEART - 1 : HEART]


def torso_current(ref, x, row):
    at = PAD + HEART * row
    here = ref[x, at : at + HEART]
    total = ref[x - 1, at : at + HEART] + ref[x + 1, at : at + HEART]
    total = total + ref[x, at - 1 : at - 1 + HEART] + ref[x, at + 1 : at + 1 + HEART]
    return total + side_sum_zero(here) - 6.0 * here


def halves(value):
    high = value.astype(jnp.bfloat16)
    return high, (value - high.astype(jnp.float32)).astype(jnp.bfloat16)


def sweep(scal, plan, even, odd, absorb, source):
    accs = [pltpu.ACC(part % 2)((PART, 256), jnp.float32) for part in range(2 * PARTS)]
    pl.run_scoped(lambda *refs: sweep_with(scal, plan, even, odd, absorb, source, refs), *accs)


def sweep_with(scal, plan, even, odd, absorb, source, accs):
    accs = (accs[:PARTS], accs[PARTS:])
    low_end, high_end = scal[4], scal[5]
    row = lax.broadcasted_iota(jnp.int32, (256, 256), 0)
    column = lax.broadcasted_iota(jnp.int32, (256, 256), 1)
    same = (row >= 128) == (column >= 128)
    apart = jnp.abs(row - column)
    beside = ((same & (apart == 1)) | (apart == 128)).astype(jnp.bfloat16)
    none = jnp.zeros((PART, 256), jnp.bfloat16)
    for unit in range(2):
        pltpu.matmul_push_rhs(beside, 0, unit)
    for number, acc in enumerate(accs[0] + accs[1]):
        pltpu.matmul_acc_lhs(acc, none, load_staged_rhs=0 if number < 2 else None)
    for acc in accs[0] + accs[1]:
        pltpu.matmul_pop(acc)

    def place(number, pair):
        _, runs = plan[number]
        first, size = runs[0]
        x = first + 2 * pair
        if len(runs) == 1:
            return x
        skip = runs[1][0] - first - size
        if isinstance(pair, int):
            return x + (skip if 2 * pair >= size else 0)
        return x + jnp.where(2 * pair >= size, skip, 0)

    def begin(number, pair, acc):
        level = plan[number][0]
        src = even if level % 2 else odd
        x = place(number, pair) + OFF
        for part in range(PARTS):
            at, to = PAD + PART * part, PAD + PART * (part + 1)
            high_0, low_0 = halves(src[x, at:to])
            high_1, low_1 = halves(src[x + 1, at:to])
            pltpu.matmul_acc_lhs(acc[part], jnp.concatenate([high_0, high_1], 1))
            pltpu.matmul_acc_lhs(acc[part], jnp.concatenate([low_0, low_1], 1))

    def finish(number, pair, acc):
        level = plan[number][0]
        src, dst = (even, odd) if level % 2 else (odd, even)
        x = place(number, pair)
        keeps, pushes = [], []
        for plane in range(2):
            inside = (x + plane >= low_end) & (x + plane < high_end)
            keeps.append(jnp.where(inside, WEIGHTS[level - 1][0], 0.0).astype(jnp.float32))
            pushes.append(jnp.where(inside, WEIGHTS[level - 1][1], 0.0).astype(jnp.float32))
        for part in range(PARTS):
            start, stop = PART * part, PART * (part + 1)
            at, to = PAD + start, PAD + stop
            sums = pltpu.matmul_pop(acc[part])
            for plane in range(2):
                here = x + plane
                total = src[here + OFF - 1 + 2 * plane, at:to]
                total = total + (src[here + OFF, at - 1 : to - 1] + src[here + OFF, at + 1 : to + 1])
                total = total + source[here, start:stop]
                total = total - absorb[here, start:stop] * src[here + OFF, at:to]
                total = pushes[plane] * (total + sums[:, 128 * plane : 128 * (plane + 1)])
                if level > 1:
                    total = total - keeps[plane] * dst[here + OFF, at:to]
                dst[here + OFF, at:to] = total

    one, other = accs
    begin(0, 0, one)
    for number, (_, runs) in enumerate(plan):
        pairs = sum(size for _, size in runs) // 2
        steps = (pairs - 1) // 2

        def two_pairs(step, carry, number=number, one=one, other=other):
            begin(number, 2 * step + 1, other)
            finish(number, 2 * step, one)
            begin(number, 2 * step + 2, one)
            finish(number, 2 * step + 1, other)
            return carry

        if steps:
            lax.fori_loop(0, steps, two_pairs, 0)
        pair = 2 * steps
        if pairs - pair == 2:
            begin(number, pair + 1, other)
            finish(number, pair, one)
            pair, one, other = pair + 1, other, one
        following = number + 1 < len(plan)
        if following and pairs > 2:
            begin(number + 1, 0, other)
        finish(number, pair, one)
        if following and pairs <= 2:
            begin(number + 1, 0, other)
        one, other = other, one


END = OWN + 2 * SLAB
INNER = [(k, [(OWN + k, 2 * SLAB - 2 * k)]) for k in range(1, SLAB)]
CLOSE = [(k, [(SLAB + k, SLAB), (END - k, SLAB)]) for k in range(1, SLAB + 1)]
OUTER = [(k, [(k, SLAB)]) for k in range(1, SLAB + 1)]
OUTER += [(k, [(k, SLOTS - 2 * k)]) for k in range(SLAB + 1, SWEEPS + 1)]


def clear_edges(even, odd):
    zero = jnp.zeros((PAD, 128), jnp.float32)

    def edge(x, carry):
        for ref in (even, odd):
            ref[x, 0:PAD] = zero
            ref[x, PAD + ROWS : PHI_PAD] = zero
        return carry

    lax.fori_loop(0, SLOTS + 2, edge, 0)


def gather_kernel(scal, pot, coef, rec, exc, got_1, got_2, got_3, msg, aux, deep):
    sec, chunk, flip = scal[0], scal[1], scal[2]
    strip = jnp.full((8, 128), scal[3].astype(jnp.float32))

    def plane(u, carry):
        x = jnp.where(flip == 1, SLAB - 1 - u, u)
        whole = SLAB * chunk + x
        for number, ref in enumerate((None, got_1, got_2, got_3)):
            at = pl.multiple_of((sec ^ number) * HEART, HEART)
            if number == 0:
                msg[u, pl.ds(at, HEART)] = pot[whole]
                deep[u, pl.ds(at, HEART)] = coef[whole]
            else:
                msg[u, pl.ds(at, HEART)] = ref[0, x]
                deep[u, pl.ds(at, HEART)] = ref[1, x]
        msg[u, D_AT : D_AT + ROWS] = deep[u, 0:ROWS]
        threshold = deep[u, ROWS : ROWS + HEART]
        active = exc[whole].astype(jnp.float32)
        voltage, recovery = ionic(msg[u, V0_AT : V0_AT + HEART], rec[whole], threshold, active)
        msg[u, V1_AT : V1_AT + HEART] = voltage
        msg[u, ROW_AT : ROW_AT + 8] = strip
        aux[0, u] = threshold
        aux[1, u] = recovery
        aux[2, u] = active
        return carry

    lax.fori_loop(0, SLAB, plane, 0)


def take(ref, first, step, even, absorb=None, volt=None, volt_1=None):
    def plane(u, carry):
        x = first + step * u
        even[x + OFF, PAD : PAD + ROWS] = ref[u, 0:ROWS]
        if absorb is not None:
            absorb[x] = ref[u, D_AT : D_AT + ROWS] + SHIFT
            put_heart(volt, x, ref[u, V0_AT : V0_AT + HEART])
            put_heart(volt_1, x, ref[u, V1_AT : V1_AT + HEART])
        return carry

    lax.fori_loop(0, SLAB, plane, 0)


def embed(low, high, mark, volt, volt_1, source, later):
    mark = jnp.broadcast_to(mark, (HEART, 128))

    def plane(x, carry):
        for ref, out in ((volt, source), (volt_1, later)):
            gain = heart_laplace(ref, x)
            for layer in range(3):
                out[x, layer * HEART : (layer + 1) * HEART] = jnp.where(mark == layer, gain, 0.0)
        return carry

    lax.fori_loop(low, high, plane, 0)


def on_layer(row, work):
    for layer in range(3):

        @pl.when(row == layer)
        def _():
            work(layer)


def couple(first, last, row, even, volt_1, aux, held):
    def work(layer):
        def plane(u, carry):
            x = OWN + u
            gain = heart_laplace(volt_1, x) + torso_current(even, x + OFF, layer)
            voltage = volt_1[x, PAD : PAD + HEART] + coupling_gain * gain
            held[u], _ = ionic(voltage, aux[1, u], aux[0, u], aux[2, u])
            return carry

        lax.fori_loop(first, last, plane, 0)

    on_layer(row, work)


def settle(first, last, row, even, volt, out):
    def work(layer):
        def plane(u, carry):
            gain = heart_laplace(volt, u + 1) + torso_current(even, OWN + OFF + u, layer)
            out[u] = volt[u + 1, PAD : PAD + HEART] + coupling_gain * gain
            return carry

        lax.fori_loop(first, last, plane, 0)

    on_layer(row, work)


def first_inner(scal, own, on, aux, even, odd, absorb, source, later, volt, volt_1, held, copy):
    def send(u, carry):
        copy[u] = own[u]
        return carry

    lax.fori_loop(0, SLAB, send, 0)
    clear_edges(even, odd)
    take(own, OWN, 1, even, absorb, volt, volt_1)
    take(on, END - 1, -1, even, absorb, volt, volt_1)
    row = jnp.full((1, 128), scal[3].astype(jnp.float32))
    embed(OWN + 1, END - 1, row, volt, volt_1, source, later)
    couple(1, SLAB, scal[3], even, volt_1, aux, held)
    sweep(scal, INNER, even, odd, absorb, source)


def first_close(scal, near, on2, aux, *refs):
    even, odd, absorb, source, later, volt, volt_1, held = refs[8:]
    take(near, OWN - 1, -1, even, absorb, volt, volt_1)
    take(on2, END, 1, even, absorb, volt, volt_1)

    @pl.when(scal[4] == OWN)
    def _():
        for ref in (volt, volt_1):
            ref[OWN - 1] = ref[OWN]

    @pl.when(scal[5] == END)
    def _():
        for ref in (volt, volt_1):
            ref[END] = ref[END - 1]

    row = jnp.full((1, 128), scal[3].astype(jnp.float32))
    for low, high, mark in (
        (SLAB + 1, OWN, near[0, ROW_AT : ROW_AT + 1]),
        (OWN, OWN + 1, row),
        (END - 1, END, row),
        (END, SLOTS - 1, on2[0, ROW_AT : ROW_AT + 1]),
    ):
        embed(low, high, mark, volt, volt_1, source, later)
    couple(0, 1, scal[3], even, volt_1, aux, held)
    sweep(scal, CLOSE, even, odd, absorb, source)


def first_outer(scal, far, held, *refs):
    msg, even, odd, absorb, source, later, volt, volt_1 = refs[7:]
    take(far, 0, 1, even, absorb, volt, volt_1)
    embed(1, SLAB + 1, far[0, ROW_AT : ROW_AT + 1], volt, volt_1, source, later)
    sweep(scal, OUTER, even, odd, absorb, source)
    for u in range(SLAB):
        msg[u] = even[OFF + OWN + u, PAD : PAD + ROWS]
    msg[SLAB, 0:HEART] = held[0]
    msg[SLAB, HEART : 2 * HEART] = held[SLAB - 1]
    msg[SLAB, 2 * HEART : ROWS] = jnp.zeros((HEART, 128), jnp.float32)


def second_inner(scal, own, on, held, absorb, source, even, odd, volt, out, copy):
    def keep(u, carry):
        copy[u] = own[u]
        put_heart(volt, u + 1, held[u])
        return carry

    lax.fori_loop(0, SLAB, keep, 0)
    clear_edges(even, odd)
    take(own, OWN, 1, even)
    take(on, END - 1, -1, even)
    put_heart(volt, SLAB + 1, on[SLAB, HEART : 2 * HEART])
    settle(1, SLAB, scal[3], even, volt, out)
    sweep(scal, INNER, even, odd, absorb, source)


def second_close(scal, near, on2, absorb, source, *refs):
    even, odd, volt, out = refs[4:]
    take(near, OWN - 1, -1, even)
    take(on2, END, 1, even)
    put_heart(volt, 0, near[SLAB, 0:HEART])

    @pl.when(scal[4] == OWN)
    def _():
        volt[0] = volt[1]

    settle(0, 1, scal[3], even, volt, out)
    sweep(scal, CLOSE, even, odd, absorb, source)


def second_outer(scal, far, absorb, source, voltage, *refs):
    outs, (even, odd), (joined,) = refs[2:6], refs[6:8], refs[8:]
    take(far, 0, 1, even)
    sweep(scal, OUTER, even, odd, absorb, source)
    sec, flip = scal[0], scal[2]

    def plane(u, carry):
        joined[u, 0:ROWS] = even[OFF + OWN + u, PAD : PAD + ROWS]
        joined[u, ROWS : ROWS + HEART] = voltage[u]
        x = jnp.where(flip == 1, SLAB - 1 - u, u)
        for number in range(4):
            at = pl.multiple_of((sec ^ number) * HEART, HEART)
            outs[number][x] = joined[u, pl.ds(at, HEART)]
        return carry

    lax.fori_loop(0, SLAB, plane, 0)


def spread_kernel(scal, own, got_1, got_2, got_3, out):
    for number, ref in enumerate((own, got_1, got_2, got_3)):
        at = scal[6 + number] * SLAB
        for u in range(SLAB):
            out[at + u] = ref[u]


def chain(sections, bricks):
    order = []
    for brick in range(bricks):
        forward = (brick + brick // 4) % 2 == 1
        for step in range(sections):
            sec = step if forward else sections - 1 - step
            order.append(sec * bricks + brick)
    return order


VMEM = pl.BlockSpec(memory_space=pltpu.VMEM)
SMEM = pl.BlockSpec(memory_space=pltpu.SMEM)


def call(kernel, args, outs, planes, scratch=(), state=(), limit=20):
    arrays = [jax.ShapeDtypeStruct(shape, jnp.float32) for shape in outs]
    arrays += [jax.ShapeDtypeStruct(ref.shape, ref.dtype) for ref in state]
    return pl.pallas_call(
        kernel,
        out_shape=arrays,
        in_specs=[SMEM] + [VMEM] * (len(args) + len(state) - 1),
        out_specs=[VMEM] * len(arrays),
        scratch_shapes=[pltpu.VMEM(shape, jnp.float32) for shape in scratch],
        input_output_aliases={len(args) + n: len(outs) + n for n in range(len(state))},
        compiler_params=pltpu.CompilerParams(vmem_limit_bytes=limit << 20),
        cost_estimate=pl.CostEstimate(
            flops=planes * 200_000, bytes_accessed=planes * 100_000, transcendentals=0
        ),
    )(*args, *state)


def body(potentials, coefficient, recovery, excitable, row_of):
    pot, coef = potentials[0], coefficient[0]
    sections, bricks = lax.axis_size("sec"), lax.axis_size("brick")
    order = chain(sections, bricks)
    count = len(order)
    last = count - 1
    partner = [(order[i], order[i ^ 1]) for i in range(count)]
    facing = []
    for i in range(1, last, 2):
        facing += [(order[i], order[i + 1]), (order[i + 1], order[i])]
    beyond = [(order[i], order[i + 2]) for i in range(0, count - 2, 2)]
    beyond += [(order[i], order[i - 2]) for i in range(3, count, 2)]

    def across(number):
        return [(sec, sec ^ number) for sec in range(sections)]

    sec = lax.axis_index("sec")
    brick = lax.axis_index("brick")
    forward = (brick + brick // 4) % 2 == 1

    def chunk_of(section):
        return jnp.where(forward, section, sections - 1 - section)

    chunk = chunk_of(sec)
    place = brick * sections + chunk
    no_facing = (place == 0) | (place == last)
    partner_end = (place == 1) | (place == last - 1)
    scal = jnp.stack(
        [
            sec,
            chunk,
            chunk % 2,
            row_of[0],
            jnp.where(no_facing, OWN, 0),
            jnp.where(partner_end, OWN + 2 * SLAB, SLOTS),
        ]
        + [chunk_of(sec ^ number) for number in range(4)]
    ).astype(jnp.int32)

    got = []
    for number in (1, 2, 3):
        start = SLAB * chunk_of(sec ^ number)
        piece = jnp.stack(
            [
                lax.dynamic_slice_in_dim(pot, start, SLAB, 0),
                lax.dynamic_slice_in_dim(coef, start, SLAB, 0),
            ]
        )
        got.append(lax.ppermute(piece, "sec", across(number)))

    msg, aux = call(
        gather_kernel,
        (scal, pot, coef, recovery, excitable, *got),
        [(SLAB, MSG, 128), (3, SLAB, HEART, 128)],
        20,
        scratch=[(SLAB, 128, 128)],
    )

    phi = (SLOTS + 2, PHI_PAD, 128)
    wide = (SLOTS, ROWS, 128)
    volt = (SLOTS, V_PAD, 128)
    heart = (SLAB, HEART, 128)

    def move(value, pairs):
        return lax.ppermute(value, AXES, pairs)

    near = move(msg, facing)
    on = move(msg, partner)
    *state, copy = call(
        first_inner,
        (scal, msg, on, aux),
        [phi, phi, wide, wide, wide, volt, volt, heart, msg.shape],
        56,
    )
    far = move(copy, beyond)
    on2 = move(near, partner)
    *state, held = call(first_close, (scal, near, on2, aux), [], 128, state=state)
    msg, _, _, absorb, _, later, _, _ = call(
        first_outer, (scal, far, held), [(SLAB + 1, ROWS, 128)], 184, state=state
    )

    near = move(msg, facing)
    on = move(msg, partner)
    *state, copy = call(
        second_inner,
        (scal, msg, on, held, absorb, later),
        [phi, phi, (SLAB + 2, V_PAD, 128), heart, (SLAB, ROWS, 128)],
        56,
    )
    far = move(copy, beyond)
    on2 = move(near, partner)
    even, odd, _, voltage = call(
        second_close, (scal, near, on2, absorb, later), [], 128, state=state
    )
    outs = call(
        second_outer,
        (scal, far, absorb, later, voltage),
        [heart] * 4,
        184,
        scratch=[(SLAB, 128, 128)],
        state=[even, odd],
    )[:4]
    back = [outs[0]] + [lax.ppermute(outs[number], "sec", across(number)) for number in (1, 2, 3)]
    (result,) = call(spread_kernel, (scal, *back), [(sections * SLAB, HEART, 128)], 5)
    return result[None]


def solution(mesh):
    in_specs = (
        P("sec", "brick", None, None),
        P("sec", "brick", None, None),
        P("brick", None, None),
        P("brick", None, None),
        P("brick"),
    )
    out_specs = P("sec", "brick", None, None)
    return jax.shard_map(body, mesh=mesh, in_specs=in_specs, out_specs=out_specs, check_vma=False)
```

time: 115 us -> 116 us (level)
  waiting for transfers between devices: 46.1 us -> 50.4 us
  starting transfers between devices: 22.8 us -> 19.7 us
  Pallas kernels: 42.7 us -> 41.4 us
    ppermute x8, waiting for transfers between devices: 30.3 us -> 34.3 us  [move(): return lax.ppermute(value, AXES, pairs)]
    ppermute x8, starting transfers between devices: 18.1 us -> 14.6 us  [move(): return lax.ppermute(value, AXES, pairs)]
    pallas_call x4 -> x8, Pallas kernels: 42.7 us -> 41.4 us  [call(): pl.pallas_call(kernel, out_shape=arrays, in_specs=[SMEM] + [VMEM] * (len(...]
  transfers between devices with their start and end apart: 14 -> 14, of which waited for: 8 -> 8; matrix products, arithmetic and copies ran while one was open for 1% -> 1% of each run, Pallas kernels for 0% -> 20%
where the time goes in v4:
time: 116 us; the launch traced here: 115 us
  waiting for transfers between devices  50.4 us (43%)
  Pallas kernels  41.4 us (36%)
  starting transfers between devices  19.7 us (17%)
  local copies, waits for them, and re-layouts  1.49 us (1%)
    pallas_call x8, Pallas kernels, call(): pl.pallas_call(kernel, out_shape=arrays, in_specs=[SMEM] + [VMEM] * (len(...  41.4 us
    ppermute x8, waiting for transfers between devices, move(): return lax.ppermute(value, AXES, pairs)  34.3 us
    ppermute x8, starting transfers between devices, move(): return lax.ppermute(value, AXES, pairs)  14.6 us
    ppermute x3, waiting for transfers between devices, body(): got.append(lax.ppermute(piece, 'sec', across(number)))  9.76 us
    ppermute x3, waiting for transfers between devices, body(): lax.ppermute(outs[number], 'sec', across(number))  6.31 us
    ppermute x3, starting transfers between devices, body(): lax.ppermute(outs[number], 'sec', across(number))  2.64 us
    ppermute x3, starting transfers between devices, body(): got.append(lax.ppermute(piece, 'sec', across(number)))  2.48 us
  transfers between devices with their start and end apart: 14, of which 8 were waited for; matrix products, arithmetic and copies ran while one was open for 1% of the time, Pallas kernels for 20%

profile of v4, /device:TPU:105, one launch (start us, length us, event | category | flops | bytes accessed | tf_op | source)
XLA Modules:
  0.0 114.6 jit_solution(9927238129627465956)
XLA Ops:
  0.1 1.4 %constant_dynamic-slice_fusion = (f32[1,8,32,128]{3,2,1,0:T(8,128)S(1)}, f32[1,8,32,128]{3,2,1,0:T(8,128)S(1)}, f32[1,8,32,128]{3,2,1,0:T(8,128)S(1)}, f32[1,8,3...) fusion(f32[1,32,32,128]{3,2,1,0:T(8,128)} %param.6, s32[]{:T(128)S(6)} %select_n.61, ...), kind=kLoop, calls=%fused_computation.3 | loop fusion | bytes 1572876 | tf_op jit(solution)/shard_map/dynamic_slice | solution.py:492
  1.8 1.0 collective-permute-start
  3.5 1.2 %collective-permute-start.2 = (f32[2,8,32,128]{3,2,1,0:T(8,128)}, f32[2,8,32,128]{3,2,1,0:T(8,128)S(1)}, u32[]{:S(2)}, u32[]{:S(2)}) collective-permute-start(f32[2,8,32,128]{3,2,1,0:T(8,128)} %pad_maximum_fusion.2), channel_id=1, source_target_pairs={{0,96},{32,64},{64,32},{96,0},{1,97},{33,65},{65,33},{97,1},{2,98}... | collective-permute-start | bytes 786440 | tf_op jit(solution)/shard_map/ppermute | solution.py:495
  5.5 3.3 %collective-permute-done.1.got_2 = f32[2,8,32,128]{3,2,1,0:T(8,128)S(1)} collective-permute-done((f32[2,8,32,128]{3,2,1,0:T(8,128)S(1)}, f32[2,8,32,128]{3,2,1,0:T(8,128)S(1)}, u32[]{:S(2)}, u32[]{:S(2)}) %collective-permute-start.1) | collective-permute-done | bytes 262176 | tf_op jit(solution)/shard_map/ppermute | solution.py:495
  8.8 6.5 %collective-permute-done.2.got_3 = f32[2,8,32,128]{3,2,1,0:T(8,128)S(1)} collective-permute-done((f32[2,8,32,128]{3,2,1,0:T(8,128)}, f32[2,8,32,128]{3,2,1,0:T(8,128)S(1)}, u32[]{:S(2)}, u32[]{:S(2)}) %collective-permute-start.2) | collective-permute-done | bytes 262176 | tf_op jit(solution)/shard_map/ppermute | solution.py:495
  15.3 1.2 %shard_map.55 = (f32[8,264,128]{2,1,0:T(8,128)S(1)}, f32[3,8,32,128]{3,2,1,0:T(8,128)S(1)}) custom-call(s32[10]{0:T(128)S(1)} %stack.51.scal, f32[32,32,128]{2,1,0:T(8,128)S(1)} %bitcast.11, f32[32,32,128]{2,1,0:T(8,128)S(1)} %bitcast.12, f32[32,32,128]{2,1,0:T(8,128)S(1)} %copy-done.2, s32[32,32,128]{2,1,0:T(8,128)S(1)} %copy-done.3, ...), custom_call_target="tpu_custom_call" | custom-call | flops 4000000 | bytes 2000000 | tf_op jit(solution)/shard_map/pallas_call | solution.py:433
  16.4 4.7 %collective-permute-start.5 = (f32[8,264,128]{2,1,0:T(8,128)S(1)}, f32[8,264,128]{2,1,0:T(8,128)S(1)}, u32[]{:S(2)}, u32[]{:S(2)}) collective-permute-start(f32[8,264,128]{2,1,0:T(8,128)S(1)} %get-tuple-element.39.own), channel_id=1, source_target_pairs={{64,32},{32,64},{0,1},{1,0},{33,65},{65,33},{97,98},{98,97},{66,34... | collective-permute-start | bytes 3244040 | tf_op jit(solution)/shard_map/ppermute | solution.py:511
  21.2 14.7 %collective-permute-done.5.near = f32[8,264,128]{2,1,0:T(8,128)S(1)} collective-permute-done((f32[8,264,128]{2,1,0:T(8,128)S(1)}, f32[8,264,128]{2,1,0:T(8,128)S(1)}, u32[]{:S(2)}, u32[]{:S(2)}) %collective-permute-start.5) | collective-permute-done | bytes 1081376 | tf_op jit(solution)/shard_map/ppermute | solution.py:511
  35.9 5.8 %shard_map.56 = (f32[42,112,128]{2,1,0:T(8,128)S(1)}, f32[42,112,128]{2,1,0:T(8,128)S(1)}, f32[40,96,128]{2,1,0:T(8,128)S(1)}, f32[40,96,128]{2,1,0:T(8,128)S(1)...) custom-call(s32[10]{0:T(128)S(1)} %stack.51.scal, ...), custom_call_target="tpu_custom_call" | custom-call | flops 11200000 | bytes 5600000 | tf_op jit(solution)/shard_map/pallas_call | solution.py:433
  41.7 1.9 %collective-permute-start.4 = (f32[8,264,128]{2,1,0:T(8,128)S(1)}, f32[8,264,128]{2,1,0:T(8,128)S(1)}, u32[]{:S(2)}, u32[]{:S(2)}) collective-permute-start(f32[8,264,128]{2,1,0:T(8,128)S(1)} %get-tuple-element.41), channel_id=1, source_target_pairs={{96,32},{32,1},{1,65},{65,98},{98,34},{34,3},{3,67},{67,4},{4,68},... | collective-permute-start | bytes 3244040 | tf_op jit(solution)/shard_map/ppermute | solution.py:511
  43.6 7.5 %shard_map.57 = (f32[42,112,128]{2,1,0:T(8,128)S(1)}, f32[42,112,128]{2,1,0:T(8,128)S(1)}, f32[40,96,128]{2,1,0:T(8,128)S(1)}, f32[40,96,128]{2,1,0:T(8,128)S(1)...) custom-call(s32[10]{0:T(128)S(1)} %stack.51.scal, ...), custom_call_target="tpu_custom_call", output_to_operand_aliasing={{0}: (4, {}), {1}: (5, {}), {2}: (6, {}), {3}: (7, {}), {4}... | custom-call | flops 25600000 | bytes 12800000 | tf_op jit(solution)/shard_map/pallas_call | solution.py:433
  51.1 9.5 %collective-permute-done.4.far = f32[8,264,128]{2,1,0:T(8,128)S(1)} collective-permute-done((f32[8,264,128]{2,1,0:T(8,128)S(1)}, f32[8,264,128]{2,1,0:T(8,128)S(1)}, u32[]{:S(2)}, u32[]{:S(2)}) %collective-permute-start.4) | collective-permute-done | bytes 1081376 | tf_op jit(solution)/shard_map/ppermute | solution.py:511
  60.6 8.2 %shard_map.58 = (f32[9,96,128]{2,1,0:T(8,128)S(1)}, f32[42,112,128]{2,1,0:T(8,128)S(1)}, f32[42,112,128]{2,1,0:T(8,128)S(1)}, f32[40,96,128]{2,1,0:T(8,128)S(1)}...) custom-call(s32[10]{0:T(128)S(1)} %stack.51.scal, ...), custom_call_target="tpu_custom_call", output_to_operand_aliasing={{1}: (3, {}), {2}: (4, {}), {3}: (5, {}), {4}: (6, {}), {5}... | custom-call | flops 36800000 | bytes 18400000 | tf_op jit(solution)/shard_map/pallas_call | solution.py:433
  68.8 5.8 %collective-permute-start.9 = (f32[9,96,128]{2,1,0:T(8,128)S(1)}, f32[9,96,128]{2,1,0:T(8,128)S(1)}, u32[]{:S(2)}, u32[]{:S(2)}) collective-permute-start(f32[9,96,128]{2,1,0:T(8,128)S(1)} %get-tuple-element.58.own), channel_id=1, source_target_pairs={{64,32},{32,64},{0,1},{1,0},{33,65},{65,33},{97,98},{98,97},{66,34... | collective-permute-start | bytes 1327112 | tf_op jit(solution)/shard_map/ppermute | solution.py:511
  74.7 6.7 %collective-permute-done.9.near = f32[9,96,128]{2,1,0:T(8,128)S(1)} collective-permute-done((f32[9,96,128]{2,1,0:T(8,128)S(1)}, f32[9,96,128]{2,1,0:T(8,128)S(1)}, u32[]{:S(2)}, u32[]{:S(2)}) %collective-permute-start.9) | collective-permute-done | bytes 442400 | tf_op jit(solution)/shard_map/ppermute | solution.py:511
  81.4 3.9 %shard_map.59 = (f32[42,112,128]{2,1,0:T(8,128)S(1)}, f32[42,112,128]{2,1,0:T(8,128)S(1)}, f32[10,48,128]{2,1,0:T(8,128)S(1)}, f32[8,32,128]{2,1,0:T(8,128)S(1)}, f32[8,96,128]{2,1,0:T(8,128)S(1)}) custom-call(s32[10]{0:T(128)S(1)} %stack.51.scal, f32[9,96,128]{2,1,0:T(8,128)S(1)} %get-tuple-element.58.own, f32[9,96,128]{2,1,0:T(8,128)S(1)} %collective-permute-done.7.on, ...), custom_call_target="tpu_custom_call" | custom-call | flops 11200000 | bytes 5600000 | tf_op jit(solution)/shard_map/pallas_call | solution.py:433
  85.3 1.9 %collective-permute-start.8 = (f32[8,96,128]{2,1,0:T(8,128)S(1)}, f32[8,96,128]{2,1,0:T(8,128)S(1)}, u32[]{:S(2)}, u32[]{:S(2)}) collective-permute-start(f32[8,96,128]{2,1,0:T(8,128)S(1)} %get-tuple-element.61), channel_id=1, source_target_pairs={{96,32},{32,1},{1,65},{65,98},{98,34},{34,3},{3,67},{67,4},{4,68},... | collective-permute-start | bytes 1179656 | tf_op jit(solution)/shard_map/ppermute | solution.py:511
  87.2 6.1 %shard_map.60 = (f32[42,112,128]{2,1,0:T(8,128)S(1)}, f32[42,112,128]{2,1,0:T(8,128)S(1)}, f32[10,48,128]{2,1,0:T(8,128)S(1)}, f32[8,32,128]{2,1,0:T(8,128)S(1)}) custom-call(s32[10]{0:T(128)S(1)} %stack.51.scal, f32[9,96,128]{2,1,0:T(8,128)S(1)} %collective-permute-done.9.near, ...), custom_call_target="tpu_custom_call", output_to_operand_aliasing={{0}: (5, {}), {1}: (6, {}), {2}: (7, {}), {3}: (8, {})} | custom-call | flops 25600000 | bytes 12800000 | tf_op jit(solution)/shard_map/pallas_call | solution.py:433
  93.3 3.5 %collective-permute-done.8.far = f32[8,96,128]{2,1,0:T(8,128)S(1)} collective-permute-done((f32[8,96,128]{2,1,0:T(8,128)S(1)}, f32[8,96,128]{2,1,0:T(8,128)S(1)}, u32[]{:S(2)}, u32[]{:S(2)}) %collective-permute-start.8) | collective-permute-done | bytes 393248 | tf_op jit(solution)/shard_map/ppermute | solution.py:511
  96.8 7.5 %shard_map.61 = (f32[8,32,128]{2,1,0:T(8,128)S(1)}, f32[8,32,128]{2,1,0:T(8,128)S(1)}, f32[8,32,128]{2,1,0:T(8,128)S(1)}, f32[8,32,128]{2,1,0:T(8,128)S(1)}, f32...) custom-call(s32[10]{0:T(128)S(1)} %stack.51.scal, ...), custom_call_target="tpu_custom_call", output_to_operand_aliasing={{4}: (5, {}), {5}: (6, {})} | custom-call | flops 36800000 | bytes 18400000 | tf_op jit(solution)/shard_map/pallas_call | solution.py:433
  105.2 1.7 %collective-permute-start.13 = (f32[8,32,128]{2,1,0:T(8,128)S(1)}, f32[8,32,128]{2,1,0:T(8,128)S(1)}, u32[]{:S(2)}, u32[]{:S(2)}) collective-permute-start(f32[8,32,128]{2,1,0:T(8,128)S(1)} %get-tuple-element.72), channel_id=1, source_target_pairs={{0,96},{32,64},{64,32},{96,0},{1,97},{33,65},{65,33},{97,1},{2,98}... | collective-permute-start | bytes 393224 | tf_op jit(solution)/shard_map/ppermute | solution.py:549
  107.0 3.2 %collective-permute-done.12.got_2 = f32[8,32,128]{2,1,0:T(8,128)S(1)} collective-permute-done((f32[8,32,128]{2,1,0:T(8,128)S(1)}, f32[8,32,128]{2,1,0:T(8,128)S(1)}, u32[]{:S(2)}, u32[]{:S(2)}) %collective-permute-start.12) | collective-permute-done | bytes 131104 | tf_op jit(solution)/shard_map/ppermute | solution.py:549
  110.2 3.1 %collective-permute-done.13.got_3 = f32[8,32,128]{2,1,0:T(8,128)S(1)} collective-permute-done((f32[8,32,128]{2,1,0:T(8,128)S(1)}, f32[8,32,128]{2,1,0:T(8,128)S(1)}, u32[]{:S(2)}, u32[]{:S(2)}) %collective-permute-start.13) | collective-permute-done | bytes 131104 | tf_op jit(solution)/shard_map/ppermute | solution.py:549
  113.3 1.4 %shard_map.62 = f32[32,32,128]{2,1,0:T(8,128)} custom-call(s32[10]{0:T(128)S(1)} %stack.51.scal, f32[8,32,128]{2,1,0:T(8,128)S(1)} %get-tuple-element.69.own, f32[8,32,128]{2,1,0:T(8,128)S(1)} %collective-permute-done.11.got_1, f32[8,32,128]{2,1,0:T(8,128)S(1)} %collective-permute-done.12.got_2, f32[8,32,128]{2,1,0:T(8,128)S(1)} %collective-permute-done.13.got_3), custom_call_target="tpu_custom_call" | custom-call | flops 1000000 | bytes 500000 | tf_op jit(solution)/shard_map/pallas_call | solution.py:433
  (25 shorter events, 2.2 us)
Async XLA Ops:
  0.0 15.2 %copy-start.1 = (f32[1,32,32,128]{3,2,1,0:T(8,128)S(1)}, f32[1,32,32,128]{3,2,1,0:T(8,128)}, u32[]{:S(2)}) copy-start(f32[1,32,32,128]{3,2,1,0:T(8,128)} %param.6) | copy-start | bytes 1572868
  0.0 15.2 %copy-start = (f32[1,32,32,128]{3,2,1,0:T(8,128)S(1)}, f32[1,32,32,128]{3,2,1,0:T(8,128)}, u32[]{:S(2)}) copy-start(f32[1,32,32,128]{3,2,1,0:T(8,128)} %param.5) | copy-start | bytes 1572868
  0.0 15.2 %copy-start.3 = (s32[32,32,128]{2,1,0:T(8,128)S(1)}, s32[32,32,128]{2,1,0:T(8,128)}, u32[]{:S(2)}) copy-start(s32[32,32,128]{2,1,0:T(8,128)} %exc.1) | copy-start | bytes 1572868
  0.0 15.2 %copy-start.2 = (f32[32,32,128]{2,1,0:T(8,128)S(1)}, f32[32,32,128]{2,1,0:T(8,128)}, u32[]{:S(2)}) copy-start(f32[32,32,128]{2,1,0:T(8,128)} %rec.1) | copy-start | bytes 1572868
  1.5 7.3 %collective-permute-start.1 = (f32[2,8,32,128]{3,2,1,0:T(8,128)S(1)}, f32[2,8,32,128]{3,2,1,0:T(8,128)S(1)}, u32[]{:S(2)}, u32[]{:S(2)}) collective-permute-start(f32[2,8,32,128]{3,2,1,0:T(8,128)S(1)} %pad_maximum_fusion.1), channel_id=1, source_target_pairs={{0,64},{32,96},{64,0},{96,32},{1,65},{33,97},{65,1},{97,33},{2,66}... | collective-permute-start | bytes 786440 | tf_op jit(solution)/shard_map/ppermute | solution.py:495
  1.8 7.0 %collective-permute-start = (f32[2,8,32,128]{3,2,1,0:T(8,128)S(1)}, f32[2,8,32,128]{3,2,1,0:T(8,128)S(1)}, u32[]{:S(2)}, u32[]{:S(2)}) collective-permute-start(f32[2,8,32,128]{3,2,1,0:T(8,128)S(1)} %pad_maximum_fusion), channel_id=1, source_target_pairs={{0,32},{32,0},{64,96},{96,64},{1,33},{33,1},{65,97},{97,65},{2,34}... | collective-permute-start | bytes 786440 | tf_op jit(solution)/shard_map/ppermute | solution.py:495
  3.5 11.7 %collective-permute-start.2 = (f32[2,8,32,128]{3,2,1,0:T(8,128)}, f32[2,8,32,128]{3,2,1,0:T(8,128)S(1)}, u32[]{:S(2)}, u32[]{:S(2)}) collective-permute-start(f32[2,8,32,128]{3,2,1,0:T(8,128)} %pad_maximum_fusion.2), channel_id=1, source_target_pairs={{0,96},{32,64},{64,32},{96,0},{1,97},{33,65},{65,33},{97,1},{2,98}... | collective-permute-start | bytes 786440 | tf_op jit(solution)/shard_map/ppermute | solution.py:495
  16.4 19.5 %collective-permute-start.5 = (f32[8,264,128]{2,1,0:T(8,128)S(1)}, f32[8,264,128]{2,1,0:T(8,128)S(1)}, u32[]{:S(2)}, u32[]{:S(2)}) collective-permute-start(f32[8,264,128]{2,1,0:T(8,128)S(1)} %get-tuple-element.39.own), channel_id=1, source_target_pairs={{64,32},{32,64},{0,1},{1,0},{33,65},{65,33},{97,98},{98,97},{66,34... | collective-permute-start | bytes 3244040 | tf_op jit(solution)/shard_map/ppermute | solution.py:511
  21.1 14.8 %collective-permute-start.3 = (f32[8,264,128]{2,1,0:T(8,128)S(1)}, f32[8,264,128]{2,1,0:T(8,128)S(1)}, u32[]{:S(2)}, u32[]{:S(2)}) collective-permute-start(f32[8,264,128]{2,1,0:T(8,128)S(1)} %get-tuple-element.39.own), channel_id=1, source_target_pairs={{96,64},{64,96},{32,0},{0,32},{1,33},{33,1},{65,97},{97,65},{98,66... | collective-permute-start | bytes 3244040 | tf_op jit(solution)/shard_map/ppermute | solution.py:511
  35.9 7.7 %collective-permute-start.6 = (f32[8,264,128]{2,1,0:T(8,128)S(1)}, f32[8,264,128]{2,1,0:T(8,128)S(1)}, u32[]{:S(2)}, u32[]{:S(2)}) collective-permute-start(f32[8,264,128]{2,1,0:T(8,128)S(1)} %collective-permute-done.5.near), channel_id=1, source_target_pairs={{96,64},{64,96},{32,0},{0,32},{1,33},{33,1},{65,97},{97,65},{98,66... | collective-permute-start | bytes 3244040 | tf_op jit(solution)/shard_map/ppermute | solution.py:511
  41.7 18.9 %collective-permute-start.4 = (f32[8,264,128]{2,1,0:T(8,128)S(1)}, f32[8,264,128]{2,1,0:T(8,128)S(1)}, u32[]{:S(2)}, u32[]{:S(2)}) collective-permute-start(f32[8,264,128]{2,1,0:T(8,128)S(1)} %get-tuple-element.41), channel_id=1, source_target_pairs={{96,32},{32,1},{1,65},{65,98},{98,34},{34,3},{3,67},{67,4},{4,68},... | collective-permute-start | bytes 3244040 | tf_op jit(solution)/shard_map/ppermute | solution.py:511
  68.8 12.6 %collective-permute-start.9 = (f32[9,96,128]{2,1,0:T(8,128)S(1)}, f32[9,96,128]{2,1,0:T(8,128)S(1)}, u32[]{:S(2)}, u32[]{:S(2)}) collective-permute-start(f32[9,96,128]{2,1,0:T(8,128)S(1)} %get-tuple-element.58.own), channel_id=1, source_target_pairs={{64,32},{32,64},{0,1},{1,0},{33,65},{65,33},{97,98},{98,97},{66,34... | collective-permute-start | bytes 1327112 | tf_op jit(solution)/shard_map/ppermute | solution.py:511
  74.6 6.8 %collective-permute-start.7 = (f32[9,96,128]{2,1,0:T(8,128)S(1)}, f32[9,96,128]{2,1,0:T(8,128)S(1)}, u32[]{:S(2)}, u32[]{:S(2)}) collective-permute-start(f32[9,96,128]{2,1,0:T(8,128)S(1)} %get-tuple-element.58.own), channel_id=1, source_target_pairs={{96,64},{64,96},{32,0},{0,32},{1,33},{33,1},{65,97},{97,65},{98,66... | collective-permute-start | bytes 1327112 | tf_op jit(solution)/shard_map/ppermute | solution.py:511
  81.4 5.8 %collective-permute-start.10 = (f32[9,96,128]{2,1,0:T(8,128)S(1)}, f32[9,96,128]{2,1,0:T(8,128)S(1)}, u32[]{:S(2)}, u32[]{:S(2)}) collective-permute-start(f32[9,96,128]{2,1,0:T(8,128)S(1)} %collective-permute-done.9.near), channel_id=1, source_target_pairs={{96,64},{64,96},{32,0},{0,32},{1,33},{33,1},{65,97},{97,65},{98,66... | collective-permute-start | bytes 1327112 | tf_op jit(solution)/shard_map/ppermute | solution.py:511
  85.3 11.5 %collective-permute-start.8 = (f32[8,96,128]{2,1,0:T(8,128)S(1)}, f32[8,96,128]{2,1,0:T(8,128)S(1)}, u32[]{:S(2)}, u32[]{:S(2)}) collective-permute-start(f32[8,96,128]{2,1,0:T(8,128)S(1)} %get-tuple-element.61), channel_id=1, source_target_pairs={{96,32},{32,1},{1,65},{65,98},{98,34},{34,3},{3,67},{67,4},{4,68},... | collective-permute-start | bytes 1179656 | tf_op jit(solution)/shard_map/ppermute | solution.py:511
  104.3 2.6 %collective-permute-start.11 = (f32[8,32,128]{2,1,0:T(8,128)S(1)}, f32[8,32,128]{2,1,0:T(8,128)S(1)}, u32[]{:S(2)}, u32[]{:S(2)}) collective-permute-start(f32[8,32,128]{2,1,0:T(8,128)S(1)} %get-tuple-element.70), channel_id=1, source_target_pairs={{0,32},{32,0},{64,96},{96,64},{1,33},{33,1},{65,97},{97,65},{2,34}... | collective-permute-start | bytes 393224 | tf_op jit(solution)/shard_map/ppermute | solution.py:549
  105.2 5.0 %collective-permute-start.12 = (f32[8,32,128]{2,1,0:T(8,128)S(1)}, f32[8,32,128]{2,1,0:T(8,128)S(1)}, u32[]{:S(2)}, u32[]{:S(2)}) collective-permute-start(f32[8,32,128]{2,1,0:T(8,128)S(1)} %get-tuple-element.71), channel_id=1, source_target_pairs={{0,64},{32,96},{64,0},{96,32},{1,65},{33,97},{65,1},{97,33},{2,66}... | collective-permute-start | bytes 393224 | tf_op jit(solution)/shard_map/ppermute | solution.py:549
  105.2 8.0 %collective-permute-start.13 = (f32[8,32,128]{2,1,0:T(8,128)S(1)}, f32[8,32,128]{2,1,0:T(8,128)S(1)}, u32[]{:S(2)}, u32[]{:S(2)}) collective-permute-start(f32[8,32,128]{2,1,0:T(8,128)S(1)} %get-tuple-element.72), channel_id=1, source_target_pairs={{0,96},{32,64},{64,32},{96,0},{1,97},{33,65},{65,33},{97,1},{2,98}... | collective-permute-start | bytes 393224 | tf_op jit(solution)/shard_map/ppermute | solution.py:549

commit v5 on v4

--- a/solution.py
+++ b/solution.py
@@ -26,7 +26,8 @@
 PART = 16
 PARTS = ROWS // PART
 AXES = ("sec", "brick")
-V0_AT, V1_AT, D_AT, ROW_AT, MSG = 96, 128, 160, 256, 264
+V0_AT, D_AT, V1_AT, ROW_AT, MSG = 96, 128, 224, 256, 264
+FAR = V1_AT
 PHI_PAD = 112
 V_PAD = 48
 
@@ -199,7 +200,8 @@
 
 END = OWN + 2 * SLAB
 INNER = [(k, [(OWN + k, 2 * SLAB - 2 * k)]) for k in range(1, SLAB)]
-CLOSE = [(k, [(SLAB + k, SLAB), (END - k, SLAB)]) for k in range(1, SLAB + 1)]
+LEFT = [(k, [(SLAB + k, SLAB)]) for k in range(1, SLAB + 1)]
+RIGHT = [(k, [(END - k, SLAB)]) for k in range(1, SLAB + 1)]
 OUTER = [(k, [(k, SLAB)]) for k in range(1, SLAB + 1)]
 OUTER += [(k, [(k, SLOTS - 2 * k)]) for k in range(SLAB + 1, SWEEPS + 1)]
 
@@ -252,17 +254,18 @@
         if absorb is not None:
             absorb[x] = ref[u, D_AT : D_AT + ROWS] + SHIFT
             put_heart(volt, x, ref[u, V0_AT : V0_AT + HEART])
+        if volt_1 is not None:
             put_heart(volt_1, x, ref[u, V1_AT : V1_AT + HEART])
         return carry
 
     lax.fori_loop(0, SLAB, plane, 0)
 
 
-def embed(low, high, mark, volt, volt_1, source, later):
+def embed(low, high, mark, *fields):
     mark = jnp.broadcast_to(mark, (HEART, 128))
 
     def plane(x, carry):
-        for ref, out in ((volt, source), (volt_1, later)):
+        for ref, out in fields:
             gain = heart_laplace(ref, x)
             for layer in range(3):
                 out[x, layer * HEART : (layer + 1) * HEART] = jnp.where(mark == layer, gain, 0.0)
@@ -307,7 +310,7 @@
 
 def first_inner(scal, own, on, aux, even, odd, absorb, source, later, volt, volt_1, held, copy):
     def send(u, carry):
-        copy[u] = own[u]
+        copy[u] = own[u, 0:FAR]
         return carry
 
     lax.fori_loop(0, SLAB, send, 0)
@@ -315,42 +318,48 @@
     take(own, OWN, 1, even, absorb, volt, volt_1)
     take(on, END - 1, -1, even, absorb, volt, volt_1)
     row = jnp.full((1, 128), scal[3].astype(jnp.float32))
-    embed(OWN + 1, END - 1, row, volt, volt_1, source, later)
+    embed(OWN + 1, END - 1, row, (volt, source), (volt_1, later))
     couple(1, SLAB, scal[3], even, volt_1, aux, held)
     sweep(scal, INNER, even, odd, absorb, source)
 
 
-def first_close(scal, near, on2, aux, *refs):
+def first_left(scal, near, aux, *refs):
     even, odd, absorb, source, later, volt, volt_1, held = refs[8:]
     take(near, OWN - 1, -1, even, absorb, volt, volt_1)
-    take(on2, END, 1, even, absorb, volt, volt_1)
 
     @pl.when(scal[4] == OWN)
     def _():
         for ref in (volt, volt_1):
             ref[OWN - 1] = ref[OWN]
 
+    row = jnp.full((1, 128), scal[3].astype(jnp.float32))
+    fields = ((volt, source), (volt_1, later))
+    embed(SLAB + 1, OWN, near[0, ROW_AT : ROW_AT + 1], *fields)
+    embed(OWN, OWN + 1, row, *fields)
+    couple(0, 1, scal[3], even, volt_1, aux, held)
+    sweep(scal, LEFT, even, odd, absorb, source)
+
+
+def first_right(scal, on2, *refs):
+    even, odd, absorb, source, later, volt, volt_1 = refs[7:]
+    take(on2, END, 1, even, absorb, volt, volt_1)
+
     @pl.when(scal[5] == END)
     def _():
         for ref in (volt, volt_1):
             ref[END] = ref[END - 1]
 
     row = jnp.full((1, 128), scal[3].astype(jnp.float32))
-    for low, high, mark in (
-        (SLAB + 1, OWN, near[0, ROW_AT : ROW_AT + 1]),
-        (OWN, OWN + 1, row),
-        (END - 1, END, row),
-        (END, SLOTS - 1, on2[0, ROW_AT : ROW_AT + 1]),
-    ):
-        embed(low, high, mark, volt, volt_1, source, later)
-    couple(0, 1, scal[3], even, volt_1, aux, held)
-    sweep(scal, CLOSE, even, odd, absorb, source)
-
-
-def first_outer(scal, far, held, *refs):
-    msg, even, odd, absorb, source, later, volt, volt_1 = refs[7:]
-    take(far, 0, 1, even, absorb, volt, volt_1)
-    embed(1, SLAB + 1, far[0, ROW_AT : ROW_AT + 1], volt, volt_1, source, later)
+    fields = ((volt, source), (volt_1, later))
+    embed(END - 1, END, row, *fields)
+    embed(END, SLOTS - 1, on2[0, ROW_AT : ROW_AT + 1], *fields)
+    sweep(scal, RIGHT, even, odd, absorb, source)
+
+
+def first_outer(scal, far, near, held, *refs):
+    msg, even, odd, absorb, source, volt = refs[5:]
+    take(far, 0, 1, even, absorb, volt)
+    embed(1, SLAB + 1, near[0, ROW_AT : ROW_AT + 1], (volt, source))
     sweep(scal, OUTER, even, odd, absorb, source)
     for u in range(SLAB):
         msg[u] = even[OFF + OWN + u, PAD : PAD + ROWS]
@@ -359,9 +368,10 @@
     msg[SLAB, 2 * HEART : ROWS] = jnp.zeros((HEART, 128), jnp.float32)
 
 
-def second_inner(scal, own, on, held, absorb, source, even, odd, volt, out, copy):
+def second_inner(scal, own, on, held, first, absorb, source, even, odd, volt, out, copy):
     def keep(u, carry):
-        copy[u] = own[u]
+        copy[u, 0:ROWS] = own[u]
+        copy[u, ROWS : ROWS + HEART] = first[u, V1_AT : V1_AT + HEART]
         put_heart(volt, u + 1, held[u])
         return carry
 
@@ -374,10 +384,9 @@
     sweep(scal, INNER, even, odd, absorb, source)
 
 
-def second_close(scal, near, on2, absorb, source, *refs):
+def second_left(scal, near, absorb, source, *refs):
     even, odd, volt, out = refs[4:]
     take(near, OWN - 1, -1, even)
-    take(on2, END, 1, even)
     put_heart(volt, 0, near[SLAB, 0:HEART])
 
     @pl.when(scal[4] == OWN)
@@ -385,16 +394,29 @@
         volt[0] = volt[1]
 
     settle(0, 1, scal[3], even, volt, out)
-    sweep(scal, CLOSE, even, odd, absorb, source)
-
-
-def second_outer(scal, far, absorb, source, voltage, *refs):
-    outs, (even, odd), (joined,) = refs[2:6], refs[6:8], refs[8:]
+    sweep(scal, LEFT, even, odd, absorb, source)
+
+
+def second_right(scal, on2, absorb, source, *refs):
+    even, odd = refs[2:]
+    take(on2, END, 1, even)
+    sweep(scal, RIGHT, even, odd, absorb, source)
+
+
+def second_outer(scal, far, near, absorb, voltage, *refs):
+    outs, (even, odd, source, volt_1), (joined,) = refs[4:8], refs[8:12], refs[12:]
     take(far, 0, 1, even)
+
+    def plane(u, carry):
+        put_heart(volt_1, u, far[u, ROWS : ROWS + HEART])
+        return carry
+
+    lax.fori_loop(0, SLAB, plane, 0)
+    embed(1, SLAB + 1, near[0, ROW_AT : ROW_AT + 1], (volt_1, source))
     sweep(scal, OUTER, even, odd, absorb, source)
     sec, flip = scal[0], scal[2]
 
-    def plane(u, carry):
+    def give(u, carry):
         joined[u, 0:ROWS] = even[OFF + OWN + u, PAD : PAD + ROWS]
         joined[u, ROWS : ROWS + HEART] = voltage[u]
         x = jnp.where(flip == 1, SLAB - 1 - u, u)
@@ -403,7 +425,7 @@
             outs[number][x] = joined[u, pl.ds(at, HEART)]
         return carry
 
-    lax.fori_loop(0, SLAB, plane, 0)
+    lax.fori_loop(0, SLAB, give, 0)
 
 
 def spread_kernel(scal, own, got_1, got_2, got_3, out):
@@ -510,43 +532,53 @@
     def move(value, pairs):
         return lax.ppermute(value, AXES, pairs)
 
-    near = move(msg, facing)
+    near_1 = move(msg, facing)
     on = move(msg, partner)
     *state, copy = call(
         first_inner,
         (scal, msg, on, aux),
-        [phi, phi, wide, wide, wide, volt, volt, heart, msg.shape],
+        [phi, phi, wide, wide, wide, volt, volt, heart, (SLAB, FAR, 128)],
         56,
     )
     far = move(copy, beyond)
-    on2 = move(near, partner)
-    *state, held = call(first_close, (scal, near, on2, aux), [], 128, state=state)
-    msg, _, _, absorb, _, later, _, _ = call(
-        first_outer, (scal, far, held), [(SLAB + 1, ROWS, 128)], 184, state=state
-    )
-
-    near = move(msg, facing)
-    on = move(msg, partner)
-    *state, copy = call(
+    on2 = move(near_1, partner)
+    *state, held = call(first_left, (scal, near_1, aux), [], 64, state=state)
+    even, odd, absorb, source, later, volt_0, volt_1 = call(
+        first_right, (scal, on2), [], 64, state=state
+    )
+    message, _, _, absorb, _, _ = call(
+        first_outer,
+        (scal, far, near_1, held),
+        [(SLAB + 1, ROWS, 128)],
+        184,
+        state=[even, odd, absorb, source, volt_0],
+    )
+
+    near = move(message, facing)
+    on = move(message, partner)
+    even, odd, volt_2, voltage, copy = call(
         second_inner,
-        (scal, msg, on, held, absorb, later),
-        [phi, phi, (SLAB + 2, V_PAD, 128), heart, (SLAB, ROWS, 128)],
+        (scal, message, on, held, msg, absorb, later),
+        [phi, phi, (SLAB + 2, V_PAD, 128), heart, (SLAB, ROWS + HEART, 128)],
         56,
     )
     far = move(copy, beyond)
     on2 = move(near, partner)
     even, odd, _, voltage = call(
-        second_close, (scal, near, on2, absorb, later), [], 128, state=state
-    )
+        second_left, (scal, near, absorb, later), [], 64, state=[even, odd, volt_2, voltage]
+    )
+    even, odd = call(second_right, (scal, on2, absorb, later), [], 64, state=[even, odd])
     outs = call(
         second_outer,
-        (scal, far, absorb, later, voltage),
+        (scal, far, near_1, absorb, voltage),
         [heart] * 4,
         184,
         scratch=[(SLAB, 128, 128)],
-        state=[even, odd],
+        state=[even, odd, later, volt_1],
     )[:4]
-    back = [outs[0]] + [lax.ppermute(outs[number], "sec", across(number)) for number in (1, 2, 3)]
+    back = [outs[0]]
+    for number in (1, 2, 3):
+        back.append(lax.ppermute(outs[number], "sec", across(number)))
     (result,) = call(spread_kernel, (scal, *back), [(sections * SLAB, HEART, 128)], 5)
     return result[None]
 

time: 116 us -> 109 us (0.940); the launches traced: 115 us -> 109 us
  waiting for transfers between devices: 50.4 us -> 42.9 us
  starting transfers between devices: 19.7 us -> 21.2 us
    ppermute x8, waiting for transfers between devices: 34.3 us -> 26.4 us  [move(): return lax.ppermute(value, AXES, pairs)]
    ppermute x8, starting transfers between devices: 14.6 us -> 16.5 us  [move(): return lax.ppermute(value, AXES, pairs)]
    pallas_call x8 -> x10, Pallas kernels: 41.4 us -> 41.6 us  [call(): pl.pallas_call(kernel, out_shape=arrays, in_specs=[SMEM] + [VMEM] * (len(...]
  transfers between devices with their start and end apart: 14 -> 14, of which waited for: 8 -> 8; matrix products, arithmetic and copies ran while one was open for 1% -> 1% of each run, Pallas kernels for 20% -> 21%
where the time goes in v5:
time: 109 us
  waiting for transfers between devices  42.9 us (39%)
  Pallas kernels  41.6 us (38%)
  starting transfers between devices  21.2 us (19%)
  local copies, waits for them, and re-layouts  1.49 us (1%)
    pallas_call x10, Pallas kernels, call(): pl.pallas_call(kernel, out_shape=arrays, in_specs=[SMEM] + [VMEM] * (len(...  41.6 us
    ppermute x8, waiting for transfers between devices, move(): return lax.ppermute(value, AXES, pairs)  26.4 us
    ppermute x8, starting transfers between devices, move(): return lax.ppermute(value, AXES, pairs)  16.5 us
    ppermute x3, waiting for transfers between devices, body(): got.append(lax.ppermute(piece, 'sec', across(number)))  10.5 us
    ppermute x3, waiting for transfers between devices, body(): back.append(lax.ppermute(outs[number], 'sec', across(number)))  5.98 us
    ppermute x3, starting transfers between devices, body(): got.append(lax.ppermute(piece, 'sec', across(number)))  2.48 us
    ppermute x3, starting transfers between devices, body(): back.append(lax.ppermute(outs[number], 'sec', across(number)))  2.21 us
  transfers between devices with their start and end apart: 14, of which 8 were waited for; matrix products, arithmetic and copies ran while one was open for 1% of the time, Pallas kernels for 21%

profile of v5, /device:TPU:105, one launch (start us, length us, event | category | flops | bytes accessed | tf_op | source)
XLA Modules:
  0.0 108.9 jit_solution(14212134239430004953)
XLA Ops:
  0.1 1.4 %constant_dynamic-slice_fusion = (f32[1,8,32,128]{3,2,1,0:T(8,128)S(1)}, f32[1,8,32,128]{3,2,1,0:T(8,128)S(1)}, f32[1,8,32,128]{3,2,1,0:T(8,128)S(1)}, f32[1,8,3...) fusion(f32[1,32,32,128]{3,2,1,0:T(8,128)} %param.6, s32[]{:T(128)S(6)} %select_n.61, ...), kind=kLoop, calls=%fused_computation.3 | loop fusion | bytes 1572876 | tf_op jit(solution)/shard_map/dynamic_slice | solution.py:514
  3.2 1.5 %collective-permute-start.2 = (f32[2,8,32,128]{3,2,1,0:T(8,128)}, f32[2,8,32,128]{3,2,1,0:T(8,128)S(1)}, u32[]{:S(2)}, u32[]{:S(2)}) collective-permute-start(f32[2,8,32,128]{3,2,1,0:T(8,128)} %pad_maximum_fusion.2), channel_id=1, source_target_pairs={{0,96},{32,64},{64,32},{96,0},{1,97},{33,65},{65,33},{97,1},{2,98}... | collective-permute-start | bytes 786440 | tf_op jit(solution)/shard_map/ppermute | solution.py:517
  5.5 4.7 %collective-permute-done.1.got_2 = f32[2,8,32,128]{3,2,1,0:T(8,128)S(1)} collective-permute-done((f32[2,8,32,128]{3,2,1,0:T(8,128)S(1)}, f32[2,8,32,128]{3,2,1,0:T(8,128)S(1)}, u32[]{:S(2)}, u32[]{:S(2)}) %collective-permute-start.1) | collective-permute-done | bytes 262176 | tf_op jit(solution)/shard_map/ppermute | solution.py:517
  10.2 5.8 %collective-permute-done.2.got_3 = f32[2,8,32,128]{3,2,1,0:T(8,128)S(1)} collective-permute-done((f32[2,8,32,128]{3,2,1,0:T(8,128)}, f32[2,8,32,128]{3,2,1,0:T(8,128)S(1)}, u32[]{:S(2)}, u32[]{:S(2)}) %collective-permute-start.2) | collective-permute-done | bytes 262176 | tf_op jit(solution)/shard_map/ppermute | solution.py:517
  16.0 1.2 %shard_map.55 = (f32[8,264,128]{2,1,0:T(8,128)S(1)}, f32[3,8,32,128]{3,2,1,0:T(8,128)S(1)}) custom-call(s32[10]{0:T(128)S(1)} %stack.51.scal, f32[32,32,128]{2,1,0:T(8,128)S(1)} %bitcast.11, f32[32,32,128]{2,1,0:T(8,128)S(1)} %bitcast.12, f32[32,32,128]{2,1,0:T(8,128)S(1)} %copy-done.2, s32[32,32,128]{2,1,0:T(8,128)S(1)} %copy-done.3, ...), custom_call_target="tpu_custom_call" | custom-call | flops 4000000 | bytes 2000000 | tf_op jit(solution)/shard_map/pallas_call | solution.py:455
  17.2 5.3 %collective-permute-start.5 = (f32[8,264,128]{2,1,0:T(8,128)S(1)}, f32[8,264,128]{2,1,0:T(8,128)S(1)}, u32[]{:S(2)}, u32[]{:S(2)}) collective-permute-start(f32[8,264,128]{2,1,0:T(8,128)S(1)} %get-tuple-element.47.own.first), channel_id=1, source_target_pairs={{64,32},{32,64},{0,1},{1,0},{33,65},{65,33},{97,98},{98,97},{66,34... | collective-permute-start | bytes 3244040 | tf_op jit(solution)/shard_map/ppermute | solution.py:533
  22.6 14.0 %collective-permute-done.5.near = f32[8,264,128]{2,1,0:T(8,128)S(1)} collective-permute-done((f32[8,264,128]{2,1,0:T(8,128)S(1)}, f32[8,264,128]{2,1,0:T(8,128)S(1)}, u32[]{:S(2)}, u32[]{:S(2)}) %collective-permute-start.5) | collective-permute-done | bytes 1081376 | tf_op jit(solution)/shard_map/ppermute | solution.py:533
  36.7 5.8 %shard_map.56 = (f32[42,112,128]{2,1,0:T(8,128)S(1)}, f32[42,112,128]{2,1,0:T(8,128)S(1)}, f32[40,96,128]{2,1,0:T(8,128)S(1)}, f32[40,96,128]{2,1,0:T(8,128)S(1)...) custom-call(s32[10]{0:T(128)S(1)} %stack.51.scal, ...), custom_call_target="tpu_custom_call" | custom-call | flops 11200000 | bytes 5600000 | tf_op jit(solution)/shard_map/pallas_call | solution.py:455
  42.4 1.9 %collective-permute-start.4 = (f32[8,224,128]{2,1,0:T(8,128)S(1)}, f32[8,224,128]{2,1,0:T(8,128)S(1)}, u32[]{:S(2)}, u32[]{:S(2)}) collective-permute-start(f32[8,224,128]{2,1,0:T(8,128)S(1)} %get-tuple-element.49), channel_id=1, source_target_pairs={{96,32},{32,1},{1,65},{65,98},{98,34},{34,3},{3,67},{67,4},{4,68},... | collective-permute-start | bytes 2752520 | tf_op jit(solution)/shard_map/ppermute | solution.py:533
  44.4 3.8 %shard_map.57 = (f32[42,112,128]{2,1,0:T(8,128)S(1)}, f32[42,112,128]{2,1,0:T(8,128)S(1)}, f32[40,96,128]{2,1,0:T(8,128)S(1)}, f32[40,96,128]{2,1,0:T(8,128)S(1)...) custom-call(s32[10]{0:T(128)S(1)} %stack.51.scal, ...), custom_call_target="tpu_custom_call", output_to_operand_aliasing={{0}: (3, {}), {1}: (4, {}), {2}: (5, {}), {3}: (6, {}), {4}... | custom-call | flops 12800000 | bytes 6400000 | tf_op jit(solution)/shard_map/pallas_call | solution.py:455
  48.2 3.6 %shard_map.58 = (f32[42,112,128]{2,1,0:T(8,128)S(1)}, f32[42,112,128]{2,1,0:T(8,128)S(1)}, f32[40,96,128]{2,1,0:T(8,128)S(1)}, f32[40,96,128]{2,1,0:T(8,128)S(1)...) custom-call(s32[10]{0:T(128)S(1)} %stack.51.scal, ...), custom_call_target="tpu_custom_call", output_to_operand_aliasing={{0}: (2, {}), {1}: (3, {}), {2}: (4, {}), {3}: (5, {}), {4}... | custom-call | flops 12800000 | bytes 6400000 | tf_op jit(solution)/shard_map/pallas_call | solution.py:455
  51.8 7.8 %collective-permute-done.4.far = f32[8,224,128]{2,1,0:T(8,128)S(1)} collective-permute-done((f32[8,224,128]{2,1,0:T(8,128)S(1)}, f32[8,224,128]{2,1,0:T(8,128)S(1)}, u32[]{:S(2)}, u32[]{:S(2)}) %collective-permute-start.4) | collective-permute-done | bytes 917536 | tf_op jit(solution)/shard_map/ppermute | solution.py:533
  59.6 8.1 %shard_map.59 = (f32[9,96,128]{2,1,0:T(8,128)S(1)}, f32[42,112,128]{2,1,0:T(8,128)S(1)}, f32[42,112,128]{2,1,0:T(8,128)S(1)}, f32[40,96,128]{2,1,0:T(8,128)S(1)}...) custom-call(s32[10]{0:T(128)S(1)} %stack.51.scal, ...), custom_call_target="tpu_custom_call", output_to_operand_aliasing={{1}: (4, {}), {2}: (5, {}), {3}: (6, {}), {4}: (7, {}), {5}... | custom-call | flops 36800000 | bytes 18400000 | tf_op jit(solution)/shard_map/pallas_call | solution.py:455
  67.8 6.5 %collective-permute-start.9 = (f32[9,96,128]{2,1,0:T(8,128)S(1)}, f32[9,96,128]{2,1,0:T(8,128)S(1)}, u32[]{:S(2)}, u32[]{:S(2)}) collective-permute-start(f32[9,96,128]{2,1,0:T(8,128)S(1)} %get-tuple-element.71.own), channel_id=1, source_target_pairs={{64,32},{32,64},{0,1},{1,0},{33,65},{65,33},{97,98},{98,97},{66,34... | collective-permute-start | bytes 1327112 | tf_op jit(solution)/shard_map/ppermute | solution.py:533
  74.3 3.9 %shard_map.60 = (f32[42,112,128]{2,1,0:T(8,128)S(1)}, f32[42,112,128]{2,1,0:T(8,128)S(1)}, f32[10,48,128]{2,1,0:T(8,128)S(1)}, f32[8,32,128]{2,1,0:T(8,128)S(1)}, f32[8,128,128]{2,1,0:T(8,128)S(1)}) custom-call(s32[10]{0:T(128)S(1)} %stack.51.scal, f32[9,96,128]{2,1,0:T(8,128)S(1)} %get-tuple-element.71.own, f32[9,96,128]{2,1,0:T(8,128)S(1)} %collective-permute-done.7.on, ...), custom_call_target="tpu_custom_call" | custom-call | flops 11200000 | bytes 5600000 | tf_op jit(solution)/shard_map/pallas_call | solution.py:455
  78.2 2.1 %collective-permute-start.8 = (f32[8,128,128]{2,1,0:T(8,128)S(1)}, f32[8,128,128]{2,1,0:T(8,128)S(1)}, u32[]{:S(2)}, u32[]{:S(2)}) collective-permute-start(f32[8,128,128]{2,1,0:T(8,128)S(1)} %get-tuple-element.74), channel_id=1, source_target_pairs={{96,32},{32,1},{1,65},{65,98},{98,34},{34,3},{3,67},{67,4},{4,68},... | collective-permute-start | bytes 1572872 | tf_op jit(solution)/shard_map/ppermute | solution.py:533
  80.9 2.9 %shard_map.61 = (f32[42,112,128]{2,1,0:T(8,128)S(1)}, f32[42,112,128]{2,1,0:T(8,128)S(1)}, f32[10,48,128]{2,1,0:T(8,128)S(1)}, f32[8,32,128]{2,1,0:T(8,128)S(1)}) custom-call(s32[10]{0:T(128)S(1)} %stack.51.scal, f32[9,96,128]{2,1,0:T(8,128)S(1)} %collective-permute-done.9.near, ...), custom_call_target="tpu_custom_call", output_to_operand_aliasing={{0}: (4, {}), {1}: (5, {}), {2}: (6, {}), {3}: (7, {})} | custom-call | flops 12800000 | bytes 6400000 | tf_op jit(solution)/shard_map/pallas_call | solution.py:455
  83.9 2.8 %shard_map.62 = (f32[42,112,128]{2,1,0:T(8,128)S(1)}, f32[42,112,128]{2,1,0:T(8,128)S(1)}) custom-call(s32[10]{0:T(128)S(1)} %stack.51.scal, f32[9,96,128]{2,1,0:T(8,128)S(1)} %collective-permute-done.10.on2, f32[40,96,128]{2,1,0:T(8,128)S(1)} %get-tuple-element.72.absorb, ...), custom_call_target="tpu_custom_call", output_to_operand_aliasing={{0}: (4, {}), {1}: (5, {})} | custom-call | flops 12800000 | bytes 6400000 | tf_op jit(solution)/shard_map/pallas_call | solution.py:455
  86.7 4.4 %collective-permute-done.8.far = f32[8,128,128]{2,1,0:T(8,128)S(1)} collective-permute-done((f32[8,128,128]{2,1,0:T(8,128)S(1)}, f32[8,128,128]{2,1,0:T(8,128)S(1)}, u32[]{:S(2)}, u32[]{:S(2)}) %collective-permute-start.8) | collective-permute-done | bytes 524320 | tf_op jit(solution)/shard_map/ppermute | solution.py:533
  91.1 8.2 %shard_map.63 = (f32[8,32,128]{2,1,0:T(8,128)S(1)}, f32[8,32,128]{2,1,0:T(8,128)S(1)}, f32[8,32,128]{2,1,0:T(8,128)S(1)}, f32[8,32,128]{2,1,0:T(8,128)S(1)}, f32...) custom-call(s32[10]{0:T(128)S(1)} %stack.51.scal, ...), custom_call_target="tpu_custom_call", output_to_operand_aliasing={{4}: (5, {}), {5}: (6, {}), {6}: (7, {}), {7}: (8, {})} | custom-call | flops 36800000 | bytes 18400000 | tf_op jit(solution)/shard_map/pallas_call | solution.py:455
  99.5 2.0 %collective-permute-start.13 = (f32[8,32,128]{2,1,0:T(8,128)S(1)}, f32[8,32,128]{2,1,0:T(8,128)S(1)}, u32[]{:S(2)}, u32[]{:S(2)}) collective-permute-start(f32[8,32,128]{2,1,0:T(8,128)S(1)} %get-tuple-element.88), channel_id=1, source_target_pairs={{0,96},{32,64},{64,32},{96,0},{1,97},{33,65},{65,33},{97,1},{2,98}... | collective-permute-start | bytes 393224 | tf_op jit(solution)/shard_map/ppermute | solution.py:581
  101.6 2.6 %collective-permute-done.12.got_2 = f32[8,32,128]{2,1,0:T(8,128)S(1)} collective-permute-done((f32[8,32,128]{2,1,0:T(8,128)S(1)}, f32[8,32,128]{2,1,0:T(8,128)S(1)}, u32[]{:S(2)}, u32[]{:S(2)}) %collective-permute-start.12) | collective-permute-done | bytes 131104 | tf_op jit(solution)/shard_map/ppermute | solution.py:581
  104.2 3.4 %collective-permute-done.13.got_3 = f32[8,32,128]{2,1,0:T(8,128)S(1)} collective-permute-done((f32[8,32,128]{2,1,0:T(8,128)S(1)}, f32[8,32,128]{2,1,0:T(8,128)S(1)}, u32[]{:S(2)}, u32[]{:S(2)}) %collective-permute-start.13) | collective-permute-done | bytes 131104 | tf_op jit(solution)/shard_map/ppermute | solution.py:581
  107.5 1.4 %shard_map.64 = f32[32,32,128]{2,1,0:T(8,128)} custom-call(s32[10]{0:T(128)S(1)} %stack.51.scal, f32[8,32,128]{2,1,0:T(8,128)S(1)} %get-tuple-element.85.own, f32[8,32,128]{2,1,0:T(8,128)S(1)} %collective-permute-done.11.got_1, f32[8,32,128]{2,1,0:T(8,128)S(1)} %collective-permute-done.12.got_2, f32[8,32,128]{2,1,0:T(8,128)S(1)} %collective-permute-done.13.got_3), custom_call_target="tpu_custom_call" | custom-call | flops 1000000 | bytes 500000 | tf_op jit(solution)/shard_map/pallas_call | solution.py:455
  (27 shorter events, 2.9 us)
Async XLA Ops:
  0.0 16.0 %copy-start = (f32[1,32,32,128]{3,2,1,0:T(8,128)S(1)}, f32[1,32,32,128]{3,2,1,0:T(8,128)}, u32[]{:S(2)}) copy-start(f32[1,32,32,128]{3,2,1,0:T(8,128)} %param.5) | copy-start | bytes 1572868
  0.0 16.0 %copy-start.1 = (f32[1,32,32,128]{3,2,1,0:T(8,128)S(1)}, f32[1,32,32,128]{3,2,1,0:T(8,128)}, u32[]{:S(2)}) copy-start(f32[1,32,32,128]{3,2,1,0:T(8,128)} %param.6) | copy-start | bytes 1572868
  0.0 16.0 %copy-start.2 = (f32[32,32,128]{2,1,0:T(8,128)S(1)}, f32[32,32,128]{2,1,0:T(8,128)}, u32[]{:S(2)}) copy-start(f32[32,32,128]{2,1,0:T(8,128)} %rec.1) | copy-start | bytes 1572868
  0.0 16.0 %copy-start.3 = (s32[32,32,128]{2,1,0:T(8,128)S(1)}, s32[32,32,128]{2,1,0:T(8,128)}, u32[]{:S(2)}) copy-start(s32[32,32,128]{2,1,0:T(8,128)} %exc.1) | copy-start | bytes 1572868
  1.5 4.0 %collective-permute-start = (f32[2,8,32,128]{3,2,1,0:T(8,128)S(1)}, f32[2,8,32,128]{3,2,1,0:T(8,128)S(1)}, u32[]{:S(2)}, u32[]{:S(2)}) collective-permute-start(f32[2,8,32,128]{3,2,1,0:T(8,128)S(1)} %pad_maximum_fusion), channel_id=1, source_target_pairs={{0,32},{32,0},{64,96},{96,64},{1,33},{33,1},{65,97},{97,65},{2,34}... | collective-permute-start | bytes 786440 | tf_op jit(solution)/shard_map/ppermute | solution.py:517
  2.3 7.9 %collective-permute-start.1 = (f32[2,8,32,128]{3,2,1,0:T(8,128)S(1)}, f32[2,8,32,128]{3,2,1,0:T(8,128)S(1)}, u32[]{:S(2)}, u32[]{:S(2)}) collective-permute-start(f32[2,8,32,128]{3,2,1,0:T(8,128)S(1)} %pad_maximum_fusion.1), channel_id=1, source_target_pairs={{0,64},{32,96},{64,0},{96,32},{1,65},{33,97},{65,1},{97,33},{2,66}... | collective-permute-start | bytes 786440 | tf_op jit(solution)/shard_map/ppermute | solution.py:517
  3.2 12.8 %collective-permute-start.2 = (f32[2,8,32,128]{3,2,1,0:T(8,128)}, f32[2,8,32,128]{3,2,1,0:T(8,128)S(1)}, u32[]{:S(2)}, u32[]{:S(2)}) collective-permute-start(f32[2,8,32,128]{3,2,1,0:T(8,128)} %pad_maximum_fusion.2), channel_id=1, source_target_pairs={{0,96},{32,64},{64,32},{96,0},{1,97},{33,65},{65,33},{97,1},{2,98}... | collective-permute-start | bytes 786440 | tf_op jit(solution)/shard_map/ppermute | solution.py:517
  17.2 19.5 %collective-permute-start.5 = (f32[8,264,128]{2,1,0:T(8,128)S(1)}, f32[8,264,128]{2,1,0:T(8,128)S(1)}, u32[]{:S(2)}, u32[]{:S(2)}) collective-permute-start(f32[8,264,128]{2,1,0:T(8,128)S(1)} %get-tuple-element.47.own.first), channel_id=1, source_target_pairs={{64,32},{32,64},{0,1},{1,0},{33,65},{65,33},{97,98},{98,97},{66,34... | collective-permute-start | bytes 3244040 | tf_op jit(solution)/shard_map/ppermute | solution.py:533
  22.5 14.1 %collective-permute-start.3 = (f32[8,264,128]{2,1,0:T(8,128)S(1)}, f32[8,264,128]{2,1,0:T(8,128)S(1)}, u32[]{:S(2)}, u32[]{:S(2)}) collective-permute-start(f32[8,264,128]{2,1,0:T(8,128)S(1)} %get-tuple-element.47.own.first), channel_id=1, source_target_pairs={{96,64},{64,96},{32,0},{0,32},{1,33},{33,1},{65,97},{97,65},{98,66... | collective-permute-start | bytes 3244040 | tf_op jit(solution)/shard_map/ppermute | solution.py:533
  36.7 11.5 %collective-permute-start.6 = (f32[8,264,128]{2,1,0:T(8,128)S(1)}, f32[8,264,128]{2,1,0:T(8,128)S(1)}, u32[]{:S(2)}, u32[]{:S(2)}) collective-permute-start(f32[8,264,128]{2,1,0:T(8,128)S(1)} %collective-permute-done.5.near), channel_id=1, source_target_pairs={{96,64},{64,96},{32,0},{0,32},{1,33},{33,1},{65,97},{97,65},{98,66... | collective-permute-start | bytes 3244040 | tf_op jit(solution)/shard_map/ppermute | solution.py:533
  42.4 17.1 %collective-permute-start.4 = (f32[8,224,128]{2,1,0:T(8,128)S(1)}, f32[8,224,128]{2,1,0:T(8,128)S(1)}, u32[]{:S(2)}, u32[]{:S(2)}) collective-permute-start(f32[8,224,128]{2,1,0:T(8,128)S(1)} %get-tuple-element.49), channel_id=1, source_target_pairs={{96,32},{32,1},{1,65},{65,98},{98,34},{34,3},{3,67},{67,4},{4,68},... | collective-permute-start | bytes 2752520 | tf_op jit(solution)/shard_map/ppermute | solution.py:533
  67.7 6.6 %collective-permute-start.7 = (f32[9,96,128]{2,1,0:T(8,128)S(1)}, f32[9,96,128]{2,1,0:T(8,128)S(1)}, u32[]{:S(2)}, u32[]{:S(2)}) collective-permute-start(f32[9,96,128]{2,1,0:T(8,128)S(1)} %get-tuple-element.71.own), channel_id=1, source_target_pairs={{96,64},{64,96},{32,0},{0,32},{1,33},{33,1},{65,97},{97,65},{98,66... | collective-permute-start | bytes 1327112 | tf_op jit(solution)/shard_map/ppermute | solution.py:533
  67.8 12.6 %collective-permute-start.9 = (f32[9,96,128]{2,1,0:T(8,128)S(1)}, f32[9,96,128]{2,1,0:T(8,128)S(1)}, u32[]{:S(2)}, u32[]{:S(2)}) collective-permute-start(f32[9,96,128]{2,1,0:T(8,128)S(1)} %get-tuple-element.71.own), channel_id=1, source_target_pairs={{64,32},{32,64},{0,1},{1,0},{33,65},{65,33},{97,98},{98,97},{66,34... | collective-permute-start | bytes 1327112 | tf_op jit(solution)/shard_map/ppermute | solution.py:533
  78.2 12.9 %collective-permute-start.8 = (f32[8,128,128]{2,1,0:T(8,128)S(1)}, f32[8,128,128]{2,1,0:T(8,128)S(1)}, u32[]{:S(2)}, u32[]{:S(2)}) collective-permute-start(f32[8,128,128]{2,1,0:T(8,128)S(1)} %get-tuple-element.74), channel_id=1, source_target_pairs={{96,32},{32,1},{1,65},{65,98},{98,34},{34,3},{3,67},{67,4},{4,68},... | collective-permute-start | bytes 1572872 | tf_op jit(solution)/shard_map/ppermute | solution.py:533
  80.4 3.5 %collective-permute-start.10 = (f32[9,96,128]{2,1,0:T(8,128)S(1)}, f32[9,96,128]{2,1,0:T(8,128)S(1)}, u32[]{:S(2)}, u32[]{:S(2)}) collective-permute-start(f32[9,96,128]{2,1,0:T(8,128)S(1)} %collective-permute-done.9.near), channel_id=1, source_target_pairs={{96,64},{64,96},{32,0},{0,32},{1,33},{33,1},{65,97},{97,65},{98,66... | collective-permute-start | bytes 1327112 | tf_op jit(solution)/shard_map/ppermute | solution.py:533
  99.3 2.2 %collective-permute-start.11 = (f32[8,32,128]{2,1,0:T(8,128)S(1)}, f32[8,32,128]{2,1,0:T(8,128)S(1)}, u32[]{:S(2)}, u32[]{:S(2)}) collective-permute-start(f32[8,32,128]{2,1,0:T(8,128)S(1)} %get-tuple-element.86), channel_id=1, source_target_pairs={{0,32},{32,0},{64,96},{96,64},{1,33},{33,1},{65,97},{97,65},{2,34}... | collective-permute-start | bytes 393224 | tf_op jit(solution)/shard_map/ppermute | solution.py:581
  99.4 4.7 %collective-permute-start.12 = (f32[8,32,128]{2,1,0:T(8,128)S(1)}, f32[8,32,128]{2,1,0:T(8,128)S(1)}, u32[]{:S(2)}, u32[]{:S(2)}) collective-permute-start(f32[8,32,128]{2,1,0:T(8,128)S(1)} %get-tuple-element.87), channel_id=1, source_target_pairs={{0,64},{32,96},{64,0},{96,32},{1,65},{33,97},{65,1},{97,33},{2,66}... | collective-permute-start | bytes 393224 | tf_op jit(solution)/shard_map/ppermute | solution.py:581
  99.5 8.0 %collective-permute-start.13 = (f32[8,32,128]{2,1,0:T(8,128)S(1)}, f32[8,32,128]{2,1,0:T(8,128)S(1)}, u32[]{:S(2)}, u32[]{:S(2)}) collective-permute-start(f32[8,32,128]{2,1,0:T(8,128)S(1)} %get-tuple-element.88), channel_id=1, source_target_pairs={{0,96},{32,64},{64,32},{96,0},{1,97},{33,65},{65,33},{97,1},{2,98}... | collective-permute-start | bytes 393224 | tf_op jit(solution)/shard_map/ppermute | solution.py:581

commit v6 on v5

--- a/solution.py
+++ b/solution.py
@@ -26,8 +26,9 @@
 PART = 16
 PARTS = ROWS // PART
 AXES = ("sec", "brick")
-V0_AT, D_AT, V1_AT, ROW_AT, MSG = 96, 128, 224, 256, 264
-FAR = V1_AT
+V0_AT, POT_ROWS = 96, 128
+V1_AT, ROW_AT, COEF_ROWS = 96, 128, 136
+FAR_ROWS = POT_ROWS + ROWS
 PHI_PAD = 112
 V_PAD = 48
 
@@ -218,25 +219,32 @@
     lax.fori_loop(0, SLOTS + 2, edge, 0)
 
 
-def gather_kernel(scal, pot, coef, rec, exc, got_1, got_2, got_3, msg, aux, deep):
+def collect(scal, own, got, u, out):
     sec, chunk, flip = scal[0], scal[1], scal[2]
+    x = jnp.where(flip == 1, SLAB - 1 - u, u)
+    for number, ref in enumerate((own, *got)):
+        at = pl.multiple_of((sec ^ number) * HEART, HEART)
+        out[u, pl.ds(at, HEART)] = ref[x]
+    return SLAB * chunk + x
+
+
+def gather_pot(scal, own, got_1, got_2, got_3, msg):
+    def plane(u, carry):
+        collect(scal, own, (got_1, got_2, got_3), u, msg)
+        return carry
+
+    lax.fori_loop(0, SLAB, plane, 0)
+
+
+def gather_coef(scal, rec, exc, pot, own, got_1, got_2, got_3, msg, aux, deep):
     strip = jnp.full((8, 128), scal[3].astype(jnp.float32))
 
     def plane(u, carry):
-        x = jnp.where(flip == 1, SLAB - 1 - u, u)
-        whole = SLAB * chunk + x
-        for number, ref in enumerate((None, got_1, got_2, got_3)):
-            at = pl.multiple_of((sec ^ number) * HEART, HEART)
-            if number == 0:
-                msg[u, pl.ds(at, HEART)] = pot[whole]
-                deep[u, pl.ds(at, HEART)] = coef[whole]
-            else:
-                msg[u, pl.ds(at, HEART)] = ref[0, x]
-                deep[u, pl.ds(at, HEART)] = ref[1, x]
-        msg[u, D_AT : D_AT + ROWS] = deep[u, 0:ROWS]
+        whole = collect(scal, own, (got_1, got_2, got_3), u, deep)
+        msg[u, 0:ROWS] = deep[u, 0:ROWS]
         threshold = deep[u, ROWS : ROWS + HEART]
         active = exc[whole].astype(jnp.float32)
-        voltage, recovery = ionic(msg[u, V0_AT : V0_AT + HEART], rec[whole], threshold, active)
+        voltage, recovery = ionic(pot[u, V0_AT : V0_AT + HEART], rec[whole], threshold, active)
         msg[u, V1_AT : V1_AT + HEART] = voltage
         msg[u, ROW_AT : ROW_AT + 8] = strip
         aux[0, u] = threshold
@@ -247,15 +255,22 @@
     lax.fori_loop(0, SLAB, plane, 0)
 
 
-def take(ref, first, step, even, absorb=None, volt=None, volt_1=None):
+def take(ref, first, step, even):
+    def plane(u, carry):
+        even[first + step * u + OFF, PAD : PAD + ROWS] = ref[u, 0:ROWS]
+        return carry
+
+    lax.fori_loop(0, SLAB, plane, 0)
+
+
+def take_first(pot, coef, at, first, step, even, absorb, volt, volt_1=None):
     def plane(u, carry):
         x = first + step * u
-        even[x + OFF, PAD : PAD + ROWS] = ref[u, 0:ROWS]
-        if absorb is not None:
-            absorb[x] = ref[u, D_AT : D_AT + ROWS] + SHIFT
-            put_heart(volt, x, ref[u, V0_AT : V0_AT + HEART])
+        even[x + OFF, PAD : PAD + ROWS] = pot[u, 0:ROWS]
+        absorb[x] = coef[u, at : at + ROWS] + SHIFT
+        put_heart(volt, x, pot[u, V0_AT : V0_AT + HEART])
         if volt_1 is not None:
-            put_heart(volt_1, x, ref[u, V1_AT : V1_AT + HEART])
+            put_heart(volt_1, x, coef[u, V1_AT : V1_AT + HEART])
         return carry
 
     lax.fori_loop(0, SLAB, plane, 0)
@@ -308,24 +323,27 @@
     on_layer(row, work)
 
 
-def first_inner(scal, own, on, aux, even, odd, absorb, source, later, volt, volt_1, held, copy):
+def first_inner(scal, pot, coef, on_pot, on_coef, aux, *refs):
+    even, odd, absorb, source, later, volt, volt_1, held, copy = refs
+
     def send(u, carry):
-        copy[u] = own[u, 0:FAR]
+        copy[u, 0:POT_ROWS] = pot[u]
+        copy[u, POT_ROWS:FAR_ROWS] = coef[u, 0:ROWS]
         return carry
 
     lax.fori_loop(0, SLAB, send, 0)
     clear_edges(even, odd)
-    take(own, OWN, 1, even, absorb, volt, volt_1)
-    take(on, END - 1, -1, even, absorb, volt, volt_1)
+    take_first(pot, coef, 0, OWN, 1, even, absorb, volt, volt_1)
+    take_first(on_pot, on_coef, 0, END - 1, -1, even, absorb, volt, volt_1)
     row = jnp.full((1, 128), scal[3].astype(jnp.float32))
     embed(OWN + 1, END - 1, row, (volt, source), (volt_1, later))
     couple(1, SLAB, scal[3], even, volt_1, aux, held)
     sweep(scal, INNER, even, odd, absorb, source)
 
 
-def first_left(scal, near, aux, *refs):
+def first_left(scal, pot, coef, aux, *refs):
     even, odd, absorb, source, later, volt, volt_1, held = refs[8:]
-    take(near, OWN - 1, -1, even, absorb, volt, volt_1)
+    take_first(pot, coef, 0, OWN - 1, -1, even, absorb, volt, volt_1)
 
     @pl.when(scal[4] == OWN)
     def _():
@@ -334,15 +352,15 @@
 
     row = jnp.full((1, 128), scal[3].astype(jnp.float32))
     fields = ((volt, source), (volt_1, later))
-    embed(SLAB + 1, OWN, near[0, ROW_AT : ROW_AT + 1], *fields)
+    embed(SLAB + 1, OWN, coef[0, ROW_AT : ROW_AT + 1], *fields)
     embed(OWN, OWN + 1, row, *fields)
     couple(0, 1, scal[3], even, volt_1, aux, held)
     sweep(scal, LEFT, even, odd, absorb, source)
 
 
-def first_right(scal, on2, *refs):
+def first_right(scal, pot, coef, *refs):
     even, odd, absorb, source, later, volt, volt_1 = refs[7:]
-    take(on2, END, 1, even, absorb, volt, volt_1)
+    take_first(pot, coef, 0, END, 1, even, absorb, volt, volt_1)
 
     @pl.when(scal[5] == END)
     def _():
@@ -352,13 +370,13 @@
     row = jnp.full((1, 128), scal[3].astype(jnp.float32))
     fields = ((volt, source), (volt_1, later))
     embed(END - 1, END, row, *fields)
-    embed(END, SLOTS - 1, on2[0, ROW_AT : ROW_AT + 1], *fields)
+    embed(END, SLOTS - 1, coef[0, ROW_AT : ROW_AT + 1], *fields)
     sweep(scal, RIGHT, even, odd, absorb, source)
 
 
 def first_outer(scal, far, near, held, *refs):
     msg, even, odd, absorb, source, volt = refs[5:]
-    take(far, 0, 1, even, absorb, volt)
+    take_first(far, far, POT_ROWS, 0, 1, even, absorb, volt)
     embed(1, SLAB + 1, near[0, ROW_AT : ROW_AT + 1], (volt, source))
     sweep(scal, OUTER, even, odd, absorb, source)
     for u in range(SLAB):
@@ -368,7 +386,7 @@
     msg[SLAB, 2 * HEART : ROWS] = jnp.zeros((HEART, 128), jnp.float32)
 
 
-def second_inner(scal, own, on, held, first, absorb, source, even, odd, volt, out, copy):
+def second_open(scal, own, on, held, first, even, odd, volt, out, copy):
     def keep(u, carry):
         copy[u, 0:ROWS] = own[u]
         copy[u, ROWS : ROWS + HEART] = first[u, V1_AT : V1_AT + HEART]
@@ -381,6 +399,10 @@
     take(on, END - 1, -1, even)
     put_heart(volt, SLAB + 1, on[SLAB, HEART : 2 * HEART])
     settle(1, SLAB, scal[3], even, volt, out)
+
+
+def second_inner(scal, absorb, source, *refs):
+    even, odd = refs[2:]
     sweep(scal, INNER, even, odd, absorb, source)
 
 
@@ -505,21 +527,20 @@
         + [chunk_of(sec ^ number) for number in range(4)]
     ).astype(jnp.int32)
 
-    got = []
-    for number in (1, 2, 3):
-        start = SLAB * chunk_of(sec ^ number)
-        piece = jnp.stack(
-            [
-                lax.dynamic_slice_in_dim(pot, start, SLAB, 0),
-                lax.dynamic_slice_in_dim(coef, start, SLAB, 0),
-            ]
-        )
-        got.append(lax.ppermute(piece, "sec", across(number)))
-
-    msg, aux = call(
-        gather_kernel,
-        (scal, pot, coef, recovery, excitable, *got),
-        [(SLAB, MSG, 128), (3, SLAB, HEART, 128)],
+    def swapped(value):
+        got = [lax.dynamic_slice_in_dim(value, SLAB * chunk, SLAB, 0)]
+        for number in (1, 2, 3):
+            piece = lax.dynamic_slice_in_dim(value, SLAB * chunk_of(sec ^ number), SLAB, 0)
+            got.append(lax.ppermute(piece, "sec", across(number)))
+        return got
+
+    got_pot = swapped(pot)
+    got_coef = swapped(coef)
+    (msg_pot,) = call(gather_pot, (scal, *got_pot), [(SLAB, POT_ROWS, 128)], 10)
+    msg_coef, aux = call(
+        gather_coef,
+        (scal, recovery, excitable, msg_pot, *got_coef),
+        [(SLAB, COEF_ROWS, 128), (3, SLAB, HEART, 128)],
         20,
         scratch=[(SLAB, 128, 128)],
     )
@@ -532,23 +553,26 @@
     def move(value, pairs):
         return lax.ppermute(value, AXES, pairs)
 
-    near_1 = move(msg, facing)
-    on = move(msg, partner)
+    near_pot = move(msg_pot, facing)
+    near_coef = move(msg_coef, facing)
+    on_pot = move(msg_pot, partner)
+    on_coef = move(msg_coef, partner)
     *state, copy = call(
         first_inner,
-        (scal, msg, on, aux),
-        [phi, phi, wide, wide, wide, volt, volt, heart, (SLAB, FAR, 128)],
+        (scal, msg_pot, msg_coef, on_pot, on_coef, aux),
+        [phi, phi, wide, wide, wide, volt, volt, heart, (SLAB, FAR_ROWS, 128)],
         56,
     )
     far = move(copy, beyond)
-    on2 = move(near_1, partner)
-    *state, held = call(first_left, (scal, near_1, aux), [], 64, state=state)
+    on2_pot = move(near_pot, partner)
+    on2_coef = move(near_coef, partner)
+    *state, held = call(first_left, (scal, near_pot, near_coef, aux), [], 64, state=state)
     even, odd, absorb, source, later, volt_0, volt_1 = call(
-        first_right, (scal, on2), [], 64, state=state
+        first_right, (scal, on2_pot, on2_coef), [], 64, state=state
     )
     message, _, _, absorb, _, _ = call(
         first_outer,
-        (scal, far, near_1, held),
+        (scal, far, near_coef, held),
         [(SLAB + 1, ROWS, 128)],
         184,
         state=[even, odd, absorb, source, volt_0],
@@ -557,12 +581,13 @@
     near = move(message, facing)
     on = move(message, partner)
     even, odd, volt_2, voltage, copy = call(
-        second_inner,
-        (scal, message, on, held, msg, absorb, later),
+        second_open,
+        (scal, message, on, held, msg_coef),
         [phi, phi, (SLAB + 2, V_PAD, 128), heart, (SLAB, ROWS + HEART, 128)],
-        56,
+        20,
     )
     far = move(copy, beyond)
+    even, odd = call(second_inner, (scal, absorb, later), [], 56, state=[even, odd])
     on2 = move(near, partner)
     even, odd, _, voltage = call(
         second_left, (scal, near, absorb, later), [], 64, state=[even, odd, volt_2, voltage]
@@ -570,7 +595,7 @@
     even, odd = call(second_right, (scal, on2, absorb, later), [], 64, state=[even, odd])
     outs = call(
         second_outer,
-        (scal, far, near_1, absorb, voltage),
+        (scal, far, near_coef, absorb, voltage),
         [heart] * 4,
         184,
         scratch=[(SLAB, 128, 128)],

time: 109 us -> 98.2 us (0.901); the launches traced: 109 us -> 96.7 us
  waiting for transfers between devices: 42.9 us -> 20.1 us
  starting transfers between devices: 21.2 us -> 30.6 us
  Pallas kernels: 41.6 us -> 42.7 us
    ppermute x8 -> x11, waiting for transfers between devices: 26.4 us -> 6.64 us  [move(): return lax.ppermute(value, AXES, pairs)]
    ppermute x8 -> x11, starting transfers between devices: 16.5 us -> 23.6 us  [move(): return lax.ppermute(value, AXES, pairs)]
    ppermute x3 -> x6, waiting for transfers between devices: 10.5 us -> 7.14 us  [swapped(): got.append(lax.ppermute(piece, 'sec', across(number)))]
    ppermute x3 -> x6, starting transfers between devices: 2.48 us -> 4.7 us  [swapped(): got.append(lax.ppermute(piece, 'sec', across(number)))]
    pallas_call x10 -> x12, Pallas kernels: 41.6 us -> 42.7 us  [call(): pl.pallas_call(kernel, out_shape=arrays, in_specs=[SMEM] + [VMEM] * (len(...]
    dynamic_slice x1 -> x2, local copies, waits for them, and re-layouts: 1.39 us -> 2.34 us  [swapped(): lax.dynamic_slice_in_dim(value, SLAB * chunk_of(sec ^ number), SLAB, 0)]
  transfers between devices with their start and end apart: 14 -> 20, of which waited for: 8 -> 7; matrix products, arithmetic and copies ran while one was open for 1% -> 1% of each run, Pallas kernels for 21% -> 25%
where the time goes in v6:
time: 98.2 us; the launch traced here: 96.7 us
  Pallas kernels  42.7 us (43%)
  starting transfers between devices  30.6 us (31%)
  waiting for transfers between devices  20.1 us (20%)
  local copies, waits for them, and re-layouts  2.44 us (2%)
    pallas_call x12, Pallas kernels, call(): pl.pallas_call(kernel, out_shape=arrays, in_specs=[SMEM] + [VMEM] * (len(...  42.7 us
    ppermute x11, starting transfers between devices, move(): return lax.ppermute(value, AXES, pairs)  23.6 us
    ppermute x6, waiting for transfers between devices, swapped(): got.append(lax.ppermute(piece, 'sec', across(number)))  7.14 us
    ppermute x11, waiting for transfers between devices, move(): return lax.ppermute(value, AXES, pairs)  6.64 us
    ppermute x3, waiting for transfers between devices, body(): back.append(lax.ppermute(outs[number], 'sec', across(number)))  6.31 us
    ppermute x6, starting transfers between devices, swapped(): got.append(lax.ppermute(piece, 'sec', across(number)))  4.7 us
    dynamic_slice x2, local copies, waits for them, and re-layouts, swapped(): lax.dynamic_slice_in_dim(value, SLAB * chunk_of(sec ^ number), SLAB, 0)  2.34 us
    ppermute x3, starting transfers between devices, body(): back.append(lax.ppermute(outs[number], 'sec', across(number)))  2.32 us
  transfers between devices with their start and end apart: 20, of which 7 were waited for; matrix products, arithmetic and copies ran while one was open for 1% of the time, Pallas kernels for 25%

profile of v6, /device:TPU:105, one launch (start us, length us, event | category | flops | bytes accessed | tf_op | source)
XLA Modules:
  0.0 96.7 jit_solution(4189341176122243173)
XLA Ops:
  2.1 1.6 %collective-permute-start.2 = (f32[8,32,128]{2,1,0:T(8,128)S(1)}, f32[8,32,128]{2,1,0:T(8,128)S(1)}, u32[]{:S(2)}, u32[]{:S(2)}) collective-permute-start(f32[8,32,128]{2,1,0:T(8,128)S(1)} %get-tuple-element.97), channel_id=1, source_target_pairs={{0,96},{32,64},{64,32},{96,0},{1,97},{33,65},{65,33},{97,1},{2,98}... | collective-permute-start | bytes 393224 | tf_op jit(solution)/shard_map/ppermute | solution.py:534
  5.2 1.8 %collective-permute-start.5 = (f32[8,32,128]{2,1,0:T(8,128)S(1)}, f32[8,32,128]{2,1,0:T(8,128)S(1)}, u32[]{:S(2)}, u32[]{:S(2)}) collective-permute-start(f32[8,32,128]{2,1,0:T(8,128)S(1)} %get-tuple-element.93), channel_id=1, source_target_pairs={{0,96},{32,64},{64,32},{96,0},{1,97},{33,65},{65,33},{97,1},{2,98}... | collective-permute-start | bytes 393224 | tf_op jit(solution)/shard_map/ppermute | solution.py:534
  7.8 2.7 %collective-permute-done.2.got_3 = f32[8,32,128]{2,1,0:T(8,128)S(1)} collective-permute-done((f32[8,32,128]{2,1,0:T(8,128)S(1)}, f32[8,32,128]{2,1,0:T(8,128)S(1)}, u32[]{:S(2)}, u32[]{:S(2)}) %collective-permute-start.2) | collective-permute-done | bytes 131104 | tf_op jit(solution)/shard_map/ppermute | solution.py:534
  12.6 3.1 %collective-permute-done.5.got_3 = f32[8,32,128]{2,1,0:T(8,128)S(1)} collective-permute-done((f32[8,32,128]{2,1,0:T(8,128)S(1)}, f32[8,32,128]{2,1,0:T(8,128)S(1)}, u32[]{:S(2)}, u32[]{:S(2)}) %collective-permute-start.5) | collective-permute-done | bytes 131104 | tf_op jit(solution)/shard_map/ppermute | solution.py:534
  17.4 5.2 %collective-permute-start.9 = (f32[8,136,128]{2,1,0:T(8,128)S(1)}, f32[8,136,128]{2,1,0:T(8,128)S(1)}, u32[]{:S(2)}, u32[]{:S(2)}) collective-permute-start(f32[8,136,128]{2,1,0:T(8,128)S(1)} %get-tuple-element.49.coef.first), channel_id=1, source_target_pairs={{64,32},{32,64},{0,1},{1,0},{33,65},{65,33},{97,98},{98,97},{66,34... | collective-permute-start | bytes 1671176 | tf_op jit(solution)/shard_map/ppermute | solution.py:554
  22.6 3.3 %collective-permute-start.10 = (f32[8,128,128]{2,1,0:T(8,128)S(1)}, f32[8,128,128]{2,1,0:T(8,128)S(1)}, u32[]{:S(2)}, u32[]{:S(2)}) collective-permute-start(f32[8,128,128]{2,1,0:T(8,128)S(1)} %shard_map.55.pot), channel_id=1, source_target_pairs={{64,32},{32,64},{0,1},{1,0},{33,65},{65,33},{97,98},{98,97},{66,34... | collective-permute-start | bytes 1572872 | tf_op jit(solution)/shard_map/ppermute | solution.py:554
  26.0 5.7 %shard_map.57 = (f32[42,112,128]{2,1,0:T(8,128)S(1)}, f32[42,112,128]{2,1,0:T(8,128)S(1)}, f32[40,96,128]{2,1,0:T(8,128)S(1)}, f32[40,96,128]{2,1,0:T(8,128)S(1)...) custom-call(s32[10]{0:T(128)S(1)} %stack.36.scal, ...), custom_call_target="tpu_custom_call" | custom-call | flops 11200000 | bytes 5600000 | tf_op jit(solution)/shard_map/pallas_call | solution.py:477
  31.7 1.9 %collective-permute-start.8 = (f32[8,224,128]{2,1,0:T(8,128)S(1)}, f32[8,224,128]{2,1,0:T(8,128)S(1)}, u32[]{:S(2)}, u32[]{:S(2)}) collective-permute-start(f32[8,224,128]{2,1,0:T(8,128)S(1)} %get-tuple-element.51), channel_id=1, source_target_pairs={{96,32},{32,1},{1,65},{65,98},{98,34},{34,3},{3,67},{67,4},{4,68},... | collective-permute-start | bytes 2752520 | tf_op jit(solution)/shard_map/ppermute | solution.py:554
  33.6 3.8 %collective-permute-start.12 = (f32[8,136,128]{2,1,0:T(8,128)S(1)}, f32[8,136,128]{2,1,0:T(8,128)S(1)}, u32[]{:S(2)}, u32[]{:S(2)}) collective-permute-start(f32[8,136,128]{2,1,0:T(8,128)S(1)} %collective-permute-done.9.coef.near), channel_id=1, source_target_pairs={{96,64},{64,96},{32,0},{0,32},{1,33},{33,1},{65,97},{97,65},{98,66... | collective-permute-start | bytes 1671176 | tf_op jit(solution)/shard_map/ppermute | solution.py:554
  37.6 3.8 %shard_map.58 = (f32[42,112,128]{2,1,0:T(8,128)S(1)}, f32[42,112,128]{2,1,0:T(8,128)S(1)}, f32[40,96,128]{2,1,0:T(8,128)S(1)}, f32[40,96,128]{2,1,0:T(8,128)S(1)...) custom-call(s32[10]{0:T(128)S(1)} %stack.36.scal, ...), custom_call_target="tpu_custom_call", output_to_operand_aliasing={{0}: (4, {}), {1}: (5, {}), {2}: (6, {}), {3}: (7, {}), {4}... | custom-call | flops 12800000 | bytes 6400000 | tf_op jit(solution)/shard_map/pallas_call | solution.py:477
  41.3 3.6 %shard_map.59 = (f32[42,112,128]{2,1,0:T(8,128)S(1)}, f32[42,112,128]{2,1,0:T(8,128)S(1)}, f32[40,96,128]{2,1,0:T(8,128)S(1)}, f32[40,96,128]{2,1,0:T(8,128)S(1)...) custom-call(s32[10]{0:T(128)S(1)} %stack.36.scal, ...), custom_call_target="tpu_custom_call", output_to_operand_aliasing={{0}: (3, {}), {1}: (4, {}), {2}: (5, {}), {3}: (6, {}), {4}... | custom-call | flops 12800000 | bytes 6400000 | tf_op jit(solution)/shard_map/pallas_call | solution.py:477
  44.9 3.9 %collective-permute-done.8.far = f32[8,224,128]{2,1,0:T(8,128)S(1)} collective-permute-done((f32[8,224,128]{2,1,0:T(8,128)S(1)}, f32[8,224,128]{2,1,0:T(8,128)S(1)}, u32[]{:S(2)}, u32[]{:S(2)}) %collective-permute-start.8) | collective-permute-done | bytes 917536 | tf_op jit(solution)/shard_map/ppermute | solution.py:554
  48.9 8.1 %shard_map.60 = (f32[9,96,128]{2,1,0:T(8,128)S(1)}, f32[42,112,128]{2,1,0:T(8,128)S(1)}, f32[42,112,128]{2,1,0:T(8,128)S(1)}, f32[40,96,128]{2,1,0:T(8,128)S(1)}...) custom-call(s32[10]{0:T(128)S(1)} %stack.36.scal, ...), custom_call_target="tpu_custom_call", output_to_operand_aliasing={{1}: (4, {}), {2}: (5, {}), {3}: (6, {}), {4}: (7, {}), {5}... | custom-call | flops 36800000 | bytes 18400000 | tf_op jit(solution)/shard_map/pallas_call | solution.py:477
  57.2 6.4 %collective-permute-start.15 = (f32[9,96,128]{2,1,0:T(8,128)S(1)}, f32[9,96,128]{2,1,0:T(8,128)S(1)}, u32[]{:S(2)}, u32[]{:S(2)}) collective-permute-start(f32[9,96,128]{2,1,0:T(8,128)S(1)} %get-tuple-element.73.own), channel_id=1, source_target_pairs={{64,32},{32,64},{0,1},{1,0},{33,65},{65,33},{97,98},{98,97},{66,34... | collective-permute-start | bytes 1327112 | tf_op jit(solution)/shard_map/ppermute | solution.py:554
  63.7 1.6 %shard_map.61 = (f32[42,112,128]{2,1,0:T(8,128)S(1)}, f32[42,112,128]{2,1,0:T(8,128)S(1)}, f32[10,48,128]{2,1,0:T(8,128)S(1)}, f32[8,32,128]{2,1,0:T(8,128)S(1)}, f32[8,128,128]{2,1,0:T(8,128)S(1)}) custom-call(s32[10]{0:T(128)S(1)} %stack.36.scal, f32[9,96,128]{2,1,0:T(8,128)S(1)} %get-tuple-element.73.own, f32[9,96,128]{2,1,0:T(8,128)S(1)} %collective-permute-done.13.on, ...), custom_call_target="tpu_custom_call" | custom-call | flops 4000000 | bytes 2000000 | tf_op jit(solution)/shard_map/pallas_call | solution.py:477
  65.2 1.9 %collective-permute-start.14 = (f32[8,128,128]{2,1,0:T(8,128)S(1)}, f32[8,128,128]{2,1,0:T(8,128)S(1)}, u32[]{:S(2)}, u32[]{:S(2)}) collective-permute-start(f32[8,128,128]{2,1,0:T(8,128)S(1)} %get-tuple-element.74), channel_id=1, source_target_pairs={{96,32},{32,1},{1,65},{65,98},{98,34},{34,3},{3,67},{67,4},{4,68},... | collective-permute-start | bytes 1572872 | tf_op jit(solution)/shard_map/ppermute | solution.py:554
  67.2 2.7 %collective-permute-done.15.near = f32[9,96,128]{2,1,0:T(8,128)S(1)} collective-permute-done((f32[9,96,128]{2,1,0:T(8,128)S(1)}, f32[9,96,128]{2,1,0:T(8,128)S(1)}, u32[]{:S(2)}, u32[]{:S(2)}) %collective-permute-start.15) | collective-permute-done | bytes 442400 | tf_op jit(solution)/shard_map/ppermute | solution.py:554
  69.9 2.8 %shard_map.62 = (f32[42,112,128]{2,1,0:T(8,128)S(1)}, f32[42,112,128]{2,1,0:T(8,128)S(1)}) custom-call(s32[10]{0:T(128)S(1)} %stack.36.scal, f32[40,96,128]{2,1,0:T(8,128)S(1)} %get-tuple-element.75.absorb, f32[40,96,128]{2,1,0:T(8,128)S(1)} %get-tuple-element.76.source.refs_2_, ...), custom_call_target="tpu_custom_call", output_to_operand_aliasing={{0}: (3, {}), {1}: (4, {})} | custom-call | flops 11200000 | bytes 5600000 | tf_op jit(solution)/shard_map/pallas_call | solution.py:477
  72.7 2.9 %shard_map.63 = (f32[42,112,128]{2,1,0:T(8,128)S(1)}, f32[42,112,128]{2,1,0:T(8,128)S(1)}, f32[10,48,128]{2,1,0:T(8,128)S(1)}, f32[8,32,128]{2,1,0:T(8,128)S(1)}) custom-call(s32[10]{0:T(128)S(1)} %stack.36.scal, f32[9,96,128]{2,1,0:T(8,128)S(1)} %collective-permute-done.15.near, ...), custom_call_target="tpu_custom_call", output_to_operand_aliasing={{0}: (4, {}), {1}: (5, {}), {2}: (6, {}), {3}: (7, {})} | custom-call | flops 12800000 | bytes 6400000 | tf_op jit(solution)/shard_map/pallas_call | solution.py:477
  75.7 2.8 %shard_map.64 = (f32[42,112,128]{2,1,0:T(8,128)S(1)}, f32[42,112,128]{2,1,0:T(8,128)S(1)}) custom-call(s32[10]{0:T(128)S(1)} %stack.36.scal, f32[9,96,128]{2,1,0:T(8,128)S(1)} %collective-permute-done.16.on2, f32[40,96,128]{2,1,0:T(8,128)S(1)} %get-tuple-element.75.absorb, ...), custom_call_target="tpu_custom_call", output_to_operand_aliasing={{0}: (4, {}), {1}: (5, {})} | custom-call | flops 12800000 | bytes 6400000 | tf_op jit(solution)/shard_map/pallas_call | solution.py:477
  78.5 8.2 %shard_map.65 = (f32[8,32,128]{2,1,0:T(8,128)S(1)}, f32[8,32,128]{2,1,0:T(8,128)S(1)}, f32[8,32,128]{2,1,0:T(8,128)S(1)}, f32[8,32,128]{2,1,0:T(8,128)S(1)}, f32...) custom-call(s32[10]{0:T(128)S(1)} %stack.36.scal, ...), custom_call_target="tpu_custom_call", output_to_operand_aliasing={{4}: (5, {}), {5}: (6, {}), {6}: (7, {}), {7}: (8, {})} | custom-call | flops 36800000 | bytes 18400000 | tf_op jit(solution)/shard_map/pallas_call | solution.py:477
  87.3 1.7 %collective-permute-start.19 = (f32[8,32,128]{2,1,0:T(8,128)S(1)}, f32[8,32,128]{2,1,0:T(8,128)S(1)}, u32[]{:S(2)}, u32[]{:S(2)}) collective-permute-start(f32[8,32,128]{2,1,0:T(8,128)S(1)} %get-tuple-element.92), channel_id=1, source_target_pairs={{0,96},{32,64},{64,32},{96,0},{1,97},{33,65},{65,33},{97,1},{2,98}... | collective-permute-start | bytes 393224 | tf_op jit(solution)/shard_map/ppermute | solution.py:606
  89.0 3.2 %collective-permute-done.18.got_2 = f32[8,32,128]{2,1,0:T(8,128)S(1)} collective-permute-done((f32[8,32,128]{2,1,0:T(8,128)S(1)}, f32[8,32,128]{2,1,0:T(8,128)S(1)}, u32[]{:S(2)}, u32[]{:S(2)}) %collective-permute-start.18) | collective-permute-done | bytes 131104 | tf_op jit(solution)/shard_map/ppermute | solution.py:606
  92.2 3.1 %collective-permute-done.19.got_3 = f32[8,32,128]{2,1,0:T(8,128)S(1)} collective-permute-done((f32[8,32,128]{2,1,0:T(8,128)S(1)}, f32[8,32,128]{2,1,0:T(8,128)S(1)}, u32[]{:S(2)}, u32[]{:S(2)}) %collective-permute-start.19) | collective-permute-done | bytes 131104 | tf_op jit(solution)/shard_map/ppermute | solution.py:606
  (35 shorter events, 9.8 us)
Async XLA Ops:
  0.0 15.6 %copy-start = (f32[32,32,128]{2,1,0:T(8,128)S(1)}, f32[32,32,128]{2,1,0:T(8,128)}, u32[]{:S(2)}) copy-start(f32[32,32,128]{2,1,0:T(8,128)} %rec.1) | copy-start | bytes 1572868
  0.0 15.6 %copy-start.1 = (s32[32,32,128]{2,1,0:T(8,128)S(1)}, s32[32,32,128]{2,1,0:T(8,128)}, u32[]{:S(2)}) copy-start(s32[32,32,128]{2,1,0:T(8,128)} %exc.1) | copy-start | bytes 1572868
  1.2 4.0 %collective-permute-start = (f32[8,32,128]{2,1,0:T(8,128)S(1)}, f32[8,32,128]{2,1,0:T(8,128)S(1)}, u32[]{:S(2)}, u32[]{:S(2)}) collective-permute-start(f32[8,32,128]{2,1,0:T(8,128)S(1)} %get-tuple-element.98), channel_id=1, source_target_pairs={{0,32},{32,0},{64,96},{96,64},{1,33},{33,1},{65,97},{97,65},{2,34}... | collective-permute-start | bytes 393224 | tf_op jit(solution)/shard_map/ppermute | solution.py:534
  2.0 5.8 %collective-permute-start.1 = (f32[8,32,128]{2,1,0:T(8,128)S(1)}, f32[8,32,128]{2,1,0:T(8,128)S(1)}, u32[]{:S(2)}, u32[]{:S(2)}) collective-permute-start(f32[8,32,128]{2,1,0:T(8,128)S(1)} %get-tuple-element.100), channel_id=1, source_target_pairs={{0,64},{32,96},{64,0},{96,32},{1,65},{33,97},{65,1},{97,33},{2,66}... | collective-permute-start | bytes 393224 | tf_op jit(solution)/shard_map/ppermute | solution.py:534
  2.1 8.4 %collective-permute-start.2 = (f32[8,32,128]{2,1,0:T(8,128)S(1)}, f32[8,32,128]{2,1,0:T(8,128)S(1)}, u32[]{:S(2)}, u32[]{:S(2)}) collective-permute-start(f32[8,32,128]{2,1,0:T(8,128)S(1)} %get-tuple-element.97), channel_id=1, source_target_pairs={{0,96},{32,64},{64,32},{96,0},{1,97},{33,65},{65,33},{97,1},{2,98}... | collective-permute-start | bytes 393224 | tf_op jit(solution)/shard_map/ppermute | solution.py:534
  4.8 6.4 %collective-permute-start.3 = (f32[8,32,128]{2,1,0:T(8,128)S(1)}, f32[8,32,128]{2,1,0:T(8,128)S(1)}, u32[]{:S(2)}, u32[]{:S(2)}) collective-permute-start(f32[8,32,128]{2,1,0:T(8,128)S(1)} %get-tuple-element.94), channel_id=1, source_target_pairs={{0,32},{32,0},{64,96},{96,64},{1,33},{33,1},{65,97},{97,65},{2,34}... | collective-permute-start | bytes 393224 | tf_op jit(solution)/shard_map/ppermute | solution.py:534
  5.1 7.5 %collective-permute-start.4 = (f32[8,32,128]{2,1,0:T(8,128)S(1)}, f32[8,32,128]{2,1,0:T(8,128)S(1)}, u32[]{:S(2)}, u32[]{:S(2)}) collective-permute-start(f32[8,32,128]{2,1,0:T(8,128)S(1)} %get-tuple-element.96), channel_id=1, source_target_pairs={{0,64},{32,96},{64,0},{96,32},{1,65},{33,97},{65,1},{97,33},{2,66}... | collective-permute-start | bytes 393224 | tf_op jit(solution)/shard_map/ppermute | solution.py:534
  5.2 10.4 %collective-permute-start.5 = (f32[8,32,128]{2,1,0:T(8,128)S(1)}, f32[8,32,128]{2,1,0:T(8,128)S(1)}, u32[]{:S(2)}, u32[]{:S(2)}) collective-permute-start(f32[8,32,128]{2,1,0:T(8,128)S(1)} %get-tuple-element.93), channel_id=1, source_target_pairs={{0,96},{32,64},{64,32},{96,0},{1,97},{33,65},{65,33},{97,1},{2,98}... | collective-permute-start | bytes 393224 | tf_op jit(solution)/shard_map/ppermute | solution.py:534
  16.8 9.2 %collective-permute-start.7 = (f32[8,136,128]{2,1,0:T(8,128)S(1)}, f32[8,136,128]{2,1,0:T(8,128)S(1)}, u32[]{:S(2)}, u32[]{:S(2)}) collective-permute-start(f32[8,136,128]{2,1,0:T(8,128)S(1)} %get-tuple-element.49.coef.first), channel_id=1, source_target_pairs={{96,64},{64,96},{32,0},{0,32},{1,33},{33,1},{65,97},{97,65},{98,66... | collective-permute-start | bytes 1671176 | tf_op jit(solution)/shard_map/ppermute | solution.py:554
  17.0 9.0 %collective-permute-start.6 = (f32[8,128,128]{2,1,0:T(8,128)S(1)}, f32[8,128,128]{2,1,0:T(8,128)S(1)}, u32[]{:S(2)}, u32[]{:S(2)}) collective-permute-start(f32[8,128,128]{2,1,0:T(8,128)S(1)} %shard_map.55.pot), channel_id=1, source_target_pairs={{96,64},{64,96},{32,0},{0,32},{1,33},{33,1},{65,97},{97,65},{98,66... | collective-permute-start | bytes 1572872 | tf_op jit(solution)/shard_map/ppermute | solution.py:554
  17.4 16.3 %collective-permute-start.9 = (f32[8,136,128]{2,1,0:T(8,128)S(1)}, f32[8,136,128]{2,1,0:T(8,128)S(1)}, u32[]{:S(2)}, u32[]{:S(2)}) collective-permute-start(f32[8,136,128]{2,1,0:T(8,128)S(1)} %get-tuple-element.49.coef.first), channel_id=1, source_target_pairs={{64,32},{32,64},{0,1},{1,0},{33,65},{65,33},{97,98},{98,97},{66,34... | collective-permute-start | bytes 1671176 | tf_op jit(solution)/shard_map/ppermute | solution.py:554
  22.6 14.8 %collective-permute-start.10 = (f32[8,128,128]{2,1,0:T(8,128)S(1)}, f32[8,128,128]{2,1,0:T(8,128)S(1)}, u32[]{:S(2)}, u32[]{:S(2)}) collective-permute-start(f32[8,128,128]{2,1,0:T(8,128)S(1)} %shard_map.55.pot), channel_id=1, source_target_pairs={{64,32},{32,64},{0,1},{1,0},{33,65},{65,33},{97,98},{98,97},{66,34... | collective-permute-start | bytes 1572872 | tf_op jit(solution)/shard_map/ppermute | solution.py:554
  31.7 17.1 %collective-permute-start.8 = (f32[8,224,128]{2,1,0:T(8,128)S(1)}, f32[8,224,128]{2,1,0:T(8,128)S(1)}, u32[]{:S(2)}, u32[]{:S(2)}) collective-permute-start(f32[8,224,128]{2,1,0:T(8,128)S(1)} %get-tuple-element.51), channel_id=1, source_target_pairs={{96,32},{32,1},{1,65},{65,98},{98,34},{34,3},{3,67},{67,4},{4,68},... | collective-permute-start | bytes 2752520 | tf_op jit(solution)/shard_map/ppermute | solution.py:554
  33.6 7.7 %collective-permute-start.12 = (f32[8,136,128]{2,1,0:T(8,128)S(1)}, f32[8,136,128]{2,1,0:T(8,128)S(1)}, u32[]{:S(2)}, u32[]{:S(2)}) collective-permute-start(f32[8,136,128]{2,1,0:T(8,128)S(1)} %collective-permute-done.9.coef.near), channel_id=1, source_target_pairs={{96,64},{64,96},{32,0},{0,32},{1,33},{33,1},{65,97},{97,65},{98,66... | collective-permute-start | bytes 1671176 | tf_op jit(solution)/shard_map/ppermute | solution.py:554
  37.5 3.9 %collective-permute-start.11 = (f32[8,128,128]{2,1,0:T(8,128)S(1)}, f32[8,128,128]{2,1,0:T(8,128)S(1)}, u32[]{:S(2)}, u32[]{:S(2)}) collective-permute-start(f32[8,128,128]{2,1,0:T(8,128)S(1)} %collective-permute-done.10.pot), channel_id=1, source_target_pairs={{96,64},{64,96},{32,0},{0,32},{1,33},{33,1},{65,97},{97,65},{98,66... | collective-permute-start | bytes 1572872 | tf_op jit(solution)/shard_map/ppermute | solution.py:554
  57.0 6.7 %collective-permute-start.13 = (f32[9,96,128]{2,1,0:T(8,128)S(1)}, f32[9,96,128]{2,1,0:T(8,128)S(1)}, u32[]{:S(2)}, u32[]{:S(2)}) collective-permute-start(f32[9,96,128]{2,1,0:T(8,128)S(1)} %get-tuple-element.73.own), channel_id=1, source_target_pairs={{96,64},{64,96},{32,0},{0,32},{1,33},{33,1},{65,97},{97,65},{98,66... | collective-permute-start | bytes 1327112 | tf_op jit(solution)/shard_map/ppermute | solution.py:554
  57.2 12.6 %collective-permute-start.15 = (f32[9,96,128]{2,1,0:T(8,128)S(1)}, f32[9,96,128]{2,1,0:T(8,128)S(1)}, u32[]{:S(2)}, u32[]{:S(2)}) collective-permute-start(f32[9,96,128]{2,1,0:T(8,128)S(1)} %get-tuple-element.73.own), channel_id=1, source_target_pairs={{64,32},{32,64},{0,1},{1,0},{33,65},{65,33},{97,98},{98,97},{66,34... | collective-permute-start | bytes 1327112 | tf_op jit(solution)/shard_map/ppermute | solution.py:554
  65.2 13.2 %collective-permute-start.14 = (f32[8,128,128]{2,1,0:T(8,128)S(1)}, f32[8,128,128]{2,1,0:T(8,128)S(1)}, u32[]{:S(2)}, u32[]{:S(2)}) collective-permute-start(f32[8,128,128]{2,1,0:T(8,128)S(1)} %get-tuple-element.74), channel_id=1, source_target_pairs={{96,32},{32,1},{1,65},{65,98},{98,34},{34,3},{3,67},{67,4},{4,68},... | collective-permute-start | bytes 1572872 | tf_op jit(solution)/shard_map/ppermute | solution.py:554
  69.9 5.8 %collective-permute-start.16 = (f32[9,96,128]{2,1,0:T(8,128)S(1)}, f32[9,96,128]{2,1,0:T(8,128)S(1)}, u32[]{:S(2)}, u32[]{:S(2)}) collective-permute-start(f32[9,96,128]{2,1,0:T(8,128)S(1)} %collective-permute-done.15.near), channel_id=1, source_target_pairs={{96,64},{64,96},{32,0},{0,32},{1,33},{33,1},{65,97},{97,65},{98,66... | collective-permute-start | bytes 1327112 | tf_op jit(solution)/shard_map/ppermute | solution.py:554
  86.7 2.3 %collective-permute-start.17 = (f32[8,32,128]{2,1,0:T(8,128)S(1)}, f32[8,32,128]{2,1,0:T(8,128)S(1)}, u32[]{:S(2)}, u32[]{:S(2)}) collective-permute-start(f32[8,32,128]{2,1,0:T(8,128)S(1)} %get-tuple-element.90), channel_id=1, source_target_pairs={{0,32},{32,0},{64,96},{96,64},{1,33},{33,1},{65,97},{97,65},{2,34}... | collective-permute-start | bytes 393224 | tf_op jit(solution)/shard_map/ppermute | solution.py:606
  87.3 5.0 %collective-permute-start.18 = (f32[8,32,128]{2,1,0:T(8,128)S(1)}, f32[8,32,128]{2,1,0:T(8,128)S(1)}, u32[]{:S(2)}, u32[]{:S(2)}) collective-permute-start(f32[8,32,128]{2,1,0:T(8,128)S(1)} %get-tuple-element.91), channel_id=1, source_target_pairs={{0,64},{32,96},{64,0},{96,32},{1,65},{33,97},{65,1},{97,33},{2,66}... | collective-permute-start | bytes 393224 | tf_op jit(solution)/shard_map/ppermute | solution.py:606
  87.3 8.0 %collective-permute-start.19 = (f32[8,32,128]{2,1,0:T(8,128)S(1)}, f32[8,32,128]{2,1,0:T(8,128)S(1)}, u32[]{:S(2)}, u32[]{:S(2)}) collective-permute-start(f32[8,32,128]{2,1,0:T(8,128)S(1)} %get-tuple-element.92), channel_id=1, source_target_pairs={{0,96},{32,64},{64,32},{96,0},{1,97},{33,65},{65,33},{97,1},{2,98}... | collective-permute-start | bytes 393224 | tf_op jit(solution)/shard_map/ppermute | solution.py:606

commit v7 on v6

--- a/solution.py
+++ b/solution.py
@@ -323,15 +323,17 @@
     on_layer(row, work)
 
 
-def first_inner(scal, pot, coef, on_pot, on_coef, aux, *refs):
-    even, odd, absorb, source, later, volt, volt_1, held, copy = refs
-
+def first_open(scal, pot, coef, copy):
     def send(u, carry):
         copy[u, 0:POT_ROWS] = pot[u]
         copy[u, POT_ROWS:FAR_ROWS] = coef[u, 0:ROWS]
         return carry
 
     lax.fori_loop(0, SLAB, send, 0)
+
+
+def first_inner(scal, pot, coef, on_pot, on_coef, aux, *refs):
+    even, odd, absorb, source, later, volt, volt_1, held = refs
     clear_edges(even, odd)
     take_first(pot, coef, 0, OWN, 1, even, absorb, volt, volt_1)
     take_first(on_pot, on_coef, 0, END - 1, -1, even, absorb, volt, volt_1)
@@ -557,13 +559,14 @@
     near_coef = move(msg_coef, facing)
     on_pot = move(msg_pot, partner)
     on_coef = move(msg_coef, partner)
-    *state, copy = call(
+    (copy,) = call(first_open, (scal, msg_pot, msg_coef), [(SLAB, FAR_ROWS, 128)], 5)
+    far = move(copy, beyond)
+    state = call(
         first_inner,
         (scal, msg_pot, msg_coef, on_pot, on_coef, aux),
-        [phi, phi, wide, wide, wide, volt, volt, heart, (SLAB, FAR_ROWS, 128)],
+        [phi, phi, wide, wide, wide, volt, volt, heart],
         56,
     )
-    far = move(copy, beyond)
     on2_pot = move(near_pot, partner)
     on2_coef = move(near_coef, partner)
     *state, held = call(first_left, (scal, near_pot, near_coef, aux), [], 64, state=state)

time: 98.2 us -> 101 us (1.029); the launches traced: 96.7 us -> 101 us
  waiting for transfers between devices: 20.1 us -> 24.1 us
    ppermute x11, waiting for transfers between devices: 6.64 us -> 10.6 us  [move(): return lax.ppermute(value, AXES, pairs)]
    pallas_call x12 -> x13, Pallas kernels: 42.7 us -> 43.2 us  [call(): pl.pallas_call(kernel, out_shape=arrays, in_specs=[SMEM] + [VMEM] * (len(...]
  transfers between devices with their start and end apart: 20 -> 20, of which waited for: 7 -> 7; matrix products, arithmetic and copies ran while one was open for 1% -> 1% of each run, Pallas kernels for 25% -> 24%
where the time goes in v7:
time: 101 us
  Pallas kernels  43.2 us (43%)
  starting transfers between devices  29.9 us (30%)
  waiting for transfers between devices  24.1 us (24%)
  local copies, waits for them, and re-layouts  2.44 us (2%)
    pallas_call x13, Pallas kernels, call(): pl.pallas_call(kernel, out_shape=arrays, in_specs=[SMEM] + [VMEM] * (len(...  43.2 us
    ppermute x11, starting transfers between devices, move(): return lax.ppermute(value, AXES, pairs)  22.9 us
    ppermute x11, waiting for transfers between devices, move(): return lax.ppermute(value, AXES, pairs)  10.6 us
    ppermute x6, waiting for transfers between devices, swapped(): got.append(lax.ppermute(piece, 'sec', across(number)))  7.15 us
    ppermute x3, waiting for transfers between devices, body(): back.append(lax.ppermute(outs[number], 'sec', across(number)))  6.31 us
    ppermute x6, starting transfers between devices, swapped(): got.append(lax.ppermute(piece, 'sec', across(number)))  4.7 us
    dynamic_slice x2, local copies, waits for them, and re-layouts, swapped(): lax.dynamic_slice_in_dim(value, SLAB * chunk_of(sec ^ number), SLAB, 0)  2.34 us
    ppermute x3, starting transfers between devices, body(): back.append(lax.ppermute(outs[number], 'sec', across(number)))  2.32 us
  transfers between devices with their start and end apart: 20, of which 7 were waited for; matrix products, arithmetic and copies ran while one was open for 1% of the time, Pallas kernels for 24%

profile of v7, /device:TPU:105, one launch (start us, length us, event | category | flops | bytes accessed | tf_op | source)
XLA Modules:
  0.0 100.6 jit_solution(912321988452219937)
XLA Ops:
  2.1 1.6 %collective-permute-start.2 = (f32[8,32,128]{2,1,0:T(8,128)S(1)}, f32[8,32,128]{2,1,0:T(8,128)S(1)}, u32[]{:S(2)}, u32[]{:S(2)}) collective-permute-start(f32[8,32,128]{2,1,0:T(8,128)S(1)} %get-tuple-element.95), channel_id=1, source_target_pairs={{0,96},{32,64},{64,32},{96,0},{1,97},{33,65},{65,33},{97,1},{2,98}... | collective-permute-start | bytes 393224 | tf_op jit(solution)/shard_map/ppermute | solution.py:536
  5.2 1.8 %collective-permute-start.5 = (f32[8,32,128]{2,1,0:T(8,128)S(1)}, f32[8,32,128]{2,1,0:T(8,128)S(1)}, u32[]{:S(2)}, u32[]{:S(2)}) collective-permute-start(f32[8,32,128]{2,1,0:T(8,128)S(1)} %get-tuple-element.91), channel_id=1, source_target_pairs={{0,96},{32,64},{64,32},{96,0},{1,97},{33,65},{65,33},{97,1},{2,98}... | collective-permute-start | bytes 393224 | tf_op jit(solution)/shard_map/ppermute | solution.py:536
  7.8 2.7 %collective-permute-done.2.got_3 = f32[8,32,128]{2,1,0:T(8,128)S(1)} collective-permute-done((f32[8,32,128]{2,1,0:T(8,128)S(1)}, f32[8,32,128]{2,1,0:T(8,128)S(1)}, u32[]{:S(2)}, u32[]{:S(2)}) %collective-permute-start.2) | collective-permute-done | bytes 131104 | tf_op jit(solution)/shard_map/ppermute | solution.py:536
  12.6 3.1 %collective-permute-done.5.got_3 = f32[8,32,128]{2,1,0:T(8,128)S(1)} collective-permute-done((f32[8,32,128]{2,1,0:T(8,128)S(1)}, f32[8,32,128]{2,1,0:T(8,128)S(1)}, u32[]{:S(2)}, u32[]{:S(2)}) %collective-permute-start.5) | collective-permute-done | bytes 131104 | tf_op jit(solution)/shard_map/ppermute | solution.py:536
  16.8 5.3 %collective-permute-start.7 = (f32[8,136,128]{2,1,0:T(8,128)S(1)}, f32[8,136,128]{2,1,0:T(8,128)S(1)}, u32[]{:S(2)}, u32[]{:S(2)}) collective-permute-start(f32[8,136,128]{2,1,0:T(8,128)S(1)} %get-tuple-element.48.coef.first), channel_id=1, source_target_pairs={{64,32},{32,64},{0,1},{1,0},{33,65},{65,33},{97,98},{98,97},{66,34... | collective-permute-start | bytes 1671176 | tf_op jit(solution)/shard_map/ppermute | solution.py:556
  22.0 3.3 %collective-permute-start.8 = (f32[8,128,128]{2,1,0:T(8,128)S(1)}, f32[8,128,128]{2,1,0:T(8,128)S(1)}, u32[]{:S(2)}, u32[]{:S(2)}) collective-permute-start(f32[8,128,128]{2,1,0:T(8,128)S(1)} %shard_map.55.pot), channel_id=1, source_target_pairs={{64,32},{32,64},{0,1},{1,0},{33,65},{65,33},{97,98},{98,97},{66,34... | collective-permute-start | bytes 1572872 | tf_op jit(solution)/shard_map/ppermute | solution.py:556
  26.0 1.9 %collective-permute-start.6 = (f32[8,224,128]{2,1,0:T(8,128)S(1)}, f32[8,224,128]{2,1,0:T(8,128)S(1)}, u32[]{:S(2)}, u32[]{:S(2)}) collective-permute-start(f32[8,224,128]{2,1,0:T(8,128)S(1)} %shard_map.57), channel_id=1, source_target_pairs={{96,32},{32,1},{1,65},{65,98},{98,34},{34,3},{3,67},{67,4},{4,68},... | collective-permute-start | bytes 2752520 | tf_op jit(solution)/shard_map/ppermute | solution.py:556
  27.9 3.8 %collective-permute-start.10 = (f32[8,136,128]{2,1,0:T(8,128)S(1)}, f32[8,136,128]{2,1,0:T(8,128)S(1)}, u32[]{:S(2)}, u32[]{:S(2)}) collective-permute-start(f32[8,136,128]{2,1,0:T(8,128)S(1)} %get-tuple-element.48.coef.first), channel_id=1, source_target_pairs={{96,64},{64,96},{32,0},{0,32},{1,33},{33,1},{65,97},{97,65},{98,66... | collective-permute-start | bytes 1671176 | tf_op jit(solution)/shard_map/ppermute | solution.py:556
  32.2 7.0 %collective-permute-done.8.pot = f32[8,128,128]{2,1,0:T(8,128)S(1)} collective-permute-done((f32[8,128,128]{2,1,0:T(8,128)S(1)}, f32[8,128,128]{2,1,0:T(8,128)S(1)}, u32[]{:S(2)}, u32[]{:S(2)}) %collective-permute-start.8) | collective-permute-done | bytes 524320 | tf_op jit(solution)/shard_map/ppermute | solution.py:556
  39.2 5.7 %shard_map.58 = (f32[42,112,128]{2,1,0:T(8,128)S(1)}, f32[42,112,128]{2,1,0:T(8,128)S(1)}, f32[40,96,128]{2,1,0:T(8,128)S(1)}, f32[40,96,128]{2,1,0:T(8,128)S(1)...) custom-call(s32[10]{0:T(128)S(1)} %stack.36.scal, ...), custom_call_target="tpu_custom_call" | custom-call | flops 11200000 | bytes 5600000 | tf_op jit(solution)/shard_map/pallas_call | solution.py:479
  44.9 3.8 %shard_map.59 = (f32[42,112,128]{2,1,0:T(8,128)S(1)}, f32[42,112,128]{2,1,0:T(8,128)S(1)}, f32[40,96,128]{2,1,0:T(8,128)S(1)}, f32[40,96,128]{2,1,0:T(8,128)S(1)...) custom-call(s32[10]{0:T(128)S(1)} %stack.36.scal, ...), custom_call_target="tpu_custom_call", output_to_operand_aliasing={{0}: (4, {}), {1}: (5, {}), {2}: (6, {}), {3}: (7, {}), {4}... | custom-call | flops 12800000 | bytes 6400000 | tf_op jit(solution)/shard_map/pallas_call | solution.py:479
  48.7 3.6 %shard_map.60 = (f32[42,112,128]{2,1,0:T(8,128)S(1)}, f32[42,112,128]{2,1,0:T(8,128)S(1)}, f32[40,96,128]{2,1,0:T(8,128)S(1)}, f32[40,96,128]{2,1,0:T(8,128)S(1)...) custom-call(s32[10]{0:T(128)S(1)} %stack.36.scal, ...), custom_call_target="tpu_custom_call", output_to_operand_aliasing={{0}: (3, {}), {1}: (4, {}), {2}: (5, {}), {3}: (6, {}), {4}... | custom-call | flops 12800000 | bytes 6400000 | tf_op jit(solution)/shard_map/pallas_call | solution.py:479
  52.3 8.1 %shard_map.61 = (f32[9,96,128]{2,1,0:T(8,128)S(1)}, f32[42,112,128]{2,1,0:T(8,128)S(1)}, f32[42,112,128]{2,1,0:T(8,128)S(1)}, f32[40,96,128]{2,1,0:T(8,128)S(1)}...) custom-call(s32[10]{0:T(128)S(1)} %stack.36.scal, ...), custom_call_target="tpu_custom_call", output_to_operand_aliasing={{1}: (4, {}), {2}: (5, {}), {3}: (6, {}), {4}: (7, {}), {5}... | custom-call | flops 36800000 | bytes 18400000 | tf_op jit(solution)/shard_map/pallas_call | solution.py:479
  61.2 5.4 %collective-permute-start.15 = (f32[9,96,128]{2,1,0:T(8,128)S(1)}, f32[9,96,128]{2,1,0:T(8,128)S(1)}, u32[]{:S(2)}, u32[]{:S(2)}) collective-permute-start(f32[9,96,128]{2,1,0:T(8,128)S(1)} %get-tuple-element.71.own), channel_id=1, source_target_pairs={{64,32},{32,64},{0,1},{1,0},{33,65},{65,33},{97,98},{98,97},{66,34... | collective-permute-start | bytes 1327112 | tf_op jit(solution)/shard_map/ppermute | solution.py:556
  66.6 1.6 %shard_map.62 = (f32[42,112,128]{2,1,0:T(8,128)S(1)}, f32[42,112,128]{2,1,0:T(8,128)S(1)}, f32[10,48,128]{2,1,0:T(8,128)S(1)}, f32[8,32,128]{2,1,0:T(8,128)S(1)}, f32[8,128,128]{2,1,0:T(8,128)S(1)}) custom-call(s32[10]{0:T(128)S(1)} %stack.36.scal, f32[9,96,128]{2,1,0:T(8,128)S(1)} %get-tuple-element.71.own, f32[9,96,128]{2,1,0:T(8,128)S(1)} %collective-permute-done.13.on, ...), custom_call_target="tpu_custom_call" | custom-call | flops 4000000 | bytes 2000000 | tf_op jit(solution)/shard_map/pallas_call | solution.py:479
  68.2 1.9 %collective-permute-start.14 = (f32[8,128,128]{2,1,0:T(8,128)S(1)}, f32[8,128,128]{2,1,0:T(8,128)S(1)}, u32[]{:S(2)}, u32[]{:S(2)}) collective-permute-start(f32[8,128,128]{2,1,0:T(8,128)S(1)} %get-tuple-element.72), channel_id=1, source_target_pairs={{96,32},{32,1},{1,65},{65,98},{98,34},{34,3},{3,67},{67,4},{4,68},... | collective-permute-start | bytes 1572872 | tf_op jit(solution)/shard_map/ppermute | solution.py:556
  70.1 3.7 %collective-permute-done.15.near = f32[9,96,128]{2,1,0:T(8,128)S(1)} collective-permute-done((f32[9,96,128]{2,1,0:T(8,128)S(1)}, f32[9,96,128]{2,1,0:T(8,128)S(1)}, u32[]{:S(2)}, u32[]{:S(2)}) %collective-permute-start.15) | collective-permute-done | bytes 442400 | tf_op jit(solution)/shard_map/ppermute | solution.py:556
  73.8 2.8 %shard_map.63 = (f32[42,112,128]{2,1,0:T(8,128)S(1)}, f32[42,112,128]{2,1,0:T(8,128)S(1)}) custom-call(s32[10]{0:T(128)S(1)} %stack.36.scal, f32[40,96,128]{2,1,0:T(8,128)S(1)} %get-tuple-element.73.absorb, f32[40,96,128]{2,1,0:T(8,128)S(1)} %get-tuple-element.74.source.refs_2_, ...), custom_call_target="tpu_custom_call", output_to_operand_aliasing={{0}: (3, {}), {1}: (4, {})} | custom-call | flops 11200000 | bytes 5600000 | tf_op jit(solution)/shard_map/pallas_call | solution.py:479
  76.6 2.9 %shard_map.64 = (f32[42,112,128]{2,1,0:T(8,128)S(1)}, f32[42,112,128]{2,1,0:T(8,128)S(1)}, f32[10,48,128]{2,1,0:T(8,128)S(1)}, f32[8,32,128]{2,1,0:T(8,128)S(1)}) custom-call(s32[10]{0:T(128)S(1)} %stack.36.scal, f32[9,96,128]{2,1,0:T(8,128)S(1)} %collective-permute-done.15.near, ...), custom_call_target="tpu_custom_call", output_to_operand_aliasing={{0}: (4, {}), {1}: (5, {}), {2}: (6, {}), {3}: (7, {})} | custom-call | flops 12800000 | bytes 6400000 | tf_op jit(solution)/shard_map/pallas_call | solution.py:479
  79.6 2.8 %shard_map.65 = (f32[42,112,128]{2,1,0:T(8,128)S(1)}, f32[42,112,128]{2,1,0:T(8,128)S(1)}) custom-call(s32[10]{0:T(128)S(1)} %stack.36.scal, f32[9,96,128]{2,1,0:T(8,128)S(1)} %collective-permute-done.16.on2, f32[40,96,128]{2,1,0:T(8,128)S(1)} %get-tuple-element.73.absorb, ...), custom_call_target="tpu_custom_call", output_to_operand_aliasing={{0}: (4, {}), {1}: (5, {})} | custom-call | flops 12800000 | bytes 6400000 | tf_op jit(solution)/shard_map/pallas_call | solution.py:479
  82.4 8.2 %shard_map.66 = (f32[8,32,128]{2,1,0:T(8,128)S(1)}, f32[8,32,128]{2,1,0:T(8,128)S(1)}, f32[8,32,128]{2,1,0:T(8,128)S(1)}, f32[8,32,128]{2,1,0:T(8,128)S(1)}, f32...) custom-call(s32[10]{0:T(128)S(1)} %stack.36.scal, ...), custom_call_target="tpu_custom_call", output_to_operand_aliasing={{4}: (5, {}), {5}: (6, {}), {6}: (7, {}), {7}: (8, {})} | custom-call | flops 36800000 | bytes 18400000 | tf_op jit(solution)/shard_map/pallas_call | solution.py:479
  91.2 1.7 %collective-permute-start.19 = (f32[8,32,128]{2,1,0:T(8,128)S(1)}, f32[8,32,128]{2,1,0:T(8,128)S(1)}, u32[]{:S(2)}, u32[]{:S(2)}) collective-permute-start(f32[8,32,128]{2,1,0:T(8,128)S(1)} %get-tuple-element.90), channel_id=1, source_target_pairs={{0,96},{32,64},{64,32},{96,0},{1,97},{33,65},{65,33},{97,1},{2,98}... | collective-permute-start | bytes 393224 | tf_op jit(solution)/shard_map/ppermute | solution.py:609
  92.9 3.2 %collective-permute-done.18.got_2 = f32[8,32,128]{2,1,0:T(8,128)S(1)} collective-permute-done((f32[8,32,128]{2,1,0:T(8,128)S(1)}, f32[8,32,128]{2,1,0:T(8,128)S(1)}, u32[]{:S(2)}, u32[]{:S(2)}) %collective-permute-start.18) | collective-permute-done | bytes 131104 | tf_op jit(solution)/shard_map/ppermute | solution.py:609
  96.2 3.1 %collective-permute-done.19.got_3 = f32[8,32,128]{2,1,0:T(8,128)S(1)} collective-permute-done((f32[8,32,128]{2,1,0:T(8,128)S(1)}, f32[8,32,128]{2,1,0:T(8,128)S(1)}, u32[]{:S(2)}, u32[]{:S(2)}) %collective-permute-start.19) | collective-permute-done | bytes 131104 | tf_op jit(solution)/shard_map/ppermute | solution.py:609
  (36 shorter events, 10.8 us)
Async XLA Ops:
  0.0 15.6 %copy-start = (f32[32,32,128]{2,1,0:T(8,128)S(1)}, f32[32,32,128]{2,1,0:T(8,128)}, u32[]{:S(2)}) copy-start(f32[32,32,128]{2,1,0:T(8,128)} %rec.1) | copy-start | bytes 1572868
  0.0 15.6 %copy-start.1 = (s32[32,32,128]{2,1,0:T(8,128)S(1)}, s32[32,32,128]{2,1,0:T(8,128)}, u32[]{:S(2)}) copy-start(s32[32,32,128]{2,1,0:T(8,128)} %exc.1) | copy-start | bytes 1572868
  1.2 4.0 %collective-permute-start = (f32[8,32,128]{2,1,0:T(8,128)S(1)}, f32[8,32,128]{2,1,0:T(8,128)S(1)}, u32[]{:S(2)}, u32[]{:S(2)}) collective-permute-start(f32[8,32,128]{2,1,0:T(8,128)S(1)} %get-tuple-element.96), channel_id=1, source_target_pairs={{0,32},{32,0},{64,96},{96,64},{1,33},{33,1},{65,97},{97,65},{2,34}... | collective-permute-start | bytes 393224 | tf_op jit(solution)/shard_map/ppermute | solution.py:536
  2.0 5.8 %collective-permute-start.1 = (f32[8,32,128]{2,1,0:T(8,128)S(1)}, f32[8,32,128]{2,1,0:T(8,128)S(1)}, u32[]{:S(2)}, u32[]{:S(2)}) collective-permute-start(f32[8,32,128]{2,1,0:T(8,128)S(1)} %get-tuple-element.98), channel_id=1, source_target_pairs={{0,64},{32,96},{64,0},{96,32},{1,65},{33,97},{65,1},{97,33},{2,66}... | collective-permute-start | bytes 393224 | tf_op jit(solution)/shard_map/ppermute | solution.py:536
  2.1 8.4 %collective-permute-start.2 = (f32[8,32,128]{2,1,0:T(8,128)S(1)}, f32[8,32,128]{2,1,0:T(8,128)S(1)}, u32[]{:S(2)}, u32[]{:S(2)}) collective-permute-start(f32[8,32,128]{2,1,0:T(8,128)S(1)} %get-tuple-element.95), channel_id=1, source_target_pairs={{0,96},{32,64},{64,32},{96,0},{1,97},{33,65},{65,33},{97,1},{2,98}... | collective-permute-start | bytes 393224 | tf_op jit(solution)/shard_map/ppermute | solution.py:536
  4.8 6.4 %collective-permute-start.3 = (f32[8,32,128]{2,1,0:T(8,128)S(1)}, f32[8,32,128]{2,1,0:T(8,128)S(1)}, u32[]{:S(2)}, u32[]{:S(2)}) collective-permute-start(f32[8,32,128]{2,1,0:T(8,128)S(1)} %get-tuple-element.92), channel_id=1, source_target_pairs={{0,32},{32,0},{64,96},{96,64},{1,33},{33,1},{65,97},{97,65},{2,34}... | collective-permute-start | bytes 393224 | tf_op jit(solution)/shard_map/ppermute | solution.py:536
  5.1 7.5 %collective-permute-start.4 = (f32[8,32,128]{2,1,0:T(8,128)S(1)}, f32[8,32,128]{2,1,0:T(8,128)S(1)}, u32[]{:S(2)}, u32[]{:S(2)}) collective-permute-start(f32[8,32,128]{2,1,0:T(8,128)S(1)} %get-tuple-element.94), channel_id=1, source_target_pairs={{0,64},{32,96},{64,0},{96,32},{1,65},{33,97},{65,1},{97,33},{2,66}... | collective-permute-start | bytes 393224 | tf_op jit(solution)/shard_map/ppermute | solution.py:536
  5.2 10.4 %collective-permute-start.5 = (f32[8,32,128]{2,1,0:T(8,128)S(1)}, f32[8,32,128]{2,1,0:T(8,128)S(1)}, u32[]{:S(2)}, u32[]{:S(2)}) collective-permute-start(f32[8,32,128]{2,1,0:T(8,128)S(1)} %get-tuple-element.91), channel_id=1, source_target_pairs={{0,96},{32,64},{64,32},{96,0},{1,97},{33,65},{65,33},{97,1},{2,98}... | collective-permute-start | bytes 393224 | tf_op jit(solution)/shard_map/ppermute | solution.py:536
  16.8 15.0 %collective-permute-start.7 = (f32[8,136,128]{2,1,0:T(8,128)S(1)}, f32[8,136,128]{2,1,0:T(8,128)S(1)}, u32[]{:S(2)}, u32[]{:S(2)}) collective-permute-start(f32[8,136,128]{2,1,0:T(8,128)S(1)} %get-tuple-element.48.coef.first), channel_id=1, source_target_pairs={{64,32},{32,64},{0,1},{1,0},{33,65},{65,33},{97,98},{98,97},{66,34... | collective-permute-start | bytes 1671176 | tf_op jit(solution)/shard_map/ppermute | solution.py:556
  22.0 17.2 %collective-permute-start.8 = (f32[8,128,128]{2,1,0:T(8,128)S(1)}, f32[8,128,128]{2,1,0:T(8,128)S(1)}, u32[]{:S(2)}, u32[]{:S(2)}) collective-permute-start(f32[8,128,128]{2,1,0:T(8,128)S(1)} %shard_map.55.pot), channel_id=1, source_target_pairs={{64,32},{32,64},{0,1},{1,0},{33,65},{65,33},{97,98},{98,97},{66,34... | collective-permute-start | bytes 1572872 | tf_op jit(solution)/shard_map/ppermute | solution.py:556
  26.0 26.3 %collective-permute-start.6 = (f32[8,224,128]{2,1,0:T(8,128)S(1)}, f32[8,224,128]{2,1,0:T(8,128)S(1)}, u32[]{:S(2)}, u32[]{:S(2)}) collective-permute-start(f32[8,224,128]{2,1,0:T(8,128)S(1)} %shard_map.57), channel_id=1, source_target_pairs={{96,32},{32,1},{1,65},{65,98},{98,34},{34,3},{3,67},{67,4},{4,68},... | collective-permute-start | bytes 2752520 | tf_op jit(solution)/shard_map/ppermute | solution.py:556
  27.9 11.3 %collective-permute-start.10 = (f32[8,136,128]{2,1,0:T(8,128)S(1)}, f32[8,136,128]{2,1,0:T(8,128)S(1)}, u32[]{:S(2)}, u32[]{:S(2)}) collective-permute-start(f32[8,136,128]{2,1,0:T(8,128)S(1)} %get-tuple-element.48.coef.first), channel_id=1, source_target_pairs={{96,64},{64,96},{32,0},{0,32},{1,33},{33,1},{65,97},{97,65},{98,66... | collective-permute-start | bytes 1671176 | tf_op jit(solution)/shard_map/ppermute | solution.py:556
  31.7 16.9 %collective-permute-start.12 = (f32[8,136,128]{2,1,0:T(8,128)S(1)}, f32[8,136,128]{2,1,0:T(8,128)S(1)}, u32[]{:S(2)}, u32[]{:S(2)}) collective-permute-start(f32[8,136,128]{2,1,0:T(8,128)S(1)} %collective-permute-done.7.coef.near), channel_id=1, source_target_pairs={{96,64},{64,96},{32,0},{0,32},{1,33},{33,1},{65,97},{97,65},{98,66... | collective-permute-start | bytes 1671176 | tf_op jit(solution)/shard_map/ppermute | solution.py:556
  31.8 7.4 %collective-permute-start.9 = (f32[8,128,128]{2,1,0:T(8,128)S(1)}, f32[8,128,128]{2,1,0:T(8,128)S(1)}, u32[]{:S(2)}, u32[]{:S(2)}) collective-permute-start(f32[8,128,128]{2,1,0:T(8,128)S(1)} %shard_map.55.pot), channel_id=1, source_target_pairs={{96,64},{64,96},{32,0},{0,32},{1,33},{33,1},{65,97},{97,65},{98,66... | collective-permute-start | bytes 1572872 | tf_op jit(solution)/shard_map/ppermute | solution.py:556
  39.2 9.5 %collective-permute-start.11 = (f32[8,128,128]{2,1,0:T(8,128)S(1)}, f32[8,128,128]{2,1,0:T(8,128)S(1)}, u32[]{:S(2)}, u32[]{:S(2)}) collective-permute-start(f32[8,128,128]{2,1,0:T(8,128)S(1)} %collective-permute-done.8.pot), channel_id=1, source_target_pairs={{96,64},{64,96},{32,0},{0,32},{1,33},{33,1},{65,97},{97,65},{98,66... | collective-permute-start | bytes 1572872 | tf_op jit(solution)/shard_map/ppermute | solution.py:556
  60.4 6.2 %collective-permute-start.13 = (f32[9,96,128]{2,1,0:T(8,128)S(1)}, f32[9,96,128]{2,1,0:T(8,128)S(1)}, u32[]{:S(2)}, u32[]{:S(2)}) collective-permute-start(f32[9,96,128]{2,1,0:T(8,128)S(1)} %get-tuple-element.71.own), channel_id=1, source_target_pairs={{96,64},{64,96},{32,0},{0,32},{1,33},{33,1},{65,97},{97,65},{98,66... | collective-permute-start | bytes 1327112 | tf_op jit(solution)/shard_map/ppermute | solution.py:556
  61.2 12.6 %collective-permute-start.15 = (f32[9,96,128]{2,1,0:T(8,128)S(1)}, f32[9,96,128]{2,1,0:T(8,128)S(1)}, u32[]{:S(2)}, u32[]{:S(2)}) collective-permute-start(f32[9,96,128]{2,1,0:T(8,128)S(1)} %get-tuple-element.71.own), channel_id=1, source_target_pairs={{64,32},{32,64},{0,1},{1,0},{33,65},{65,33},{97,98},{98,97},{66,34... | collective-permute-start | bytes 1327112 | tf_op jit(solution)/shard_map/ppermute | solution.py:556
  68.2 14.2 %collective-permute-start.14 = (f32[8,128,128]{2,1,0:T(8,128)S(1)}, f32[8,128,128]{2,1,0:T(8,128)S(1)}, u32[]{:S(2)}, u32[]{:S(2)}) collective-permute-start(f32[8,128,128]{2,1,0:T(8,128)S(1)} %get-tuple-element.72), channel_id=1, source_target_pairs={{96,32},{32,1},{1,65},{65,98},{98,34},{34,3},{3,67},{67,4},{4,68},... | collective-permute-start | bytes 1572872 | tf_op jit(solution)/shard_map/ppermute | solution.py:556
  73.8 5.8 %collective-permute-start.16 = (f32[9,96,128]{2,1,0:T(8,128)S(1)}, f32[9,96,128]{2,1,0:T(8,128)S(1)}, u32[]{:S(2)}, u32[]{:S(2)}) collective-permute-start(f32[9,96,128]{2,1,0:T(8,128)S(1)} %collective-permute-done.15.near), channel_id=1, source_target_pairs={{96,64},{64,96},{32,0},{0,32},{1,33},{33,1},{65,97},{97,65},{98,66... | collective-permute-start | bytes 1327112 | tf_op jit(solution)/shard_map/ppermute | solution.py:556
  90.6 2.3 %collective-permute-start.17 = (f32[8,32,128]{2,1,0:T(8,128)S(1)}, f32[8,32,128]{2,1,0:T(8,128)S(1)}, u32[]{:S(2)}, u32[]{:S(2)}) collective-permute-start(f32[8,32,128]{2,1,0:T(8,128)S(1)} %get-tuple-element.88), channel_id=1, source_target_pairs={{0,32},{32,0},{64,96},{96,64},{1,33},{33,1},{65,97},{97,65},{2,34}... | collective-permute-start | bytes 393224 | tf_op jit(solution)/shard_map/ppermute | solution.py:609
  91.2 5.0 %collective-permute-start.18 = (f32[8,32,128]{2,1,0:T(8,128)S(1)}, f32[8,32,128]{2,1,0:T(8,128)S(1)}, u32[]{:S(2)}, u32[]{:S(2)}) collective-permute-start(f32[8,32,128]{2,1,0:T(8,128)S(1)} %get-tuple-element.89), channel_id=1, source_target_pairs={{0,64},{32,96},{64,0},{96,32},{1,65},{33,97},{65,1},{97,33},{2,66}... | collective-permute-start | bytes 393224 | tf_op jit(solution)/shard_map/ppermute | solution.py:609
  91.2 8.0 %collective-permute-start.19 = (f32[8,32,128]{2,1,0:T(8,128)S(1)}, f32[8,32,128]{2,1,0:T(8,128)S(1)}, u32[]{:S(2)}, u32[]{:S(2)}) collective-permute-start(f32[8,32,128]{2,1,0:T(8,128)S(1)} %get-tuple-element.90), channel_id=1, source_target_pairs={{0,96},{32,64},{64,32},{96,0},{1,97},{33,65},{65,33},{97,1},{2,98}... | collective-permute-start | bytes 393224 | tf_op jit(solution)/shard_map/ppermute | solution.py:609

commit v8 on v7

--- a/solution.py
+++ b/solution.py
@@ -33,21 +33,20 @@
 V_PAD = 48
 
 
-def chebyshev_weights(count):
-    center = 0.5 * (spectrum_high + spectrum_low)
-    spread = 0.5 * (spectrum_high - spectrum_low)
-    ratio = center / spread
-    current = 1.0 / ratio
-    weights = [(0.0, 1.0 / center)]
-    for _ in range(count):
-        following = 1.0 / (2.0 * ratio - current)
-        weights.append((following * current, 2.0 * following / spread))
-        current = following
-    return weights
-
-
-WEIGHTS = chebyshev_weights(SWEEPS - 1)
-SHIFT = 6.0 - 0.5 * (spectrum_high + spectrum_low)
+CENTER = 0.5 * (spectrum_high + spectrum_low)
+SPREAD = 0.5 * (spectrum_high - spectrum_low)
+
+
+def chebyshev_polynomials(count):
+    ratio = CENTER / SPREAD
+    values = [1.0, ratio]
+    while len(values) <= count:
+        values.append(2.0 * ratio * values[-1] - values[-2])
+    return values
+
+
+SCALES = chebyshev_polynomials(SWEEPS)
+SHIFT = 6.0 - CENTER
 
 
 def ionic(voltage, recovery, threshold, active):
@@ -103,12 +102,18 @@
     return high, (value - high.astype(jnp.float32)).astype(jnp.bfloat16)
 
 
-def sweep(scal, plan, even, odd, absorb, source):
+def sweep(scal, plan, even, odd, absorb, source, rows):
     accs = [pltpu.ACC(part % 2)((PART, 256), jnp.float32) for part in range(2 * PARTS)]
-    pl.run_scoped(lambda *refs: sweep_with(scal, plan, even, odd, absorb, source, refs), *accs)
-
-
-def sweep_with(scal, plan, even, odd, absorb, source, accs):
+    pl.run_scoped(
+        lambda *refs: sweep_with(scal, plan, even, odd, absorb, source, rows, refs), *accs
+    )
+
+
+def row_mark(ref):
+    return jnp.max(ref[0, ROW_AT : ROW_AT + 8]).astype(jnp.int32)
+
+
+def sweep_with(scal, plan, even, odd, absorb, source, rows, accs):
     accs = (accs[:PARTS], accs[PARTS:])
     low_end, high_end = scal[4], scal[5]
     row = lax.broadcasted_iota(jnp.int32, (256, 256), 0)
@@ -135,10 +140,23 @@
             return x + (skip if 2 * pair >= size else 0)
         return x + jnp.where(2 * pair >= size, skip, 0)
 
+    def weight(level, x):
+        inside = (x >= low_end) & (x < high_end)
+        push = (1.0 if level == 1 else 2.0) / SPREAD
+        return jnp.where(inside, push, 0.0).astype(jnp.float32)
+
     def begin(number, pair, acc):
         level = plan[number][0]
-        src = even if level % 2 else odd
-        x = place(number, pair) + OFF
+        src, dst = (even, odd) if level % 2 else (odd, even)
+        x = place(number, pair)
+        if level > 1:
+            for plane in range(2):
+                here = x + plane
+                at = pl.multiple_of(rows(here) * HEART, HEART)
+                to = pl.multiple_of(rows(here) * HEART + PAD, PAD)
+                part = weight(level, here) * SCALES[level - 1] * source[here, pl.ds(at, HEART)]
+                dst[here + OFF, pl.ds(to, HEART)] = dst[here + OFF, pl.ds(to, HEART)] - part
+        x = x + OFF
         for part in range(PARTS):
             at, to = PAD + PART * part, PAD + PART * (part + 1)
             high_0, low_0 = halves(src[x, at:to])
@@ -150,11 +168,7 @@
         level = plan[number][0]
         src, dst = (even, odd) if level % 2 else (odd, even)
         x = place(number, pair)
-        keeps, pushes = [], []
-        for plane in range(2):
-            inside = (x + plane >= low_end) & (x + plane < high_end)
-            keeps.append(jnp.where(inside, WEIGHTS[level - 1][0], 0.0).astype(jnp.float32))
-            pushes.append(jnp.where(inside, WEIGHTS[level - 1][1], 0.0).astype(jnp.float32))
+        pushes = [weight(level, x + plane) for plane in range(2)]
         for part in range(PARTS):
             start, stop = PART * part, PART * (part + 1)
             at, to = PAD + start, PAD + stop
@@ -163,11 +177,12 @@
                 here = x + plane
                 total = src[here + OFF - 1 + 2 * plane, at:to]
                 total = total + (src[here + OFF, at - 1 : to - 1] + src[here + OFF, at + 1 : to + 1])
-                total = total + source[here, start:stop]
+                if level == 1:
+                    total = total + source[here, start:stop]
                 total = total - absorb[here, start:stop] * src[here + OFF, at:to]
                 total = pushes[plane] * (total + sums[:, 128 * plane : 128 * (plane + 1)])
                 if level > 1:
-                    total = total - keeps[plane] * dst[here + OFF, at:to]
+                    total = total - dst[here + OFF, at:to]
                 dst[here + OFF, at:to] = total
 
     one, other = accs
@@ -340,7 +355,7 @@
     row = jnp.full((1, 128), scal[3].astype(jnp.float32))
     embed(OWN + 1, END - 1, row, (volt, source), (volt_1, later))
     couple(1, SLAB, scal[3], even, volt_1, aux, held)
-    sweep(scal, INNER, even, odd, absorb, source)
+    sweep(scal, INNER, even, odd, absorb, source, lambda x: scal[3])
 
 
 def first_left(scal, pot, coef, aux, *refs):
@@ -357,7 +372,8 @@
     embed(SLAB + 1, OWN, coef[0, ROW_AT : ROW_AT + 1], *fields)
     embed(OWN, OWN + 1, row, *fields)
     couple(0, 1, scal[3], even, volt_1, aux, held)
-    sweep(scal, LEFT, even, odd, absorb, source)
+    near_row = row_mark(coef)
+    sweep(scal, LEFT, even, odd, absorb, source, lambda x: jnp.where(x < OWN, near_row, scal[3]))
 
 
 def first_right(scal, pot, coef, *refs):
@@ -373,16 +389,18 @@
     fields = ((volt, source), (volt_1, later))
     embed(END - 1, END, row, *fields)
     embed(END, SLOTS - 1, coef[0, ROW_AT : ROW_AT + 1], *fields)
-    sweep(scal, RIGHT, even, odd, absorb, source)
+    far_row = row_mark(coef)
+    sweep(scal, RIGHT, even, odd, absorb, source, lambda x: jnp.where(x < END, scal[3], far_row))
 
 
 def first_outer(scal, far, near, held, *refs):
     msg, even, odd, absorb, source, volt = refs[5:]
     take_first(far, far, POT_ROWS, 0, 1, even, absorb, volt)
     embed(1, SLAB + 1, near[0, ROW_AT : ROW_AT + 1], (volt, source))
-    sweep(scal, OUTER, even, odd, absorb, source)
+    near_row = row_mark(near)
+    sweep(scal, OUTER, even, odd, absorb, source, lambda x: jnp.where(x < OWN, near_row, scal[3]))
     for u in range(SLAB):
-        msg[u] = even[OFF + OWN + u, PAD : PAD + ROWS]
+        msg[u] = even[OFF + OWN + u, PAD : PAD + ROWS] * (1.0 / SCALES[SWEEPS])
     msg[SLAB, 0:HEART] = held[0]
     msg[SLAB, HEART : 2 * HEART] = held[SLAB - 1]
     msg[SLAB, 2 * HEART : ROWS] = jnp.zeros((HEART, 128), jnp.float32)
@@ -405,10 +423,10 @@
 
 def second_inner(scal, absorb, source, *refs):
     even, odd = refs[2:]
-    sweep(scal, INNER, even, odd, absorb, source)
-
-
-def second_left(scal, near, absorb, source, *refs):
+    sweep(scal, INNER, even, odd, absorb, source, lambda x: scal[3])
+
+
+def second_left(scal, near, mark, absorb, source, *refs):
     even, odd, volt, out = refs[4:]
     take(near, OWN - 1, -1, even)
     put_heart(volt, 0, near[SLAB, 0:HEART])
@@ -418,13 +436,15 @@
         volt[0] = volt[1]
 
     settle(0, 1, scal[3], even, volt, out)
-    sweep(scal, LEFT, even, odd, absorb, source)
-
-
-def second_right(scal, on2, absorb, source, *refs):
+    near_row = row_mark(mark)
+    sweep(scal, LEFT, even, odd, absorb, source, lambda x: jnp.where(x < OWN, near_row, scal[3]))
+
+
+def second_right(scal, on2, mark, absorb, source, *refs):
     even, odd = refs[2:]
     take(on2, END, 1, even)
-    sweep(scal, RIGHT, even, odd, absorb, source)
+    far_row = row_mark(mark)
+    sweep(scal, RIGHT, even, odd, absorb, source, lambda x: jnp.where(x < END, scal[3], far_row))
 
 
 def second_outer(scal, far, near, absorb, voltage, *refs):
@@ -437,11 +457,12 @@
 
     lax.fori_loop(0, SLAB, plane, 0)
     embed(1, SLAB + 1, near[0, ROW_AT : ROW_AT + 1], (volt_1, source))
-    sweep(scal, OUTER, even, odd, absorb, source)
+    near_row = row_mark(near)
+    sweep(scal, OUTER, even, odd, absorb, source, lambda x: jnp.where(x < OWN, near_row, scal[3]))
     sec, flip = scal[0], scal[2]
 
     def give(u, carry):
-        joined[u, 0:ROWS] = even[OFF + OWN + u, PAD : PAD + ROWS]
+        joined[u, 0:ROWS] = even[OFF + OWN + u, PAD : PAD + ROWS] * (1.0 / SCALES[SWEEPS])
         joined[u, ROWS : ROWS + HEART] = voltage[u]
         x = jnp.where(flip == 1, SLAB - 1 - u, u)
         for number in range(4):
@@ -452,11 +473,15 @@
     lax.fori_loop(0, SLAB, give, 0)
 
 
-def spread_kernel(scal, own, got_1, got_2, got_3, out):
+def spread_kernel(scal, own, got_1, got_2, got_3, out, done):
+    copies = []
     for number, ref in enumerate((own, got_1, got_2, got_3)):
-        at = scal[6 + number] * SLAB
-        for u in range(SLAB):
-            out[at + u] = ref[u]
+        at = pl.ds(pl.multiple_of(scal[6 + number] * SLAB, SLAB), SLAB)
+        copies.append(pltpu.make_async_copy(ref, out.at[at], done.at[number]))
+    for copy in copies:
+        copy.start()
+    for copy in copies:
+        copy.wait()
 
 
 def chain(sections, bricks):
@@ -593,9 +618,13 @@
     even, odd = call(second_inner, (scal, absorb, later), [], 56, state=[even, odd])
     on2 = move(near, partner)
     even, odd, _, voltage = call(
-        second_left, (scal, near, absorb, later), [], 64, state=[even, odd, volt_2, voltage]
-    )
-    even, odd = call(second_right, (scal, on2, absorb, later), [], 64, state=[even, odd])
+        second_left,
+        (scal, near, near_coef, absorb, later),
+        [],
+        64,
+        state=[even, odd, volt_2, voltage],
+    )
+    even, odd = call(second_right, (scal, on2, on2_coef, absorb, later), [], 64, state=[even, odd])
     outs = call(
         second_outer,
         (scal, far, near_coef, absorb, voltage),
@@ -607,7 +636,15 @@
     back = [outs[0]]
     for number in (1, 2, 3):
         back.append(lax.ppermute(outs[number], "sec", across(number)))
-    (result,) = call(spread_kernel, (scal, *back), [(sections * SLAB, HEART, 128)], 5)
+    result = pl.pallas_call(
+        spread_kernel,
+        out_shape=jax.ShapeDtypeStruct((sections * SLAB, HEART, 128), jnp.float32),
+        in_specs=[SMEM] + [VMEM] * 4,
+        out_specs=pl.BlockSpec(memory_space=pl.ANY),
+        scratch_shapes=[pltpu.SemaphoreType.DMA((4,))],
+        compiler_params=pltpu.CompilerParams(vmem_limit_bytes=20 << 20),
+        name="spread",
+    )(scal, *back)
     return result[None]
 
 

time: 101 us -> 108 us (1.069)
  Pallas kernels: 43.2 us -> 49.9 us
    pallas_call x13 -> x12, Pallas kernels: 43.2 us -> 48.6 us  [call(): pl.pallas_call(kernel, out_shape=arrays, in_specs=[SMEM] + [VMEM] * (len(...]
    pallas_call x0 -> x1, Pallas kernels: none -> 1.36 us  [body(): pl.pallas_call(spread_kernel, out_shape=jax.ShapeDtypeStruct((sections *...]
  transfers between devices with their start and end apart: 20 -> 20, of which waited for: 7 -> 7; matrix products, arithmetic and copies ran while one was open for 1% -> 1% of each run, Pallas kernels for 24% -> 27%
where the time goes in v8:
time: 108 us; the launch traced here: 107 us
  Pallas kernels  49.9 us (46%)
  starting transfers between devices  29.8 us (28%)
  waiting for transfers between devices  24.1 us (22%)
  local copies, waits for them, and re-layouts  2.44 us (2%)
    pallas_call x12, Pallas kernels, call(): pl.pallas_call(kernel, out_shape=arrays, in_specs=[SMEM] + [VMEM] * (len(...  48.6 us
    ppermute x11, starting transfers between devices, move(): return lax.ppermute(value, AXES, pairs)  22.7 us
    ppermute x11, waiting for transfers between devices, move(): return lax.ppermute(value, AXES, pairs)  10.6 us
    ppermute x6, waiting for transfers between devices, swapped(): got.append(lax.ppermute(piece, 'sec', across(number)))  7.15 us
    ppermute x3, waiting for transfers between devices, body(): back.append(lax.ppermute(outs[number], 'sec', across(number)))  6.31 us
    ppermute x6, starting transfers between devices, swapped(): got.append(lax.ppermute(piece, 'sec', across(number)))  4.7 us
    dynamic_slice x2, local copies, waits for them, and re-layouts, swapped(): lax.dynamic_slice_in_dim(value, SLAB * chunk_of(sec ^ number), SLAB, 0)  2.34 us
    ppermute x3, starting transfers between devices, body(): back.append(lax.ppermute(outs[number], 'sec', across(number)))  2.32 us
  transfers between devices with their start and end apart: 20, of which 7 were waited for; matrix products, arithmetic and copies ran while one was open for 1% of the time, Pallas kernels for 27%

profile of v8, /device:TPU:105, one launch (start us, length us, event | category | flops | bytes accessed | tf_op | source)
XLA Modules:
  0.0 107.3 jit_solution(2557287204194589663)
XLA Ops:
  2.1 1.6 %collective-permute-start.2 = (f32[8,32,128]{2,1,0:T(8,128)S(1)}, f32[8,32,128]{2,1,0:T(8,128)S(1)}, u32[]{:S(2)}, u32[]{:S(2)}) collective-permute-start(f32[8,32,128]{2,1,0:T(8,128)S(1)} %get-tuple-element.95), channel_id=1, source_target_pairs={{0,96},{32,64},{64,32},{96,0},{1,97},{33,65},{65,33},{97,1},{2,98}... | collective-permute-start | bytes 393224 | tf_op jit(solution)/shard_map/ppermute | solution.py:561
  5.2 1.8 %collective-permute-start.5 = (f32[8,32,128]{2,1,0:T(8,128)S(1)}, f32[8,32,128]{2,1,0:T(8,128)S(1)}, u32[]{:S(2)}, u32[]{:S(2)}) collective-permute-start(f32[8,32,128]{2,1,0:T(8,128)S(1)} %get-tuple-element.91), channel_id=1, source_target_pairs={{0,96},{32,64},{64,32},{96,0},{1,97},{33,65},{65,33},{97,1},{2,98}... | collective-permute-start | bytes 393224 | tf_op jit(solution)/shard_map/ppermute | solution.py:561
  7.8 2.7 %collective-permute-done.2.got_3 = f32[8,32,128]{2,1,0:T(8,128)S(1)} collective-permute-done((f32[8,32,128]{2,1,0:T(8,128)S(1)}, f32[8,32,128]{2,1,0:T(8,128)S(1)}, u32[]{:S(2)}, u32[]{:S(2)}) %collective-permute-start.2) | collective-permute-done | bytes 131104 | tf_op jit(solution)/shard_map/ppermute | solution.py:561
  12.6 3.1 %collective-permute-done.5.got_3 = f32[8,32,128]{2,1,0:T(8,128)S(1)} collective-permute-done((f32[8,32,128]{2,1,0:T(8,128)S(1)}, f32[8,32,128]{2,1,0:T(8,128)S(1)}, u32[]{:S(2)}, u32[]{:S(2)}) %collective-permute-start.5) | collective-permute-done | bytes 131104 | tf_op jit(solution)/shard_map/ppermute | solution.py:561
  16.8 5.3 %collective-permute-start.7 = (f32[8,136,128]{2,1,0:T(8,128)S(1)}, f32[8,136,128]{2,1,0:T(8,128)S(1)}, u32[]{:S(2)}, u32[]{:S(2)}) collective-permute-start(f32[8,136,128]{2,1,0:T(8,128)S(1)} %get-tuple-element.48.coef.first), channel_id=1, source_target_pairs={{64,32},{32,64},{0,1},{1,0},{33,65},{65,33},{97,98},{98,97},{66,34... | collective-permute-start | bytes 1671176 | tf_op jit(solution)/shard_map/ppermute | solution.py:581
  22.0 3.3 %collective-permute-start.8 = (f32[8,128,128]{2,1,0:T(8,128)S(1)}, f32[8,128,128]{2,1,0:T(8,128)S(1)}, u32[]{:S(2)}, u32[]{:S(2)}) collective-permute-start(f32[8,128,128]{2,1,0:T(8,128)S(1)} %shard_map.55.pot), channel_id=1, source_target_pairs={{64,32},{32,64},{0,1},{1,0},{33,65},{65,33},{97,98},{98,97},{66,34... | collective-permute-start | bytes 1572872 | tf_op jit(solution)/shard_map/ppermute | solution.py:581
  26.0 1.9 %collective-permute-start.6 = (f32[8,224,128]{2,1,0:T(8,128)S(1)}, f32[8,224,128]{2,1,0:T(8,128)S(1)}, u32[]{:S(2)}, u32[]{:S(2)}) collective-permute-start(f32[8,224,128]{2,1,0:T(8,128)S(1)} %shard_map.57), channel_id=1, source_target_pairs={{96,32},{32,1},{1,65},{65,98},{98,34},{34,3},{3,67},{67,4},{4,68},... | collective-permute-start | bytes 2752520 | tf_op jit(solution)/shard_map/ppermute | solution.py:581
  27.9 3.8 %collective-permute-start.10 = (f32[8,136,128]{2,1,0:T(8,128)S(1)}, f32[8,136,128]{2,1,0:T(8,128)S(1)}, u32[]{:S(2)}, u32[]{:S(2)}) collective-permute-start(f32[8,136,128]{2,1,0:T(8,128)S(1)} %get-tuple-element.48.coef.first), channel_id=1, source_target_pairs={{96,64},{64,96},{32,0},{0,32},{1,33},{33,1},{65,97},{97,65},{98,66... | collective-permute-start | bytes 1671176 | tf_op jit(solution)/shard_map/ppermute | solution.py:581
  32.2 7.0 %collective-permute-done.8.pot = f32[8,128,128]{2,1,0:T(8,128)S(1)} collective-permute-done((f32[8,128,128]{2,1,0:T(8,128)S(1)}, f32[8,128,128]{2,1,0:T(8,128)S(1)}, u32[]{:S(2)}, u32[]{:S(2)}) %collective-permute-start.8) | collective-permute-done | bytes 524320 | tf_op jit(solution)/shard_map/ppermute | solution.py:581
  39.2 5.9 %shard_map.58 = (f32[42,112,128]{2,1,0:T(8,128)S(1)}, f32[42,112,128]{2,1,0:T(8,128)S(1)}, f32[40,96,128]{2,1,0:T(8,128)S(1)}, f32[40,96,128]{2,1,0:T(8,128)S(1)...) custom-call(s32[10]{0:T(128)S(1)} %stack.36.scal, ...), custom_call_target="tpu_custom_call" | custom-call | flops 11200000 | bytes 5600000 | tf_op jit(solution)/shard_map/pallas_call | solution.py:504
  45.1 4.7 %shard_map.59 = (f32[42,112,128]{2,1,0:T(8,128)S(1)}, f32[42,112,128]{2,1,0:T(8,128)S(1)}, f32[40,96,128]{2,1,0:T(8,128)S(1)}, f32[40,96,128]{2,1,0:T(8,128)S(1)...) custom-call(s32[10]{0:T(128)S(1)} %stack.36.scal, ...), custom_call_target="tpu_custom_call", output_to_operand_aliasing={{0}: (4, {}), {1}: (5, {}), {2}: (6, {}), {3}: (7, {}), {4}... | custom-call | flops 12800000 | bytes 6400000 | tf_op jit(solution)/shard_map/pallas_call | solution.py:504
  49.8 4.7 %shard_map.60 = (f32[42,112,128]{2,1,0:T(8,128)S(1)}, f32[42,112,128]{2,1,0:T(8,128)S(1)}, f32[40,96,128]{2,1,0:T(8,128)S(1)}, f32[40,96,128]{2,1,0:T(8,128)S(1)...) custom-call(s32[10]{0:T(128)S(1)} %stack.36.scal, ...), custom_call_target="tpu_custom_call", output_to_operand_aliasing={{0}: (3, {}), {1}: (4, {}), {2}: (5, {}), {3}: (6, {}), {4}... | custom-call | flops 12800000 | bytes 6400000 | tf_op jit(solution)/shard_map/pallas_call | solution.py:504
  54.5 9.2 %shard_map.61 = (f32[9,96,128]{2,1,0:T(8,128)S(1)}, f32[42,112,128]{2,1,0:T(8,128)S(1)}, f32[42,112,128]{2,1,0:T(8,128)S(1)}, f32[40,96,128]{2,1,0:T(8,128)S(1)}...) custom-call(s32[10]{0:T(128)S(1)} %stack.36.scal, ...), custom_call_target="tpu_custom_call", output_to_operand_aliasing={{1}: (4, {}), {2}: (5, {}), {3}: (6, {}), {4}: (7, {}), {5}... | custom-call | flops 36800000 | bytes 18400000 | tf_op jit(solution)/shard_map/pallas_call | solution.py:504
  64.3 5.4 %collective-permute-start.15 = (f32[9,96,128]{2,1,0:T(8,128)S(1)}, f32[9,96,128]{2,1,0:T(8,128)S(1)}, u32[]{:S(2)}, u32[]{:S(2)}) collective-permute-start(f32[9,96,128]{2,1,0:T(8,128)S(1)} %get-tuple-element.71.own), channel_id=1, source_target_pairs={{64,32},{32,64},{0,1},{1,0},{33,65},{65,33},{97,98},{98,97},{66,34... | collective-permute-start | bytes 1327112 | tf_op jit(solution)/shard_map/ppermute | solution.py:581
  69.7 1.6 %shard_map.62 = (f32[42,112,128]{2,1,0:T(8,128)S(1)}, f32[42,112,128]{2,1,0:T(8,128)S(1)}, f32[10,48,128]{2,1,0:T(8,128)S(1)}, f32[8,32,128]{2,1,0:T(8,128)S(1)}, f32[8,128,128]{2,1,0:T(8,128)S(1)}) custom-call(s32[10]{0:T(128)S(1)} %stack.36.scal, f32[9,96,128]{2,1,0:T(8,128)S(1)} %get-tuple-element.71.own, f32[9,96,128]{2,1,0:T(8,128)S(1)} %collective-permute-done.13.on, ...), custom_call_target="tpu_custom_call" | custom-call | flops 4000000 | bytes 2000000 | tf_op jit(solution)/shard_map/pallas_call | solution.py:504
  71.3 1.9 %collective-permute-start.14 = (f32[8,128,128]{2,1,0:T(8,128)S(1)}, f32[8,128,128]{2,1,0:T(8,128)S(1)}, u32[]{:S(2)}, u32[]{:S(2)}) collective-permute-start(f32[8,128,128]{2,1,0:T(8,128)S(1)} %get-tuple-element.72), channel_id=1, source_target_pairs={{96,32},{32,1},{1,65},{65,98},{98,34},{34,3},{3,67},{67,4},{4,68},... | collective-permute-start | bytes 1572872 | tf_op jit(solution)/shard_map/ppermute | solution.py:581
  73.2 3.7 %collective-permute-done.15.near = f32[9,96,128]{2,1,0:T(8,128)S(1)} collective-permute-done((f32[9,96,128]{2,1,0:T(8,128)S(1)}, f32[9,96,128]{2,1,0:T(8,128)S(1)}, u32[]{:S(2)}, u32[]{:S(2)}) %collective-permute-start.15) | collective-permute-done | bytes 442400 | tf_op jit(solution)/shard_map/ppermute | solution.py:581
  76.9 3.0 %shard_map.63 = (f32[42,112,128]{2,1,0:T(8,128)S(1)}, f32[42,112,128]{2,1,0:T(8,128)S(1)}) custom-call(s32[10]{0:T(128)S(1)} %stack.36.scal, f32[40,96,128]{2,1,0:T(8,128)S(1)} %get-tuple-element.73.absorb, f32[40,96,128]{2,1,0:T(8,128)S(1)} %get-tuple-element.74.source.refs_2_, ...), custom_call_target="tpu_custom_call", output_to_operand_aliasing={{0}: (3, {}), {1}: (4, {})} | custom-call | flops 11200000 | bytes 5600000 | tf_op jit(solution)/shard_map/pallas_call | solution.py:504
  79.9 4.1 %shard_map.64 = (f32[42,112,128]{2,1,0:T(8,128)S(1)}, f32[42,112,128]{2,1,0:T(8,128)S(1)}, f32[10,48,128]{2,1,0:T(8,128)S(1)}, f32[8,32,128]{2,1,0:T(8,128)S(1)}) custom-call(s32[10]{0:T(128)S(1)} %stack.36.scal, f32[9,96,128]{2,1,0:T(8,128)S(1)} %collective-permute-done.15.near, ...), custom_call_target="tpu_custom_call", output_to_operand_aliasing={{0}: (5, {}), {1}: (6, {}), {2}: (7, {}), {3}: (8, {})} | custom-call | flops 12800000 | bytes 6400000 | tf_op jit(solution)/shard_map/pallas_call | solution.py:504
  84.0 3.7 %shard_map.65 = (f32[42,112,128]{2,1,0:T(8,128)S(1)}, f32[42,112,128]{2,1,0:T(8,128)S(1)}) custom-call(s32[10]{0:T(128)S(1)} %stack.36.scal, f32[9,96,128]{2,1,0:T(8,128)S(1)} %collective-permute-done.16.on2, f32[8,136,128]{2,1,0:T(8,128)S(1)} %collective-permute-done.12.coef.mark, ...), custom_call_target="tpu_custom_call", output_to_operand_aliasing={{0}: (5, {}), {1}: (6, {})} | custom-call | flops 12800000 | bytes 6400000 | tf_op jit(solution)/shard_map/pallas_call | solution.py:504
  87.7 9.3 %shard_map.66 = (f32[8,32,128]{2,1,0:T(8,128)S(1)}, f32[8,32,128]{2,1,0:T(8,128)S(1)}, f32[8,32,128]{2,1,0:T(8,128)S(1)}, f32[8,32,128]{2,1,0:T(8,128)S(1)}, f32...) custom-call(s32[10]{0:T(128)S(1)} %stack.36.scal, ...), custom_call_target="tpu_custom_call", output_to_operand_aliasing={{4}: (5, {}), {5}: (6, {}), {6}: (7, {}), {7}: (8, {})} | custom-call | flops 36800000 | bytes 18400000 | tf_op jit(solution)/shard_map/pallas_call | solution.py:504
  97.7 1.7 %collective-permute-start.19 = (f32[8,32,128]{2,1,0:T(8,128)S(1)}, f32[8,32,128]{2,1,0:T(8,128)S(1)}, u32[]{:S(2)}, u32[]{:S(2)}) collective-permute-start(f32[8,32,128]{2,1,0:T(8,128)S(1)} %get-tuple-element.90), channel_id=1, source_target_pairs={{0,96},{32,64},{64,32},{96,0},{1,97},{33,65},{65,33},{97,1},{2,98}... | collective-permute-start | bytes 393224 | tf_op jit(solution)/shard_map/ppermute | solution.py:638
  99.4 3.2 %collective-permute-done.18.got_2 = f32[8,32,128]{2,1,0:T(8,128)S(1)} collective-permute-done((f32[8,32,128]{2,1,0:T(8,128)S(1)}, f32[8,32,128]{2,1,0:T(8,128)S(1)}, u32[]{:S(2)}, u32[]{:S(2)}) %collective-permute-start.18) | collective-permute-done | bytes 131104 | tf_op jit(solution)/shard_map/ppermute | solution.py:638
  102.6 3.1 %collective-permute-done.19.got_3 = f32[8,32,128]{2,1,0:T(8,128)S(1)} collective-permute-done((f32[8,32,128]{2,1,0:T(8,128)S(1)}, f32[8,32,128]{2,1,0:T(8,128)S(1)}, u32[]{:S(2)}, u32[]{:S(2)}) %collective-permute-start.19) | collective-permute-done | bytes 131104 | tf_op jit(solution)/shard_map/ppermute | solution.py:638
  (36 shorter events, 10.6 us)
Async XLA Ops:
  0.0 15.6 %copy-start = (f32[32,32,128]{2,1,0:T(8,128)S(1)}, f32[32,32,128]{2,1,0:T(8,128)}, u32[]{:S(2)}) copy-start(f32[32,32,128]{2,1,0:T(8,128)} %rec.1) | copy-start | bytes 1572868
  0.0 15.6 %copy-start.1 = (s32[32,32,128]{2,1,0:T(8,128)S(1)}, s32[32,32,128]{2,1,0:T(8,128)}, u32[]{:S(2)}) copy-start(s32[32,32,128]{2,1,0:T(8,128)} %exc.1) | copy-start | bytes 1572868
  1.2 4.0 %collective-permute-start = (f32[8,32,128]{2,1,0:T(8,128)S(1)}, f32[8,32,128]{2,1,0:T(8,128)S(1)}, u32[]{:S(2)}, u32[]{:S(2)}) collective-permute-start(f32[8,32,128]{2,1,0:T(8,128)S(1)} %get-tuple-element.96), channel_id=1, source_target_pairs={{0,32},{32,0},{64,96},{96,64},{1,33},{33,1},{65,97},{97,65},{2,34}... | collective-permute-start | bytes 393224 | tf_op jit(solution)/shard_map/ppermute | solution.py:561
  2.0 5.8 %collective-permute-start.1 = (f32[8,32,128]{2,1,0:T(8,128)S(1)}, f32[8,32,128]{2,1,0:T(8,128)S(1)}, u32[]{:S(2)}, u32[]{:S(2)}) collective-permute-start(f32[8,32,128]{2,1,0:T(8,128)S(1)} %get-tuple-element.98), channel_id=1, source_target_pairs={{0,64},{32,96},{64,0},{96,32},{1,65},{33,97},{65,1},{97,33},{2,66}... | collective-permute-start | bytes 393224 | tf_op jit(solution)/shard_map/ppermute | solution.py:561
  2.1 8.4 %collective-permute-start.2 = (f32[8,32,128]{2,1,0:T(8,128)S(1)}, f32[8,32,128]{2,1,0:T(8,128)S(1)}, u32[]{:S(2)}, u32[]{:S(2)}) collective-permute-start(f32[8,32,128]{2,1,0:T(8,128)S(1)} %get-tuple-element.95), channel_id=1, source_target_pairs={{0,96},{32,64},{64,32},{96,0},{1,97},{33,65},{65,33},{97,1},{2,98}... | collective-permute-start | bytes 393224 | tf_op jit(solution)/shard_map/ppermute | solution.py:561
  4.8 6.4 %collective-permute-start.3 = (f32[8,32,128]{2,1,0:T(8,128)S(1)}, f32[8,32,128]{2,1,0:T(8,128)S(1)}, u32[]{:S(2)}, u32[]{:S(2)}) collective-permute-start(f32[8,32,128]{2,1,0:T(8,128)S(1)} %get-tuple-element.92), channel_id=1, source_target_pairs={{0,32},{32,0},{64,96},{96,64},{1,33},{33,1},{65,97},{97,65},{2,34}... | collective-permute-start | bytes 393224 | tf_op jit(solution)/shard_map/ppermute | solution.py:561
  5.1 7.5 %collective-permute-start.4 = (f32[8,32,128]{2,1,0:T(8,128)S(1)}, f32[8,32,128]{2,1,0:T(8,128)S(1)}, u32[]{:S(2)}, u32[]{:S(2)}) collective-permute-start(f32[8,32,128]{2,1,0:T(8,128)S(1)} %get-tuple-element.94), channel_id=1, source_target_pairs={{0,64},{32,96},{64,0},{96,32},{1,65},{33,97},{65,1},{97,33},{2,66}... | collective-permute-start | bytes 393224 | tf_op jit(solution)/shard_map/ppermute | solution.py:561
  5.2 10.4 %collective-permute-start.5 = (f32[8,32,128]{2,1,0:T(8,128)S(1)}, f32[8,32,128]{2,1,0:T(8,128)S(1)}, u32[]{:S(2)}, u32[]{:S(2)}) collective-permute-start(f32[8,32,128]{2,1,0:T(8,128)S(1)} %get-tuple-element.91), channel_id=1, source_target_pairs={{0,96},{32,64},{64,32},{96,0},{1,97},{33,65},{65,33},{97,1},{2,98}... | collective-permute-start | bytes 393224 | tf_op jit(solution)/shard_map/ppermute | solution.py:561
  16.8 15.0 %collective-permute-start.7 = (f32[8,136,128]{2,1,0:T(8,128)S(1)}, f32[8,136,128]{2,1,0:T(8,128)S(1)}, u32[]{:S(2)}, u32[]{:S(2)}) collective-permute-start(f32[8,136,128]{2,1,0:T(8,128)S(1)} %get-tuple-element.48.coef.first), channel_id=1, source_target_pairs={{64,32},{32,64},{0,1},{1,0},{33,65},{65,33},{97,98},{98,97},{66,34... | collective-permute-start | bytes 1671176 | tf_op jit(solution)/shard_map/ppermute | solution.py:581
  22.0 17.2 %collective-permute-start.8 = (f32[8,128,128]{2,1,0:T(8,128)S(1)}, f32[8,128,128]{2,1,0:T(8,128)S(1)}, u32[]{:S(2)}, u32[]{:S(2)}) collective-permute-start(f32[8,128,128]{2,1,0:T(8,128)S(1)} %shard_map.55.pot), channel_id=1, source_target_pairs={{64,32},{32,64},{0,1},{1,0},{33,65},{65,33},{97,98},{98,97},{66,34... | collective-permute-start | bytes 1572872 | tf_op jit(solution)/shard_map/ppermute | solution.py:581
  26.0 28.5 %collective-permute-start.6 = (f32[8,224,128]{2,1,0:T(8,128)S(1)}, f32[8,224,128]{2,1,0:T(8,128)S(1)}, u32[]{:S(2)}, u32[]{:S(2)}) collective-permute-start(f32[8,224,128]{2,1,0:T(8,128)S(1)} %shard_map.57), channel_id=1, source_target_pairs={{96,32},{32,1},{1,65},{65,98},{98,34},{34,3},{3,67},{67,4},{4,68},... | collective-permute-start | bytes 2752520 | tf_op jit(solution)/shard_map/ppermute | solution.py:581
  27.9 11.3 %collective-permute-start.10 = (f32[8,136,128]{2,1,0:T(8,128)S(1)}, f32[8,136,128]{2,1,0:T(8,128)S(1)}, u32[]{:S(2)}, u32[]{:S(2)}) collective-permute-start(f32[8,136,128]{2,1,0:T(8,128)S(1)} %get-tuple-element.48.coef.first), channel_id=1, source_target_pairs={{96,64},{64,96},{32,0},{0,32},{1,33},{33,1},{65,97},{97,65},{98,66... | collective-permute-start | bytes 1671176 | tf_op jit(solution)/shard_map/ppermute | solution.py:581
  31.7 18.1 %collective-permute-start.12 = (f32[8,136,128]{2,1,0:T(8,128)S(1)}, f32[8,136,128]{2,1,0:T(8,128)S(1)}, u32[]{:S(2)}, u32[]{:S(2)}) collective-permute-start(f32[8,136,128]{2,1,0:T(8,128)S(1)} %collective-permute-done.7.coef.near.mark), channel_id=1, source_target_pairs={{96,64},{64,96},{32,0},{0,32},{1,33},{33,1},{65,97},{97,65},{98,66... | collective-permute-start | bytes 1671176 | tf_op jit(solution)/shard_map/ppermute | solution.py:581
  31.8 7.4 %collective-permute-start.9 = (f32[8,128,128]{2,1,0:T(8,128)S(1)}, f32[8,128,128]{2,1,0:T(8,128)S(1)}, u32[]{:S(2)}, u32[]{:S(2)}) collective-permute-start(f32[8,128,128]{2,1,0:T(8,128)S(1)} %shard_map.55.pot), channel_id=1, source_target_pairs={{96,64},{64,96},{32,0},{0,32},{1,33},{33,1},{65,97},{97,65},{98,66... | collective-permute-start | bytes 1572872 | tf_op jit(solution)/shard_map/ppermute | solution.py:581
  39.2 10.6 %collective-permute-start.11 = (f32[8,128,128]{2,1,0:T(8,128)S(1)}, f32[8,128,128]{2,1,0:T(8,128)S(1)}, u32[]{:S(2)}, u32[]{:S(2)}) collective-permute-start(f32[8,128,128]{2,1,0:T(8,128)S(1)} %collective-permute-done.8.pot), channel_id=1, source_target_pairs={{96,64},{64,96},{32,0},{0,32},{1,33},{33,1},{65,97},{97,65},{98,66... | collective-permute-start | bytes 1572872 | tf_op jit(solution)/shard_map/ppermute | solution.py:581
  63.7 6.0 %collective-permute-start.13 = (f32[9,96,128]{2,1,0:T(8,128)S(1)}, f32[9,96,128]{2,1,0:T(8,128)S(1)}, u32[]{:S(2)}, u32[]{:S(2)}) collective-permute-start(f32[9,96,128]{2,1,0:T(8,128)S(1)} %get-tuple-element.71.own), channel_id=1, source_target_pairs={{96,64},{64,96},{32,0},{0,32},{1,33},{33,1},{65,97},{97,65},{98,66... | collective-permute-start | bytes 1327112 | tf_op jit(solution)/shard_map/ppermute | solution.py:581
  64.3 12.6 %collective-permute-start.15 = (f32[9,96,128]{2,1,0:T(8,128)S(1)}, f32[9,96,128]{2,1,0:T(8,128)S(1)}, u32[]{:S(2)}, u32[]{:S(2)}) collective-permute-start(f32[9,96,128]{2,1,0:T(8,128)S(1)} %get-tuple-element.71.own), channel_id=1, source_target_pairs={{64,32},{32,64},{0,1},{1,0},{33,65},{65,33},{97,98},{98,97},{66,34... | collective-permute-start | bytes 1327112 | tf_op jit(solution)/shard_map/ppermute | solution.py:581
  71.3 16.4 %collective-permute-start.14 = (f32[8,128,128]{2,1,0:T(8,128)S(1)}, f32[8,128,128]{2,1,0:T(8,128)S(1)}, u32[]{:S(2)}, u32[]{:S(2)}) collective-permute-start(f32[8,128,128]{2,1,0:T(8,128)S(1)} %get-tuple-element.72), channel_id=1, source_target_pairs={{96,32},{32,1},{1,65},{65,98},{98,34},{34,3},{3,67},{67,4},{4,68},... | collective-permute-start | bytes 1572872 | tf_op jit(solution)/shard_map/ppermute | solution.py:581
  76.9 7.1 %collective-permute-start.16 = (f32[9,96,128]{2,1,0:T(8,128)S(1)}, f32[9,96,128]{2,1,0:T(8,128)S(1)}, u32[]{:S(2)}, u32[]{:S(2)}) collective-permute-start(f32[9,96,128]{2,1,0:T(8,128)S(1)} %collective-permute-done.15.near), channel_id=1, source_target_pairs={{96,64},{64,96},{32,0},{0,32},{1,33},{33,1},{65,97},{97,65},{98,66... | collective-permute-start | bytes 1327112 | tf_op jit(solution)/shard_map/ppermute | solution.py:581
  97.1 2.3 %collective-permute-start.17 = (f32[8,32,128]{2,1,0:T(8,128)S(1)}, f32[8,32,128]{2,1,0:T(8,128)S(1)}, u32[]{:S(2)}, u32[]{:S(2)}) collective-permute-start(f32[8,32,128]{2,1,0:T(8,128)S(1)} %get-tuple-element.88), channel_id=1, source_target_pairs={{0,32},{32,0},{64,96},{96,64},{1,33},{33,1},{65,97},{97,65},{2,34}... | collective-permute-start | bytes 393224 | tf_op jit(solution)/shard_map/ppermute | solution.py:638
  97.7 5.0 %collective-permute-start.18 = (f32[8,32,128]{2,1,0:T(8,128)S(1)}, f32[8,32,128]{2,1,0:T(8,128)S(1)}, u32[]{:S(2)}, u32[]{:S(2)}) collective-permute-start(f32[8,32,128]{2,1,0:T(8,128)S(1)} %get-tuple-element.89), channel_id=1, source_target_pairs={{0,64},{32,96},{64,0},{96,32},{1,65},{33,97},{65,1},{97,33},{2,66}... | collective-permute-start | bytes 393224 | tf_op jit(solution)/shard_map/ppermute | solution.py:638
  97.7 8.0 %collective-permute-start.19 = (f32[8,32,128]{2,1,0:T(8,128)S(1)}, f32[8,32,128]{2,1,0:T(8,128)S(1)}, u32[]{:S(2)}, u32[]{:S(2)}) collective-permute-start(f32[8,32,128]{2,1,0:T(8,128)S(1)} %get-tuple-element.90), channel_id=1, source_target_pairs={{0,96},{32,64},{64,32},{96,0},{1,97},{33,65},{65,33},{97,1},{2,98}... | collective-permute-start | bytes 393224 | tf_op jit(solution)/shard_map/ppermute | solution.py:638

commit v9 on v7

--- a/solution.py
+++ b/solution.py
@@ -236,12 +236,14 @@
     lax.fori_loop(0, SLAB, plane, 0)
 
 
-def gather_coef(scal, rec, exc, pot, own, got_1, got_2, got_3, msg, aux, deep):
+def gather_coef(scal, rec, exc, pot, own, got_1, got_2, got_3, msg, far, aux, deep):
     strip = jnp.full((8, 128), scal[3].astype(jnp.float32))
 
     def plane(u, carry):
         whole = collect(scal, own, (got_1, got_2, got_3), u, deep)
         msg[u, 0:ROWS] = deep[u, 0:ROWS]
+        far[u, 0:POT_ROWS] = pot[u]
+        far[u, POT_ROWS:FAR_ROWS] = deep[u, 0:ROWS]
         threshold = deep[u, ROWS : ROWS + HEART]
         active = exc[whole].astype(jnp.float32)
         voltage, recovery = ionic(pot[u, V0_AT : V0_AT + HEART], rec[whole], threshold, active)
@@ -321,15 +323,6 @@
         lax.fori_loop(first, last, plane, 0)
 
     on_layer(row, work)
-
-
-def first_open(scal, pot, coef, copy):
-    def send(u, carry):
-        copy[u, 0:POT_ROWS] = pot[u]
-        copy[u, POT_ROWS:FAR_ROWS] = coef[u, 0:ROWS]
-        return carry
-
-    lax.fori_loop(0, SLAB, send, 0)
 
 
 def first_inner(scal, pot, coef, on_pot, on_coef, aux, *refs):
@@ -376,35 +369,32 @@
     sweep(scal, RIGHT, even, odd, absorb, source)
 
 
-def first_outer(scal, far, near, held, *refs):
-    msg, even, odd, absorb, source, volt = refs[5:]
+def first_outer(scal, far, near, held, first, *refs):
+    msg, copy, even, odd, absorb, source, volt = refs[5:]
     take_first(far, far, POT_ROWS, 0, 1, even, absorb, volt)
     embed(1, SLAB + 1, near[0, ROW_AT : ROW_AT + 1], (volt, source))
     sweep(scal, OUTER, even, odd, absorb, source)
     for u in range(SLAB):
         msg[u] = even[OFF + OWN + u, PAD : PAD + ROWS]
+        copy[u, 0:ROWS] = even[OFF + OWN + u, PAD : PAD + ROWS]
+        copy[u, ROWS : ROWS + HEART] = first[u, V1_AT : V1_AT + HEART]
     msg[SLAB, 0:HEART] = held[0]
     msg[SLAB, HEART : 2 * HEART] = held[SLAB - 1]
     msg[SLAB, 2 * HEART : ROWS] = jnp.zeros((HEART, 128), jnp.float32)
 
 
-def second_open(scal, own, on, held, first, even, odd, volt, out, copy):
+def second_inner(scal, own, on, held, absorb, source, *refs):
+    volt, out, even, odd = refs[2:]
+
     def keep(u, carry):
-        copy[u, 0:ROWS] = own[u]
-        copy[u, ROWS : ROWS + HEART] = first[u, V1_AT : V1_AT + HEART]
         put_heart(volt, u + 1, held[u])
         return carry
 
     lax.fori_loop(0, SLAB, keep, 0)
-    clear_edges(even, odd)
     take(own, OWN, 1, even)
     take(on, END - 1, -1, even)
     put_heart(volt, SLAB + 1, on[SLAB, HEART : 2 * HEART])
     settle(1, SLAB, scal[3], even, volt, out)
-
-
-def second_inner(scal, absorb, source, *refs):
-    even, odd = refs[2:]
     sweep(scal, INNER, even, odd, absorb, source)
 
 
@@ -539,10 +529,10 @@
     got_pot = swapped(pot)
     got_coef = swapped(coef)
     (msg_pot,) = call(gather_pot, (scal, *got_pot), [(SLAB, POT_ROWS, 128)], 10)
-    msg_coef, aux = call(
+    msg_coef, copy, aux = call(
         gather_coef,
         (scal, recovery, excitable, msg_pot, *got_coef),
-        [(SLAB, COEF_ROWS, 128), (3, SLAB, HEART, 128)],
+        [(SLAB, COEF_ROWS, 128), (SLAB, FAR_ROWS, 128), (3, SLAB, HEART, 128)],
         20,
         scratch=[(SLAB, 128, 128)],
     )
@@ -559,7 +549,6 @@
     near_coef = move(msg_coef, facing)
     on_pot = move(msg_pot, partner)
     on_coef = move(msg_coef, partner)
-    (copy,) = call(first_open, (scal, msg_pot, msg_coef), [(SLAB, FAR_ROWS, 128)], 5)
     far = move(copy, beyond)
     state = call(
         first_inner,
@@ -573,24 +562,24 @@
     even, odd, absorb, source, later, volt_0, volt_1 = call(
         first_right, (scal, on2_pot, on2_coef), [], 64, state=state
     )
-    message, _, _, absorb, _, _ = call(
+    message, copy, even, odd, absorb, _, _ = call(
         first_outer,
-        (scal, far, near_coef, held),
-        [(SLAB + 1, ROWS, 128)],
+        (scal, far, near_coef, held, msg_coef),
+        [(SLAB + 1, ROWS, 128), (SLAB, ROWS + HEART, 128)],
         184,
         state=[even, odd, absorb, source, volt_0],
     )
 
     near = move(message, facing)
     on = move(message, partner)
-    even, odd, volt_2, voltage, copy = call(
-        second_open,
-        (scal, message, on, held, msg_coef),
-        [phi, phi, (SLAB + 2, V_PAD, 128), heart, (SLAB, ROWS + HEART, 128)],
-        20,
+    far = move(copy, beyond)
+    volt_2, voltage, even, odd = call(
+        second_inner,
+        (scal, message, on, held, absorb, later),
+        [(SLAB + 2, V_PAD, 128), heart],
+        56,
+        state=[even, odd],
     )
-    far = move(copy, beyond)
-    even, odd = call(second_inner, (scal, absorb, later), [], 56, state=[even, odd])
     on2 = move(near, partner)
     even, odd, _, voltage = call(
         second_left, (scal, near, absorb, later), [], 64, state=[even, odd, volt_2, voltage]

time: 101 us -> 103 us (1.020)
  the two profiles are of different devices: /device:TPU:105 before, /device:TPU:87 now
where the time goes in v9:
time: 103 us
  Pallas kernels  41.9 us (41%)
  starting transfers between devices  30.8 us (30%)
  waiting for transfers between devices  27.2 us (26%)
  local copies, waits for them, and re-layouts  2.44 us (2%)
    pallas_call x11, Pallas kernels, call(): pl.pallas_call(kernel, out_shape=arrays, in_specs=[SMEM] + [VMEM] * (len(...  41.9 us
    ppermute x11, starting transfers between devices, move(): return lax.ppermute(value, AXES, pairs)  23.9 us
    ppermute x11, waiting for transfers between devices, move(): return lax.ppermute(value, AXES, pairs)  14.1 us
    ppermute x6, waiting for transfers between devices, swapped(): got.append(lax.ppermute(piece, 'sec', across(number)))  7.14 us
    ppermute x3, waiting for transfers between devices, body(): back.append(lax.ppermute(outs[number], 'sec', across(number)))  5.98 us
    ppermute x6, starting transfers between devices, swapped(): got.append(lax.ppermute(piece, 'sec', across(number)))  4.7 us
    dynamic_slice x2, local copies, waits for them, and re-layouts, swapped(): lax.dynamic_slice_in_dim(value, SLAB * chunk_of(sec ^ number), SLAB, 0)  2.34 us
    ppermute x3, starting transfers between devices, body(): back.append(lax.ppermute(outs[number], 'sec', across(number)))  2.21 us
  transfers between devices with their start and end apart: 20, of which 8 were waited for; matrix products, arithmetic and copies ran while one was open for 1% of the time, Pallas kernels for 22%

profile of v9, /device:TPU:87, one launch (start us, length us, event | category | flops | bytes accessed | tf_op | source)
XLA Modules:
  0.0 103.2 jit_solution(15140878696234328921)
XLA Ops:
  7.8 2.7 %collective-permute-done.2.got_3 = f32[8,32,128]{2,1,0:T(8,128)S(1)} collective-permute-done((f32[8,32,128]{2,1,0:T(8,128)S(1)}, f32[8,32,128]{2,1,0:T(8,128)S(1)}, u32[]{:S(2)}, u32[]{:S(2)}) %collective-permute-start.2) | collective-permute-done | bytes 131104 | tf_op jit(solution)/shard_map/ppermute | solution.py:526
  11.2 1.3 %collective-permute-done.4.got_2 = f32[8,32,128]{2,1,0:T(8,128)S(1)} collective-permute-done((f32[8,32,128]{2,1,0:T(8,128)S(1)}, f32[8,32,128]{2,1,0:T(8,128)S(1)}, u32[]{:S(2)}, u32[]{:S(2)}) %collective-permute-start.4) | collective-permute-done | bytes 131104 | tf_op jit(solution)/shard_map/ppermute | solution.py:526
  12.6 3.1 %collective-permute-done.5.got_3 = f32[8,32,128]{2,1,0:T(8,128)S(1)} collective-permute-done((f32[8,32,128]{2,1,0:T(8,128)S(1)}, f32[8,32,128]{2,1,0:T(8,128)S(1)}, u32[]{:S(2)}, u32[]{:S(2)}) %collective-permute-start.5) | collective-permute-done | bytes 131104 | tf_op jit(solution)/shard_map/ppermute | solution.py:526
  16.8 2.9 %collective-permute-start.7 = (f32[8,136,128]{2,1,0:T(8,128)S(1)}, f32[8,136,128]{2,1,0:T(8,128)S(1)}, u32[]{:S(2)}, u32[]{:S(2)}) collective-permute-start(f32[8,136,128]{2,1,0:T(8,128)S(1)} %get-tuple-element.50.coef.first), channel_id=1, source_target_pairs={{64,32},{32,64},{0,1},{1,0},{33,65},{65,33},{97,98},{98,97},{66,34... | collective-permute-start | bytes 1671176 | tf_op jit(solution)/shard_map/ppermute | solution.py:546
  19.7 2.6 %collective-permute-start.8 = (f32[8,128,128]{2,1,0:T(8,128)S(1)}, f32[8,128,128]{2,1,0:T(8,128)S(1)}, u32[]{:S(2)}, u32[]{:S(2)}) collective-permute-start(f32[8,128,128]{2,1,0:T(8,128)S(1)} %shard_map.55.pot), channel_id=1, source_target_pairs={{64,32},{32,64},{0,1},{1,0},{33,65},{65,33},{97,98},{98,97},{66,34... | collective-permute-start | bytes 1572872 | tf_op jit(solution)/shard_map/ppermute | solution.py:546
  22.4 6.1 %collective-permute-start.6 = (f32[8,224,128]{2,1,0:T(8,128)S(1)}, f32[8,224,128]{2,1,0:T(8,128)S(1)}, u32[]{:S(2)}, u32[]{:S(2)}) collective-permute-start(f32[8,224,128]{2,1,0:T(8,128)S(1)} %get-tuple-element.49), channel_id=1, source_target_pairs={{96,32},{32,1},{1,65},{65,98},{98,34},{34,3},{3,67},{67,4},{4,68},... | collective-permute-start | bytes 2752520 | tf_op jit(solution)/shard_map/ppermute | solution.py:546
  28.9 1.9 %collective-permute-start.12 = (f32[8,136,128]{2,1,0:T(8,128)S(1)}, f32[8,136,128]{2,1,0:T(8,128)S(1)}, u32[]{:S(2)}, u32[]{:S(2)}) collective-permute-start(f32[8,136,128]{2,1,0:T(8,128)S(1)} %collective-permute-done.7.coef.near), channel_id=1, source_target_pairs={{96,64},{64,96},{32,0},{0,32},{1,33},{33,1},{65,97},{97,65},{98,66... | collective-permute-start | bytes 1671176 | tf_op jit(solution)/shard_map/ppermute | solution.py:546
  30.8 9.3 %collective-permute-done.8.pot = f32[8,128,128]{2,1,0:T(8,128)S(1)} collective-permute-done((f32[8,128,128]{2,1,0:T(8,128)S(1)}, f32[8,128,128]{2,1,0:T(8,128)S(1)}, u32[]{:S(2)}, u32[]{:S(2)}) %collective-permute-start.8) | collective-permute-done | bytes 524320 | tf_op jit(solution)/shard_map/ppermute | solution.py:546
  40.2 5.7 %shard_map.57 = (f32[42,112,128]{2,1,0:T(8,128)S(1)}, f32[42,112,128]{2,1,0:T(8,128)S(1)}, f32[40,96,128]{2,1,0:T(8,128)S(1)}, f32[40,96,128]{2,1,0:T(8,128)S(1)...) custom-call(s32[10]{0:T(128)S(1)} %stack.36.scal, ...), custom_call_target="tpu_custom_call" | custom-call | flops 11200000 | bytes 5600000 | tf_op jit(solution)/shard_map/pallas_call | solution.py:469
  45.8 3.8 %shard_map.58 = (f32[42,112,128]{2,1,0:T(8,128)S(1)}, f32[42,112,128]{2,1,0:T(8,128)S(1)}, f32[40,96,128]{2,1,0:T(8,128)S(1)}, f32[40,96,128]{2,1,0:T(8,128)S(1)...) custom-call(s32[10]{0:T(128)S(1)} %stack.36.scal, ...), custom_call_target="tpu_custom_call", output_to_operand_aliasing={{0}: (4, {}), {1}: (5, {}), {2}: (6, {}), {3}: (7, {}), {4}... | custom-call | flops 12800000 | bytes 6400000 | tf_op jit(solution)/shard_map/pallas_call | solution.py:469
  49.6 3.6 %shard_map.59 = (f32[42,112,128]{2,1,0:T(8,128)S(1)}, f32[42,112,128]{2,1,0:T(8,128)S(1)}, f32[40,96,128]{2,1,0:T(8,128)S(1)}, f32[40,96,128]{2,1,0:T(8,128)S(1)...) custom-call(s32[10]{0:T(128)S(1)} %stack.36.scal, ...), custom_call_target="tpu_custom_call", output_to_operand_aliasing={{0}: (3, {}), {1}: (4, {}), {2}: (5, {}), {3}: (6, {}), {4}... | custom-call | flops 12800000 | bytes 6400000 | tf_op jit(solution)/shard_map/pallas_call | solution.py:469
  53.2 8.1 %shard_map.60 = (f32[9,96,128]{2,1,0:T(8,128)S(1)}, f32[8,128,128]{2,1,0:T(8,128)S(1)}, f32[42,112,128]{2,1,0:T(8,128)S(1)}, f32[42,112,128]{2,1,0:T(8,128)S(1)}...) custom-call(s32[10]{0:T(128)S(1)} %stack.36.scal, ...), custom_call_target="tpu_custom_call", output_to_operand_aliasing={{2}: (5, {}), {3}: (6, {}), {4}: (7, {}), {5}: (8, {}), {6}... | custom-call | flops 36800000 | bytes 18400000 | tf_op jit(solution)/shard_map/pallas_call | solution.py:469
  61.4 1.9 %collective-permute-start.14 = (f32[9,96,128]{2,1,0:T(8,128)S(1)}, f32[9,96,128]{2,1,0:T(8,128)S(1)}, u32[]{:S(2)}, u32[]{:S(2)}) collective-permute-start(f32[9,96,128]{2,1,0:T(8,128)S(1)} %get-tuple-element.75.own), channel_id=1, source_target_pairs={{64,32},{32,64},{0,1},{1,0},{33,65},{65,33},{97,98},{98,97},{66,34... | collective-permute-start | bytes 1327112 | tf_op jit(solution)/shard_map/ppermute | solution.py:546
  63.3 6.8 %collective-permute-start.13 = (f32[8,128,128]{2,1,0:T(8,128)S(1)}, f32[8,128,128]{2,1,0:T(8,128)S(1)}, u32[]{:S(2)}, u32[]{:S(2)}) collective-permute-start(f32[8,128,128]{2,1,0:T(8,128)S(1)} %get-tuple-element.73), channel_id=1, source_target_pairs={{96,32},{32,1},{1,65},{65,98},{98,34},{34,3},{3,67},{67,4},{4,68},... | collective-permute-start | bytes 1572872 | tf_op jit(solution)/shard_map/ppermute | solution.py:546
  70.3 4.3 %collective-permute-done.14.near = f32[9,96,128]{2,1,0:T(8,128)S(1)} collective-permute-done((f32[9,96,128]{2,1,0:T(8,128)S(1)}, f32[9,96,128]{2,1,0:T(8,128)S(1)}, u32[]{:S(2)}, u32[]{:S(2)}) %collective-permute-start.14) | collective-permute-done | bytes 442400 | tf_op jit(solution)/shard_map/ppermute | solution.py:546
  74.7 1.3 %collective-permute-start.16 = (f32[9,96,128]{2,1,0:T(8,128)S(1)}, f32[9,96,128]{2,1,0:T(8,128)S(1)}, u32[]{:S(2)}, u32[]{:S(2)}) collective-permute-start(f32[9,96,128]{2,1,0:T(8,128)S(1)} %collective-permute-done.14.near), channel_id=1, source_target_pairs={{96,64},{64,96},{32,0},{0,32},{1,33},{33,1},{65,97},{97,65},{98,66... | collective-permute-start | bytes 1327112 | tf_op jit(solution)/shard_map/ppermute | solution.py:546
  76.0 3.7 %shard_map.61 = (f32[10,48,128]{2,1,0:T(8,128)S(1)}, f32[8,32,128]{2,1,0:T(8,128)S(1)}, f32[42,112,128]{2,1,0:T(8,128)S(1)}, f32[42,112,128]{2,1,0:T(8,128)S(1)}) custom-call(s32[10]{0:T(128)S(1)} %stack.36.scal, f32[9,96,128]{2,1,0:T(8,128)S(1)} %get-tuple-element.75.own, ...), custom_call_target="tpu_custom_call", output_to_operand_aliasing={{2}: (6, {}), {3}: (7, {})} | custom-call | flops 11200000 | bytes 5600000 | tf_op jit(solution)/shard_map/pallas_call | solution.py:469
  79.6 2.9 %shard_map.62 = (f32[42,112,128]{2,1,0:T(8,128)S(1)}, f32[42,112,128]{2,1,0:T(8,128)S(1)}, f32[10,48,128]{2,1,0:T(8,128)S(1)}, f32[8,32,128]{2,1,0:T(8,128)S(1)}) custom-call(s32[10]{0:T(128)S(1)} %stack.36.scal, f32[9,96,128]{2,1,0:T(8,128)S(1)} %collective-permute-done.14.near, ...), custom_call_target="tpu_custom_call", output_to_operand_aliasing={{0}: (4, {}), {1}: (5, {}), {2}: (6, {}), {3}: (7, {})} | custom-call | flops 12800000 | bytes 6400000 | tf_op jit(solution)/shard_map/pallas_call | solution.py:469
  82.6 2.8 %shard_map.63 = (f32[42,112,128]{2,1,0:T(8,128)S(1)}, f32[42,112,128]{2,1,0:T(8,128)S(1)}) custom-call(s32[10]{0:T(128)S(1)} %stack.36.scal, f32[9,96,128]{2,1,0:T(8,128)S(1)} %collective-permute-done.16.on2, f32[40,96,128]{2,1,0:T(8,128)S(1)} %get-tuple-element.74.absorb, ...), custom_call_target="tpu_custom_call", output_to_operand_aliasing={{0}: (4, {}), {1}: (5, {})} | custom-call | flops 12800000 | bytes 6400000 | tf_op jit(solution)/shard_map/pallas_call | solution.py:469
  85.4 8.2 %shard_map.64 = (f32[8,32,128]{2,1,0:T(8,128)S(1)}, f32[8,32,128]{2,1,0:T(8,128)S(1)}, f32[8,32,128]{2,1,0:T(8,128)S(1)}, f32[8,32,128]{2,1,0:T(8,128)S(1)}, f32...) custom-call(s32[10]{0:T(128)S(1)} %stack.36.scal, ...), custom_call_target="tpu_custom_call", output_to_operand_aliasing={{4}: (5, {}), {5}: (6, {}), {6}: (7, {}), {7}: (8, {})} | custom-call | flops 36800000 | bytes 18400000 | tf_op jit(solution)/shard_map/pallas_call | solution.py:469
  93.8 2.0 %collective-permute-start.19 = (f32[8,32,128]{2,1,0:T(8,128)S(1)}, f32[8,32,128]{2,1,0:T(8,128)S(1)}, u32[]{:S(2)}, u32[]{:S(2)}) collective-permute-start(f32[8,32,128]{2,1,0:T(8,128)S(1)} %get-tuple-element.92), channel_id=1, source_target_pairs={{0,96},{32,64},{64,32},{96,0},{1,97},{33,65},{65,33},{97,1},{2,98}... | collective-permute-start | bytes 393224 | tf_op jit(solution)/shard_map/ppermute | solution.py:598
  95.8 2.6 %collective-permute-done.18.got_2 = f32[8,32,128]{2,1,0:T(8,128)S(1)} collective-permute-done((f32[8,32,128]{2,1,0:T(8,128)S(1)}, f32[8,32,128]{2,1,0:T(8,128)S(1)}, u32[]{:S(2)}, u32[]{:S(2)}) %collective-permute-start.18) | collective-permute-done | bytes 131104 | tf_op jit(solution)/shard_map/ppermute | solution.py:598
  98.4 3.4 %collective-permute-done.19.got_3 = f32[8,32,128]{2,1,0:T(8,128)S(1)} collective-permute-done((f32[8,32,128]{2,1,0:T(8,128)S(1)}, f32[8,32,128]{2,1,0:T(8,128)S(1)}, u32[]{:S(2)}, u32[]{:S(2)}) %collective-permute-start.19) | collective-permute-done | bytes 131104 | tf_op jit(solution)/shard_map/ppermute | solution.py:598
  101.8 1.4 %shard_map.65 = f32[32,32,128]{2,1,0:T(8,128)} custom-call(s32[10]{0:T(128)S(1)} %stack.36.scal, f32[8,32,128]{2,1,0:T(8,128)S(1)} %get-tuple-element.89.own, f32[8,32,128]{2,1,0:T(8,128)S(1)} %collective-permute-done.17.got_1, f32[8,32,128]{2,1,0:T(8,128)S(1)} %collective-permute-done.18.got_2, f32[8,32,128]{2,1,0:T(8,128)S(1)} %collective-permute-done.19.got_3), custom_call_target="tpu_custom_call" | custom-call | flops 1000000 | bytes 500000 | tf_op jit(solution)/shard_map/pallas_call | solution.py:469
  (34 shorter events, 9.9 us)
Async XLA Ops:
  0.0 15.6 %copy-start = (f32[32,32,128]{2,1,0:T(8,128)S(1)}, f32[32,32,128]{2,1,0:T(8,128)}, u32[]{:S(2)}) copy-start(f32[32,32,128]{2,1,0:T(8,128)} %rec.1) | copy-start | bytes 1572868
  0.0 15.6 %copy-start.1 = (s32[32,32,128]{2,1,0:T(8,128)S(1)}, s32[32,32,128]{2,1,0:T(8,128)}, u32[]{:S(2)}) copy-start(s32[32,32,128]{2,1,0:T(8,128)} %exc.1) | copy-start | bytes 1572868
  1.2 4.8 %collective-permute-start = (f32[8,32,128]{2,1,0:T(8,128)S(1)}, f32[8,32,128]{2,1,0:T(8,128)S(1)}, u32[]{:S(2)}, u32[]{:S(2)}) collective-permute-start(f32[8,32,128]{2,1,0:T(8,128)S(1)} %get-tuple-element.98), channel_id=1, source_target_pairs={{0,32},{32,0},{64,96},{96,64},{1,33},{33,1},{65,97},{97,65},{2,34}... | collective-permute-start | bytes 393224 | tf_op jit(solution)/shard_map/ppermute | solution.py:526
  2.0 5.8 %collective-permute-start.1 = (f32[8,32,128]{2,1,0:T(8,128)S(1)}, f32[8,32,128]{2,1,0:T(8,128)S(1)}, u32[]{:S(2)}, u32[]{:S(2)}) collective-permute-start(f32[8,32,128]{2,1,0:T(8,128)S(1)} %get-tuple-element.100), channel_id=1, source_target_pairs={{0,64},{32,96},{64,0},{96,32},{1,65},{33,97},{65,1},{97,33},{2,66}... | collective-permute-start | bytes 393224 | tf_op jit(solution)/shard_map/ppermute | solution.py:526
  3.0 7.6 %collective-permute-start.2 = (f32[8,32,128]{2,1,0:T(8,128)S(1)}, f32[8,32,128]{2,1,0:T(8,128)S(1)}, u32[]{:S(2)}, u32[]{:S(2)}) collective-permute-start(f32[8,32,128]{2,1,0:T(8,128)S(1)} %get-tuple-element.97), channel_id=1, source_target_pairs={{0,96},{32,64},{64,32},{96,0},{1,97},{33,65},{65,33},{97,1},{2,98}... | collective-permute-start | bytes 393224 | tf_op jit(solution)/shard_map/ppermute | solution.py:526
  4.8 6.4 %collective-permute-start.3 = (f32[8,32,128]{2,1,0:T(8,128)S(1)}, f32[8,32,128]{2,1,0:T(8,128)S(1)}, u32[]{:S(2)}, u32[]{:S(2)}) collective-permute-start(f32[8,32,128]{2,1,0:T(8,128)S(1)} %get-tuple-element.94), channel_id=1, source_target_pairs={{0,32},{32,0},{64,96},{96,64},{1,33},{33,1},{65,97},{97,65},{2,34}... | collective-permute-start | bytes 393224 | tf_op jit(solution)/shard_map/ppermute | solution.py:526
  5.1 7.5 %collective-permute-start.4 = (f32[8,32,128]{2,1,0:T(8,128)S(1)}, f32[8,32,128]{2,1,0:T(8,128)S(1)}, u32[]{:S(2)}, u32[]{:S(2)}) collective-permute-start(f32[8,32,128]{2,1,0:T(8,128)S(1)} %get-tuple-element.96), channel_id=1, source_target_pairs={{0,64},{32,96},{64,0},{96,32},{1,65},{33,97},{65,1},{97,33},{2,66}... | collective-permute-start | bytes 393224 | tf_op jit(solution)/shard_map/ppermute | solution.py:526
  6.1 9.6 %collective-permute-start.5 = (f32[8,32,128]{2,1,0:T(8,128)S(1)}, f32[8,32,128]{2,1,0:T(8,128)S(1)}, u32[]{:S(2)}, u32[]{:S(2)}) collective-permute-start(f32[8,32,128]{2,1,0:T(8,128)S(1)} %get-tuple-element.93), channel_id=1, source_target_pairs={{0,96},{32,64},{64,32},{96,0},{1,97},{33,65},{65,33},{97,1},{2,98}... | collective-permute-start | bytes 393224 | tf_op jit(solution)/shard_map/ppermute | solution.py:526
  16.8 12.1 %collective-permute-start.7 = (f32[8,136,128]{2,1,0:T(8,128)S(1)}, f32[8,136,128]{2,1,0:T(8,128)S(1)}, u32[]{:S(2)}, u32[]{:S(2)}) collective-permute-start(f32[8,136,128]{2,1,0:T(8,128)S(1)} %get-tuple-element.50.coef.first), channel_id=1, source_target_pairs={{64,32},{32,64},{0,1},{1,0},{33,65},{65,33},{97,98},{98,97},{66,34... | collective-permute-start | bytes 1671176 | tf_op jit(solution)/shard_map/ppermute | solution.py:546
  19.7 20.4 %collective-permute-start.8 = (f32[8,128,128]{2,1,0:T(8,128)S(1)}, f32[8,128,128]{2,1,0:T(8,128)S(1)}, u32[]{:S(2)}, u32[]{:S(2)}) collective-permute-start(f32[8,128,128]{2,1,0:T(8,128)S(1)} %shard_map.55.pot), channel_id=1, source_target_pairs={{64,32},{32,64},{0,1},{1,0},{33,65},{65,33},{97,98},{98,97},{66,34... | collective-permute-start | bytes 1572872 | tf_op jit(solution)/shard_map/ppermute | solution.py:546
  22.4 30.8 %collective-permute-start.6 = (f32[8,224,128]{2,1,0:T(8,128)S(1)}, f32[8,224,128]{2,1,0:T(8,128)S(1)}, u32[]{:S(2)}, u32[]{:S(2)}) collective-permute-start(f32[8,224,128]{2,1,0:T(8,128)S(1)} %get-tuple-element.49), channel_id=1, source_target_pairs={{96,32},{32,1},{1,65},{65,98},{98,34},{34,3},{3,67},{67,4},{4,68},... | collective-permute-start | bytes 2752520 | tf_op jit(solution)/shard_map/ppermute | solution.py:546
  28.5 11.7 %collective-permute-start.10 = (f32[8,136,128]{2,1,0:T(8,128)S(1)}, f32[8,136,128]{2,1,0:T(8,128)S(1)}, u32[]{:S(2)}, u32[]{:S(2)}) collective-permute-start(f32[8,136,128]{2,1,0:T(8,128)S(1)} %get-tuple-element.50.coef.first), channel_id=1, source_target_pairs={{96,64},{64,96},{32,0},{0,32},{1,33},{33,1},{65,97},{97,65},{98,66... | collective-permute-start | bytes 1671176 | tf_op jit(solution)/shard_map/ppermute | solution.py:546
  28.9 20.7 %collective-permute-start.12 = (f32[8,136,128]{2,1,0:T(8,128)S(1)}, f32[8,136,128]{2,1,0:T(8,128)S(1)}, u32[]{:S(2)}, u32[]{:S(2)}) collective-permute-start(f32[8,136,128]{2,1,0:T(8,128)S(1)} %collective-permute-done.7.coef.near), channel_id=1, source_target_pairs={{96,64},{64,96},{32,0},{0,32},{1,33},{33,1},{65,97},{97,65},{98,66... | collective-permute-start | bytes 1671176 | tf_op jit(solution)/shard_map/ppermute | solution.py:546
  30.8 9.4 %collective-permute-start.9 = (f32[8,128,128]{2,1,0:T(8,128)S(1)}, f32[8,128,128]{2,1,0:T(8,128)S(1)}, u32[]{:S(2)}, u32[]{:S(2)}) collective-permute-start(f32[8,128,128]{2,1,0:T(8,128)S(1)} %shard_map.55.pot), channel_id=1, source_target_pairs={{96,64},{64,96},{32,0},{0,32},{1,33},{33,1},{65,97},{97,65},{98,66... | collective-permute-start | bytes 1572872 | tf_op jit(solution)/shard_map/ppermute | solution.py:546
  40.1 9.5 %collective-permute-start.11 = (f32[8,128,128]{2,1,0:T(8,128)S(1)}, f32[8,128,128]{2,1,0:T(8,128)S(1)}, u32[]{:S(2)}, u32[]{:S(2)}) collective-permute-start(f32[8,128,128]{2,1,0:T(8,128)S(1)} %collective-permute-done.8.pot), channel_id=1, source_target_pairs={{96,64},{64,96},{32,0},{0,32},{1,33},{33,1},{65,97},{97,65},{98,66... | collective-permute-start | bytes 1572872 | tf_op jit(solution)/shard_map/ppermute | solution.py:546
  61.4 13.3 %collective-permute-start.14 = (f32[9,96,128]{2,1,0:T(8,128)S(1)}, f32[9,96,128]{2,1,0:T(8,128)S(1)}, u32[]{:S(2)}, u32[]{:S(2)}) collective-permute-start(f32[9,96,128]{2,1,0:T(8,128)S(1)} %get-tuple-element.75.own), channel_id=1, source_target_pairs={{64,32},{32,64},{0,1},{1,0},{33,65},{65,33},{97,98},{98,97},{66,34... | collective-permute-start | bytes 1327112 | tf_op jit(solution)/shard_map/ppermute | solution.py:546
  63.3 22.1 %collective-permute-start.13 = (f32[8,128,128]{2,1,0:T(8,128)S(1)}, f32[8,128,128]{2,1,0:T(8,128)S(1)}, u32[]{:S(2)}, u32[]{:S(2)}) collective-permute-start(f32[8,128,128]{2,1,0:T(8,128)S(1)} %get-tuple-element.73), channel_id=1, source_target_pairs={{96,32},{32,1},{1,65},{65,98},{98,34},{34,3},{3,67},{67,4},{4,68},... | collective-permute-start | bytes 1572872 | tf_op jit(solution)/shard_map/ppermute | solution.py:546
  70.0 5.9 %collective-permute-start.15 = (f32[9,96,128]{2,1,0:T(8,128)S(1)}, f32[9,96,128]{2,1,0:T(8,128)S(1)}, u32[]{:S(2)}, u32[]{:S(2)}) collective-permute-start(f32[9,96,128]{2,1,0:T(8,128)S(1)} %get-tuple-element.75.own), channel_id=1, source_target_pairs={{96,64},{64,96},{32,0},{0,32},{1,33},{33,1},{65,97},{97,65},{98,66... | collective-permute-start | bytes 1327112 | tf_op jit(solution)/shard_map/ppermute | solution.py:546
  74.7 7.9 %collective-permute-start.16 = (f32[9,96,128]{2,1,0:T(8,128)S(1)}, f32[9,96,128]{2,1,0:T(8,128)S(1)}, u32[]{:S(2)}, u32[]{:S(2)}) collective-permute-start(f32[9,96,128]{2,1,0:T(8,128)S(1)} %collective-permute-done.14.near), channel_id=1, source_target_pairs={{96,64},{64,96},{32,0},{0,32},{1,33},{33,1},{65,97},{97,65},{98,66... | collective-permute-start | bytes 1327112 | tf_op jit(solution)/shard_map/ppermute | solution.py:546
  93.6 2.2 %collective-permute-start.17 = (f32[8,32,128]{2,1,0:T(8,128)S(1)}, f32[8,32,128]{2,1,0:T(8,128)S(1)}, u32[]{:S(2)}, u32[]{:S(2)}) collective-permute-start(f32[8,32,128]{2,1,0:T(8,128)S(1)} %get-tuple-element.90), channel_id=1, source_target_pairs={{0,32},{32,0},{64,96},{96,64},{1,33},{33,1},{65,97},{97,65},{2,34}... | collective-permute-start | bytes 393224 | tf_op jit(solution)/shard_map/ppermute | solution.py:598
  93.7 4.7 %collective-permute-start.18 = (f32[8,32,128]{2,1,0:T(8,128)S(1)}, f32[8,32,128]{2,1,0:T(8,128)S(1)}, u32[]{:S(2)}, u32[]{:S(2)}) collective-permute-start(f32[8,32,128]{2,1,0:T(8,128)S(1)} %get-tuple-element.91), channel_id=1, source_target_pairs={{0,64},{32,96},{64,0},{96,32},{1,65},{33,97},{65,1},{97,33},{2,66}... | collective-permute-start | bytes 393224 | tf_op jit(solution)/shard_map/ppermute | solution.py:598
  93.8 8.0 %collective-permute-start.19 = (f32[8,32,128]{2,1,0:T(8,128)S(1)}, f32[8,32,128]{2,1,0:T(8,128)S(1)}, u32[]{:S(2)}, u32[]{:S(2)}) collective-permute-start(f32[8,32,128]{2,1,0:T(8,128)S(1)} %get-tuple-element.92), channel_id=1, source_target_pairs={{0,96},{32,64},{64,32},{96,0},{1,97},{33,65},{65,33},{97,1},{2,98}... | collective-permute-start | bytes 393224 | tf_op jit(solution)/shard_map/ppermute | solution.py:598
